TPU v7x, 128 devices: a whole 4x4x4 slice. The times are simulated.
128 devices in a mesh: row: 16 (over x, y), col: 8 (over z, core).
Axes of the slice: x: 4, y: 4, z: 4, core: 2. Of those that a mesh axis runs over, the one named last changes fastest.
Arguments:
- sources: bfloat16 [16, 32768], P(None, ('row', 'col')), may hold values from -6 to 6
- dipole_tiles: bfloat16 [4096, 256, 256], P(('row', 'col')), may hold values from -0.1875 to 0.1875
- dipole_rows: int32 [4096], P(('row', 'col')), may hold values from 0 to 7
- dipole_columns: int32 [4096], P(('row', 'col')), may hold values from 0 to 15
- dipole_count: int32 [128], P(('row', 'col')), may hold values from 1 to 32, as said below
- energies: float32 [32768], P(('row', 'col')), may hold values from -3 to 3
- h_tiles: bfloat16 [4096, 256, 256], P(('row', 'col')), may hold values from -0.0625 to 0.0625
- tile_rows: int32 [4096], P(('row', 'col')), may hold values from 0 to 7, as said below
- tile_columns: int32 [4096], P(('row', 'col')), may hold values from 0 to 15
- tile_count: int32 [128], P(('row', 'col')), may hold values from 1 to 32, as said below
Outputs:
- solution: float32 [64, 32768], P(None, ('row', 'col'))
- residual: float32 [64, 32768], P(None, ('row', 'col'))
- checksum: float32 [3, 64], replicated
Inputs may be any that keep to these rules, and one draw needn't show every extreme that they name: `tile_rows`: for every Hamiltonian slot, padded ones too, the block row I does not exceed the block column J. `tile_count`: some device has all 32 slots live in every draw; the live slots of one device name distinct pairs of block row and block column. `dipole_count`: some device has all 32 slots live in every draw.
All inputs are finite; a program needn't handle non-finite values.
Results may differ from a plain program's by a relative error of at most 0.0003.
Values may be sent and summed in bfloat16 or wider, within the bound.
No kernel may reach another device: no remote copies, remote signals or barrier semaphores. Data moves between devices by JAX's collectives and lax.ppermute only.
A program may use at most 128 MiB of HBM per device.

v0:
```python
import jax
import jax.numpy as jnp
from jax import lax
from jax.sharding import PartitionSpec as P

NV = 16
SHIFTS = 4
ITERS = 3


EPSILON = 1e-06


def split_parts(vectors):
    upper = vectors.astype(jnp.bfloat16)
    rest = vectors - lax.optimization_barrier(upper).astype(jnp.float32)
    return jnp.concatenate([upper, rest.astype(jnp.bfloat16)], axis=0)


def direct_terms(column_set, tiles, rows, columns, live, half, row_groups):
    picked_columns = jnp.take(column_set, columns, axis=1)
    direct = jnp.einsum("vts,tks->tvk", picked_columns, tiles, preferred_element_type=jnp.float32)
    direct = direct[:, :half] + direct[:, half:]
    row_hits = (rows[:, None] == jnp.arange(row_groups, dtype=jnp.int32)[None, :]).astype(
        jnp.float32
    ) * live[:, None]
    return jnp.einsum("ti,tvk->vik", row_hits, direct, precision=lax.Precision.HIGHEST)


def back_terms(row_set, tiles, rows, columns, live, half, column_groups):
    picked_rows = jnp.take(row_set, rows, axis=1)
    back = jnp.einsum("vtk,tks->tvs", picked_rows, tiles, preferred_element_type=jnp.float32)
    back = back[:, :half] + back[:, half:]
    column_hits = (columns[:, None] == jnp.arange(column_groups, dtype=jnp.int32)[None, :]).astype(
        jnp.float32
    ) * live[:, None]
    return jnp.einsum("tj,tvs->vjs", column_hits, back, precision=lax.Precision.HIGHEST)


def hamiltonian(vectors, energies, tiles, rows, columns, count):
    half = vectors.shape[0]
    width = vectors.shape[1]
    row_groups = lax.axis_size("col")
    column_groups = lax.axis_size("row")
    stacked = split_parts(vectors)
    column_set = lax.all_gather(stacked, "row", axis=1, tiled=True).reshape(2 * half, -1, width)
    slots = tiles.shape[0]
    live = (jnp.arange(slots, dtype=jnp.int32) < count[0]).astype(jnp.float32)
    direct_total = direct_terms(column_set, tiles, rows, columns, live, half, row_groups)
    row_set = lax.all_gather(stacked, "col", axis=1, tiled=True).reshape(2 * half, -1, width)
    back_total = back_terms(row_set, tiles, rows, columns, live, half, column_groups)
    back_part = lax.psum_scatter(
        back_total.reshape(half, -1), "row", scatter_dimension=1, tiled=True
    )
    direct_part = lax.psum_scatter(
        direct_total.reshape(half, -1), "col", scatter_dimension=1, tiled=True
    )
    result = energies[None, :] * vectors + direct_part
    result = result + back_part
    return result


def dipole_field(sources, dipole_tiles, dipole_rows, dipole_columns, dipole_count):
    height = sources.shape[0]
    width = sources.shape[1]
    gathered = lax.all_gather(sources, "row", axis=1, tiled=True).reshape(height, -1, width)
    picked = jnp.take(gathered, dipole_columns, axis=1)
    terms = jnp.einsum("vts,tks->tvk", picked, dipole_tiles, preferred_element_type=jnp.float32)
    live = (jnp.arange(dipole_tiles.shape[0], dtype=jnp.int32) < dipole_count[0]).astype(
        jnp.float32
    )
    hits = (
        dipole_rows[:, None] == jnp.arange(lax.axis_size("col"), dtype=jnp.int32)[None, :]
    ).astype(jnp.float32) * live[:, None]
    field = jnp.einsum("ti,tvk->vik", hits, terms, precision=lax.Precision.HIGHEST).reshape(
        height, -1
    )
    return lax.psum_scatter(field, "col", scatter_dimension=1, tiled=True)


def square_sums(residual):
    return lax.psum(jnp.sum(residual * residual, axis=1), ("row", "col"))


def body(
    sources,
    dipole_tiles,
    dipole_rows,
    dipole_columns,
    dipole_count,
    energies,
    h_tiles,
    tile_rows,
    tile_columns,
    tile_count,
):
    phi = dipole_field(sources, dipole_tiles, dipole_rows, dipole_columns, dipole_count)
    rhs = jnp.tile(phi, (SHIFTS, 1))
    centre = (jnp.arange(SHIFTS * NV, dtype=jnp.int32) // NV).astype(jnp.float32)
    shift = (-2.0 + 4.0 * (centre + 0.5) / SHIFTS)[:, None]
    solution = jnp.zeros_like(rhs)
    residual = rhs
    checks = []
    direction = rhs
    norm_now = square_sums(residual)
    for index in range(ITERS):
        inner = (
            hamiltonian(direction, energies, h_tiles, tile_rows, tile_columns, tile_count)
            - shift * direction
        )
        image = (
            hamiltonian(inner, energies, h_tiles, tile_rows, tile_columns, tile_count)
            - shift * inner
            + direction
        )
        curvature, image_sum, image_square = lax.psum(
            (
                jnp.sum(direction * image, axis=1),
                jnp.sum(image, axis=1),
                jnp.sum(image * image, axis=1),
            ),
            ("row", "col"),
        )
        checks.append(image_sum / jnp.sqrt(image_square + EPSILON))
        alpha = norm_now / curvature
        solution = solution + alpha[:, None] * direction
        residual = residual - alpha[:, None] * image
        if index + 1 < ITERS:
            norm_next = square_sums(residual)
            direction = residual + (norm_next / norm_now)[:, None] * direction
            norm_now = norm_next
    return (solution, residual, jnp.stack(checks, axis=0))


def solution(mesh):
    return jax.shard_map(
        body,
        mesh=mesh,
        in_specs=(
            P(None, ("row", "col")),
            P(("row", "col"), None, None),
            P(("row", "col")),
            P(("row", "col")),
            P(("row", "col")),
            P(("row", "col")),
            P(("row", "col"), None, None),
            P(("row", "col")),
            P(("row", "col")),
            P(("row", "col")),
        ),
        out_specs=(P(None, ("row", "col")), P(None, ("row", "col")), P()),
        check_vma=False,
    )
```

profile of v0, /device:TPU:1, one launch (start us, length us, event | category | flops | bytes accessed | tf_op | source)
XLA Modules:
  0.0 1318.8 jit_solution(2394421423285425288)
XLA Ops:
  8.5 19.5 %all_gather.39 = bf16[16,4096]{1,0:T(8,128)(2,1)S(1)} all-gather(bf16[16,256]{1,0:T(8,128)(2,1)} %param.14), channel_id=1, replica_groups=mesh['row'=16,'col'=8] {'row'}, dimensions={1}, use_global_device_ids=true | all-gather | bytes 139264 | tf_op jit(solution)/shard_map/all_gather | solution.py:66
  34.8 33.0 %reduce-scatter.14.cloned.1.call-done = f32[16,256]{1,0:T(8,128)} async-done(((f32[16,2048]{1,0:T(8,128)}), f32[16,256]{1,0:T(8,128)}) %reduce-scatter.14.cloned.1.call-update) | async-done | bytes 16400 | tf_op jit(solution)/shard_map/reduce_scatter | solution.py:78
  95.8 17.6 %all-gather.7.cloned.1.call-done = bf16[128,4096]{1,0:T(8,128)(2,1)} async-done(((bf16[128,256]{1,0:T(8,128)(2,1)}), bf16[128,4096]{1,0:T(8,128)(2,1)}) %all-gather.7.cloned.1.call-update) | async-done | bytes 1048592 | tf_op jit(solution)/shard_map/all_gather | solution.py:46
  123.8 66.1 %reduce-scatter.18.cloned.1.call-done = f32[64,256]{1,0:T(8,128)} async-done(((f32[64,4096]{1,0:T(8,128)}), f32[64,256]{1,0:T(8,128)}) %reduce-scatter.18.cloned.1.call-update) | async-done | bytes 65552 | tf_op jit(solution)/shard_map/reduce_scatter | solution.py:52
  189.9 32.1 %reduce-scatter.16.cloned.1.call-done = f32[64,256]{1,0:T(8,128)} async-done(((f32[64,2048]{1,0:T(8,128)}), f32[64,256]{1,0:T(8,128)}) %reduce-scatter.16.cloned.1.call-update) | async-done | bytes 65552 | tf_op jit(solution)/shard_map/reduce_scatter | solution.py:55
  249.1 18.2 %all-gather.9.cloned.1.call-done = bf16[128,4096]{1,0:T(8,128)(2,1)} async-done(((bf16[128,256]{1,0:T(8,128)(2,1)}), bf16[128,4096]{1,0:T(8,128)(2,1)}) %all-gather.9.cloned.1.call-update) | async-done | bytes 1048592 | tf_op jit(solution)/shard_map/all_gather | solution.py:46
  277.9 65.8 %reduce-scatter.22.cloned.1.call-done = f32[64,256]{1,0:T(8,128)} async-done(((f32[64,4096]{1,0:T(8,128)}), f32[64,256]{1,0:T(8,128)}) %reduce-scatter.22.cloned.1.call-update) | async-done | bytes 65552 | tf_op jit(solution)/shard_map/reduce_scatter | solution.py:52
  343.7 32.2 %reduce-scatter.20.cloned.1.call-done = f32[64,256]{1,0:T(8,128)} async-done(((f32[64,2048]{1,0:T(8,128)}), f32[64,256]{1,0:T(8,128)}) %reduce-scatter.20.cloned.1.call-update) | async-done | bytes 65552 | tf_op jit(solution)/shard_map/reduce_scatter | solution.py:55
  377.0 67.2 %all-reduce.1 = (f32[64]{0:T(128)S(1)}, f32[64]{0:T(128)S(1)}) all-reduce(f32[64]{0:T(128)S(1)} %reduce_sum.111, f32[64]{0:T(128)S(1)} %get-tuple-element.35), channel_id=1, replica_groups=mesh['row'=16,'col'=8] {'row','col'}, use_global_device_ids=true, to_apply=%region_2.3 | all-reduce | flops 128 | bytes 1024 | tf_op jit(solution)/shard_map/psum | solution.py:82
  444.4 62.5 %psum.86 = f32[64]{0:T(128)S(1)} all-reduce(f32[64]{0:T(128)S(1)} %multiply_reduce_fusion.6), channel_id=1, replica_groups=mesh['row'=16,'col'=8] {'row','col'}, use_global_device_ids=true, to_apply=%region_10.13 | all-reduce | flops 64 | bytes 512 | tf_op jit(solution)/shard_map/psum | solution.py:82
  556.7 66.2 %reduce-scatter.26.cloned.1.call-done = f32[64,256]{1,0:T(8,128)} async-done(((f32[64,4096]{1,0:T(8,128)}), f32[64,256]{1,0:T(8,128)}) %reduce-scatter.26.cloned.1.call-update) | async-done | bytes 65552 | tf_op jit(solution)/shard_map/reduce_scatter | solution.py:52
  622.9 32.1 %reduce-scatter.24.cloned.1.call-done = f32[64,256]{1,0:T(8,128)} async-done(((f32[64,2048]{1,0:T(8,128)}), f32[64,256]{1,0:T(8,128)}) %reduce-scatter.24.cloned.1.call-update) | async-done | bytes 65552 | tf_op jit(solution)/shard_map/reduce_scatter | solution.py:55
  682.0 18.4 %all-gather.13.cloned.1.call-done = bf16[128,4096]{1,0:T(8,128)(2,1)} async-done(((bf16[128,256]{1,0:T(8,128)(2,1)}), bf16[128,4096]{1,0:T(8,128)(2,1)}) %all-gather.13.cloned.1.call-update) | async-done | bytes 1048592 | tf_op jit(solution)/shard_map/all_gather | solution.py:46
  710.8 66.0 %reduce-scatter.30.cloned.1.call-done = f32[64,256]{1,0:T(8,128)} async-done(((f32[64,4096]{1,0:T(8,128)}), f32[64,256]{1,0:T(8,128)}) %reduce-scatter.30.cloned.1.call-update) | async-done | bytes 65552 | tf_op jit(solution)/shard_map/reduce_scatter | solution.py:52
  776.8 32.2 %reduce-scatter.28.cloned.1.call-done = f32[64,256]{1,0:T(8,128)} async-done(((f32[64,2048]{1,0:T(8,128)}), f32[64,256]{1,0:T(8,128)}) %reduce-scatter.28.cloned.1.call-update) | async-done | bytes 65552 | tf_op jit(solution)/shard_map/reduce_scatter | solution.py:55
  810.2 67.2 %psum.87 = f32[64]{0:T(128)S(1)} all-reduce(f32[64]{0:T(128)S(1)} %get-tuple-element.9), channel_id=1, replica_groups=mesh['row'=16,'col'=8] {'row','col'}, use_global_device_ids=true, to_apply=%region_16.19 | all-reduce | flops 64 | bytes 512 | tf_op jit(solution)/shard_map/psum | solution.py:116
  877.6 62.8 %psum.88 = f32[64]{0:T(128)S(1)} all-reduce(f32[64]{0:T(128)S(1)} %get-tuple-element.30), channel_id=1, replica_groups=mesh['row'=16,'col'=8] {'row','col'}, use_global_device_ids=true, to_apply=%region_18.21 | all-reduce | flops 64 | bytes 512 | tf_op jit(solution)/shard_map/psum | solution.py:82
  990.1 66.0 %reduce-scatter.34.cloned.1.call-done = f32[64,256]{1,0:T(8,128)} async-done(((f32[64,4096]{1,0:T(8,128)}), f32[64,256]{1,0:T(8,128)}) %reduce-scatter.34.cloned.1.call-update) | async-done | bytes 65552 | tf_op jit(solution)/shard_map/reduce_scatter | solution.py:52
  1056.2 32.0 %reduce-scatter.32.cloned.1.call-done = f32[64,256]{1,0:T(8,128)} async-done(((f32[64,2048]{1,0:T(8,128)}), f32[64,256]{1,0:T(8,128)}) %reduce-scatter.32.cloned.1.call-update) | async-done | bytes 65552 | tf_op jit(solution)/shard_map/reduce_scatter | solution.py:55
  1089.9 16.8 %all_gather.51 = bf16[128,2048]{1,0:T(8,128)(2,1)S(1)} all-gather(bf16[128,256]{1,0:T(8,128)(2,1)} %pad_maximum_fusion.5), channel_id=1, replica_groups=mesh['row'=16,'col'=8] {'col'}, dimensions={1}, use_global_device_ids=true | all-gather | bytes 589824 | tf_op jit(solution)/shard_map/all_gather | solution.py:50
  1115.3 18.3 %all-gather.17.cloned.1.call-done = bf16[128,4096]{1,0:T(8,128)(2,1)} async-done(((bf16[128,256]{1,0:T(8,128)(2,1)}), bf16[128,4096]{1,0:T(8,128)(2,1)}) %all-gather.17.cloned.1.call-update) | async-done | bytes 1048592 | tf_op jit(solution)/shard_map/all_gather | solution.py:46
  1143.8 66.0 %reduce-scatter.38.cloned.1.call-done = f32[64,256]{1,0:T(8,128)} async-done(((f32[64,4096]{1,0:T(8,128)}), f32[64,256]{1,0:T(8,128)}) %reduce-scatter.38.cloned.1.call-update) | async-done | bytes 65552 | tf_op jit(solution)/shard_map/reduce_scatter | solution.py:52
  1209.9 32.2 %reduce-scatter.36.cloned.1.call-done = f32[64,256]{1,0:T(8,128)} async-done(((f32[64,2048]{1,0:T(8,128)}), f32[64,256]{1,0:T(8,128)}) %reduce-scatter.36.cloned.1.call-update) | async-done | bytes 65552 | tf_op jit(solution)/shard_map/reduce_scatter | solution.py:55
  1243.2 67.2 %all-reduce = (f32[64]{0:T(128)S(1)}, f32[64]{0:T(128)S(1)}, f32[64]{0:T(128)S(1)}, f32[64]{0:T(128)S(1)}, f32[64]{0:T(128)S(1)}, /*index=5*/f32[64]{0:T(128)S(1)}, f32[64]{0:T(128)S(1)}) all-reduce(f32[64]{0:T(128)S(1)} %get-tuple-element.15, f32[64]{0:T(128)S(1)} %get-tuple-element.14, ...), channel_id=1, replica_groups=mesh['row'=16,'col'=8] {'row','col'}, use_global_device_ids=true, to_apply=%region_24.27 | all-reduce | flops 448 | bytes 3584 | tf_op jit(solution)/shard_map/psum | solution.py:116
  (191 shorter events, 244.2 us)
Async XLA Ops:
  7.2 60.7 %reduce-scatter.14.cloned.1.call-start = ((), (), s32[]{:S(2)}) async-start(), calls=%async_computation.13 | async-start | bytes 147456 | tf_op jit(solution)/shard_map/reduce_scatter | solution.py:78
  29.3 3.4 copy-start.4
  29.3 40.7 %copy-start.3 = (s32[32]{0:T(128)S(1)}, s32[32]{0:T(128)}, u32[]{:S(2)}) copy-start(s32[32]{0:T(128)} %param.21) | copy-start | bytes 388
  34.1 79.3 %all-gather.7.cloned.1.call-start = ((), (), s32[]{:S(2)}) async-start(), calls=%async_computation.14 | async-start | bytes 1114112 | tf_op jit(solution)/shard_map/all_gather | solution.py:46
  70.0 119.9 %reduce-scatter.18.cloned.1.call-start = ((), (), s32[]{:S(2)}) async-start(), calls=%async_computation.16 | async-start | bytes 1114112 | tf_op jit(solution)/shard_map/reduce_scatter | solution.py:52
  90.8 0.7 copy-start.2
  95.5 126.5 %reduce-scatter.16.cloned.1.call-start = ((), (), s32[]{:S(2)}) async-start(), calls=%async_computation.15 | async-start | bytes 589824 | tf_op jit(solution)/shard_map/reduce_scatter | solution.py:55
  120.3 101.7 %copy-start = (f32[16,256]{1,0:T(8,128)S(1)}, f32[16,256]{1,0:T(8,128)}, u32[]{:S(2)}) copy-start(f32[16,256]{1,0:T(8,128)} %reduce-scatter.14.cloned.1.call-done) | copy-start | bytes 49156
  120.3 101.7 %copy-start.1 = (f32[256]{0:T(256)S(1)}, f32[256]{0:T(256)}, u32[]{:S(2)}) copy-start(f32[256]{0:T(256)} %param.19) | copy-start | bytes 3076
  123.7 143.6 %all-gather.9.cloned.1.call-start = ((), (), s32[]{:S(2)}) async-start(), calls=%async_computation.17 | async-start | bytes 1114112 | tf_op jit(solution)/shard_map/all_gather | solution.py:46
  223.6 120.0 %reduce-scatter.22.cloned.1.call-start = ((), (), s32[]{:S(2)}) async-start(), calls=%async_computation.19 | async-start | bytes 1114112 | tf_op jit(solution)/shard_map/reduce_scatter | solution.py:52
  248.8 127.1 %reduce-scatter.20.cloned.1.call-start = ((), (), s32[]{:S(2)}) async-start(), calls=%async_computation.18 | async-start | bytes 589824 | tf_op jit(solution)/shard_map/reduce_scatter | solution.py:55
  277.6 268.8 %all-gather.11.cloned.1.call-start = ((), (), s32[]{:S(2)}) async-start(), calls=%async_computation.20 | async-start | bytes 1114112 | tf_op jit(solution)/shard_map/all_gather | solution.py:46
  507.8 115.1 %reduce-scatter.26.cloned.1.call-start = ((), (), s32[]{:S(2)}) async-start(), calls=%async_computation.22 | async-start | bytes 1114112 | tf_op jit(solution)/shard_map/reduce_scatter | solution.py:52
  530.5 124.5 %reduce-scatter.24.cloned.1.call-start = ((), (), s32[]{:S(2)}) async-start(), calls=%async_computation.21 | async-start | bytes 589824 | tf_op jit(solution)/shard_map/reduce_scatter | solution.py:55
  556.7 143.8 %all-gather.13.cloned.1.call-start = ((), (), s32[]{:S(2)}) async-start(), calls=%async_computation.23 | async-start | bytes 1114112 | tf_op jit(solution)/shard_map/all_gather | solution.py:46
  656.6 120.2 %reduce-scatter.30.cloned.1.call-start = ((), (), s32[]{:S(2)}) async-start(), calls=%async_computation.25 | async-start | bytes 1114112 | tf_op jit(solution)/shard_map/reduce_scatter | solution.py:52
  682.0 127.1 %reduce-scatter.28.cloned.1.call-start = ((), (), s32[]{:S(2)}) async-start(), calls=%async_computation.24 | async-start | bytes 589824 | tf_op jit(solution)/shard_map/reduce_scatter | solution.py:55
  710.7 269.0 %all-gather.15.cloned.1.call-start = ((), (), s32[]{:S(2)}) async-start(), calls=%async_computation.26 | async-start | bytes 1114112 | tf_op jit(solution)/shard_map/all_gather | solution.py:46
  941.2 115.0 %reduce-scatter.34.cloned.1.call-start = ((), (), s32[]{:S(2)}) async-start(), calls=%async_computation.28 | async-start | bytes 1114112 | tf_op jit(solution)/shard_map/reduce_scatter | solution.py:52
  963.5 124.7 %reduce-scatter.32.cloned.1.call-start = ((), (), s32[]{:S(2)}) async-start(), calls=%async_computation.27 | async-start | bytes 589824 | tf_op jit(solution)/shard_map/reduce_scatter | solution.py:55
  990.1 143.5 %all-gather.17.cloned.1.call-start = ((), (), s32[]{:S(2)}) async-start(), calls=%async_computation.29 | async-start | bytes 1114112 | tf_op jit(solution)/shard_map/all_gather | solution.py:46
  1089.8 120.1 %reduce-scatter.38.cloned.1.call-start = ((), (), s32[]{:S(2)}) async-start(), calls=%async_computation.31 | async-start | bytes 1114112 | tf_op jit(solution)/shard_map/reduce_scatter | solution.py:52
  1115.2 126.9 %reduce-scatter.36.cloned.1.call-start = ((), (), s32[]{:S(2)}) async-start(), calls=%async_computation.30 | async-start | bytes 589824 | tf_op jit(solution)/shard_map/reduce_scatter | solution.py:55
Sparse Core Ops, SparseCore 0:
  34.3 33.5 reduce-scatter.13
  70.6 42.7 all-gather.6
  116.6 73.2 reduce-scatter.17
  192.1 29.8 reduce-scatter.15
  224.5 42.7 all-gather.8
  270.4 73.2 reduce-scatter.21
  346.0 29.8 reduce-scatter.19
  507.9 38.4 all-gather.10
  549.6 73.2 reduce-scatter.25
  625.1 29.8 reduce-scatter.23
  657.7 42.7 all-gather.12
  703.5 73.2 reduce-scatter.29
  779.2 29.8 reduce-scatter.27
  941.3 38.4 all-gather.14
  982.8 73.2 reduce-scatter.33
  1058.4 29.7 reduce-scatter.31
  1090.7 42.8 all-gather.16
  1136.6 73.2 reduce-scatter.37
  1212.3 29.8 reduce-scatter.35
where the time goes:
time: 1330 us; the launch traced here: 1320 us
  waiting for transfers between devices  727 us (55%)
  blocking collectives  441 us (33%)
  matrix products  72.6 us (5%)
  local copies, waits for them, and re-layouts  41.9 us (3%)
  other arithmetic  18.1 us (1%)
  between operations  16.5 us (1%)
    reduce_scatter x6, waiting for transfers between devices, hamiltonian(): lax.psum_scatter(back_total.reshape(half, -1), 'row', scatter_dimension=1...  396 us
    reduce_scatter x6, waiting for transfers between devices, hamiltonian(): lax.psum_scatter(direct_total.reshape(half, -1), 'col', scatter_dimension...  193 us
    psum x3, blocking collectives, square_sums(): return lax.psum(jnp.sum(residual * residual, axis=1), ('row', 'col'))  193 us
    psum x2, blocking collectives, body(): lax.psum((jnp.sum(direction * image, axis=1), jnp.sum(image, axis=1), jnp...  134 us
    all_gather x6, waiting for transfers between devices, hamiltonian(): lax.all_gather(stacked, 'row', axis=1, tiled=True)  105 us
    all_gather x6, blocking collectives, hamiltonian(): lax.all_gather(stacked, 'col', axis=1, tiled=True)  94.7 us
    reduce_scatter x1, waiting for transfers between devices, dipole_field(): return lax.psum_scatter(field, 'col', scatter_dimension=1, tiled=True)  33 us
  transfers between devices with their start and end apart: 19, of which 19 were waited for; matrix products, arithmetic and copies ran while one was open for 8% of the time, Pallas kernels for 0%

commit v1 on v0

v1 whole, which is shorter than its diff:
```python
import functools

import jax
import jax.numpy as jnp
from jax import lax
from jax.experimental import pallas as pl
from jax.experimental.pallas import tpu as pltpu
from jax.sharding import PartitionSpec as P

NV = 16
SHIFTS = 4
ITERS = 3
EPSILON = 1e-06
DEGREE = 2 * ITERS
F32 = jnp.float32
BF16 = jnp.bfloat16

VM = pl.BlockSpec(memory_space=pltpu.VMEM)
SM = pl.BlockSpec(memory_space=pltpu.SMEM)


def call(kernel, out_shape, n_smem, n_vmem, scratch=()):
    return pl.pallas_call(
        kernel,
        out_shape=out_shape,
        in_specs=[SM] * n_smem + [VM] * n_vmem,
        out_specs=jax.tree.map(lambda _: VM, out_shape),
        scratch_shapes=list(scratch),
        compiler_params=pltpu.CompilerParams(vmem_limit_bytes=24 << 20),
    )


def split_into(target, index, value):
    upper = value.astype(BF16)
    target[index, :NV] = upper
    target[index, NV:] = (value - upper.astype(F32)).astype(BF16)


def row_sums(a):
    total = a[0]
    for i in range(1, a.shape[0]):
        total = total + a[i]
    return jnp.sum(total, axis=-1, keepdims=True)


def lanes_of(parts, shape):
    lane = lax.broadcasted_iota(jnp.int32, shape, 1)
    out = jnp.zeros(shape, F32)
    for i, part in enumerate(parts):
        out = jnp.where(lane == i, part, out)
    return out


def dots_of(z_mine, z_other, q_mine, q_other, shape):
    norm = row_sums(z_mine * z_mine) + row_sums(z_other * z_other)
    along = row_sums(z_mine * q_mine) + row_sums(z_other * q_other)
    total = row_sums(z_mine) + row_sums(z_other)
    return lanes_of((norm, along, total), shape)


def dipole_kernel(cin, rout, gathered, tiles, p_mine, p_other, xs, acc):
    groups = gathered.shape[0]
    for i in range(groups):
        xs[i] = gathered[i]
    xs[groups] = jnp.zeros(xs.shape[1:], BF16)
    acc[...] = jnp.zeros(acc.shape, F32)
    for t in range(tiles.shape[0]):
        res = lax.dot_general(xs[cin[t]], tiles[t], (((1,), (1,)), ((), ())), preferred_element_type=F32)
        acc[rout[t]] += res
    half = p_mine.shape[0]
    p_mine[...] = acc[:half]
    p_other[...] = acc[half:]


def back_kernel(place, rin, cout, z_mine, z_other, q_mine, q_other, tiles, out, ys):
    half = z_mine.shape[0]
    for i in range(half):
        split_into(ys, i, z_mine[i])
        split_into(ys, half + i, z_other[i])
    ys[2 * half] = jnp.zeros(ys.shape[1:], BF16)
    peers = out.shape[0]
    own = z_mine[place[0]]
    dots = dots_of(z_mine[...], z_other[...], q_mine[...], q_other[...], own.shape)
    for p in range(peers):
        out[p, 0] = own
        out[p, 1] = jnp.zeros_like(own)
        out[p, 2] = dots
    for t in range(tiles.shape[0]):
        res = jnp.dot(ys[rin[t]], tiles[t], preferred_element_type=F32)
        out[cout[t], 1] += res[:NV] + res[NV:]


def direct_kernel(
    has_old, place, cin, rout, gathered, tiles, energies, z_mine, z_other, q_mine, q_other, qp_mine, qp_other, zp_mine, state,
    p_mine, p_other, qn_mine, qn_other, state_out, xs, acc,
):
    groups = gathered.shape[0]
    for i in range(groups):
        split_into(xs, i, gathered[i, 0])
    xs[groups] = jnp.zeros(xs.shape[1:], BF16)
    acc[...] = jnp.zeros(acc.shape, F32)
    for t in range(tiles.shape[0]):
        res = lax.dot_general(xs[cin[t]], tiles[t], (((1,), (1,)), ((), ())), preferred_element_type=F32)
        acc[rout[t]] += res[:NV] + res[NV:]
    back = gathered[0, 1]
    dots = gathered[0, 2]
    for i in range(1, groups):
        back = back + gathered[i, 1]
        dots = dots + gathered[i, 2]
    norm, alpha, total = dots[:, 0:1], dots[:, 1:2], dots[:, 2:3]
    old = state[...]
    s_now, s_old = old[:, 2:3], old[:, 3:4]
    beta = old[:, 1:2] if has_old else jnp.zeros_like(s_now)
    square = norm - alpha * alpha - beta * beta
    beta_next = jnp.sqrt(jnp.maximum(square, 1e-12 * norm + 1e-30))
    scale = 1.0 / beta_next
    s_next = (total - alpha * s_now - beta * s_old) * scale
    state_out[...] = lanes_of((alpha, beta_next, s_next, s_now), state_out.shape)
    qn_mine[...] = (z_mine[...] - alpha * q_mine[...] - beta * qp_mine[...]) * scale
    qn_other[...] = (z_other[...] - alpha * q_other[...] - beta * qp_other[...]) * scale
    own = z_mine[place[0]]
    local = energies[...] * own + back - alpha * own - beta * zp_mine[place[0]]
    acc[place[0]] += local
    half = p_mine.shape[0]
    p_mine[...] = acc[:half] * scale
    p_other[...] = acc[half:] * scale


def apply_h(coefs, alphas, betas, shift):
    out = [None] * (DEGREE + 1)

    def add(j, value):
        out[j] = value if out[j] is None else out[j] + value

    for j, c in enumerate(coefs):
        if c is None:
            continue
        add(j, -shift * c)
        if j + 1 < DEGREE:
            add(j + 1, betas[j + 1] * c)
            add(j, alphas[j] * c)
            if j:
                add(j - 1, betas[j] * c)
        else:
            add(DEGREE, c)
    return out


def vec(op, *vectors):
    return [op(*[0.0 if e is None else e for e in es]) if any(e is not None for e in es) else None for es in zip(*vectors)]


def inner(a, b):
    terms = [x * y for x, y in zip(a, b) if x is not None and y is not None]
    return functools.reduce(lambda x, y: x + y, terms)


def finish_kernel(place, *refs):
    states, qs = refs[:DEGREE], refs[DEGREE : 2 * DEGREE]
    solution_out, partial_out, last_out, aux_out = refs[2 * DEGREE :]
    shape = aux_out.shape[1:]
    lane = lax.broadcasted_iota(jnp.int32, shape, 1)
    shift = -2.0 + 4.0 * (lane.astype(F32) + 0.5) / SHIFTS
    full = [s[...] for s in states]
    spread = lambda a: jnp.broadcast_to(a, shape)
    alphas = [spread(full[j + 1][:, 0:1]) for j in range(DEGREE - 1)]
    betas = [spread(full[j][:, 1:2]) for j in range(DEGREE)]
    sums = [spread(full[j][:, 2:3]) for j in range(DEGREE)]
    residual = [betas[0]] + [None] * DEGREE
    direction = list(residual)
    answer = [None] * (DEGREE + 1)
    norm_now = inner(residual, residual)
    checks = []
    for index in range(ITERS):
        inside = apply_h(direction, alphas, betas, shift)
        image = vec(lambda x, y: x + y, apply_h(inside, alphas, betas, shift), direction)
        curvature = inner(inside, inside) + inner(direction, direction)
        alpha = norm_now / curvature
        if index + 1 < ITERS:
            image_sum = inner(image[:DEGREE], sums)
            checks.append(image_sum / jnp.sqrt(inner(image, image) + EPSILON))
        answer = vec(lambda x, d: x + alpha * d, answer, direction)
        residual = vec(lambda x, d: x - alpha * d, residual, image)
        if index + 1 < ITERS:
            norm_next = inner(residual, residual)
            ratio = norm_next / norm_now
            direction = vec(lambda x, d: x + ratio * d, residual, direction)
            norm_now = norm_next
    known = image[:DEGREE]
    aux_out[0] = checks[0]
    aux_out[1] = checks[1]
    aux_out[2] = inner(known, sums)
    aux_out[3] = inner(known, known)
    aux_out[4] = image[DEGREE]
    aux_out[5] = 2.0 * image[DEGREE] * image[DEGREE - 1]
    aux_out[6] = 2.0 * image[DEGREE] * image[DEGREE - 2] * betas[DEGREE - 1]
    last_out[...] = residual[DEGREE]
    own = [q[place[0]] for q in qs]
    for k in range(SHIFTS):
        rows = slice(k * NV, (k + 1) * NV)
        solution_out[rows] = inner([c[:, k : k + 1] for c in answer[: DEGREE - 1]], own)
        partial_out[rows] = inner([c[:, k : k + 1] for c in residual[:DEGREE]], own)


def tail_kernel(place, z_mine, z_other, q_mine, q_other, partial, last, residual_out, dots_out):
    own = z_mine[place[0]]
    for k in range(SHIFTS):
        rows = slice(k * NV, (k + 1) * NV)
        residual_out[rows] = partial[rows] + last[:, k : k + 1] * own
    dots = dots_of(z_mine[...], z_other[...], q_mine[...], q_other[...], dots_out.shape[1:])
    for p in range(dots_out.shape[0]):
        dots_out[p] = dots


def check_kernel(gathered, aux, out):
    dots = gathered[0]
    for i in range(1, gathered.shape[0]):
        dots = dots + gathered[i]
    norm, along, total = dots[:, 0:1], dots[:, 1:2], dots[:, 2:3]
    image_sum = aux[2] + aux[4] * total
    image_square = aux[3] + aux[4] * aux[4] * norm + aux[5] * along + aux[6]
    rows = (aux[0], aux[1], image_sum / jnp.sqrt(image_square + EPSILON))
    for i, row in enumerate(rows):
        out[i] = jnp.transpose(row)[:SHIFTS]


def body(
    sources,
    dipole_tiles,
    dipole_rows,
    dipole_columns,
    dipole_count,
    energies,
    h_tiles,
    tile_rows,
    tile_columns,
    tile_count,
):
    width = sources.shape[1]
    rows_n = lax.axis_size("row")
    cols_n = lax.axis_size("col")
    half = cols_n // 2
    col = lax.axis_index("col")
    parity = col % 2
    place = (col // 2).reshape(1).astype(jnp.int32)

    def tables(rows, columns, count):
        live = jnp.arange(rows.shape[0], dtype=jnp.int32) < count[0]
        position = ((rows % 2) ^ parity) * half + rows // 2
        return (
            position,
            jnp.where(live, position, cols_n),
            columns,
            jnp.where(live, columns, rows_n),
        )

    d_rout, _, _, d_cin = tables(dipole_rows, dipole_columns, dipole_count)
    h_rout, h_rin, h_cout, h_cin = tables(tile_rows, tile_columns, tile_count)

    pair = [(i, i ^ 1) for i in range(cols_n)]
    ring = lambda d: [(2 * z + k, 2 * ((z + d) % half) + k) for z in range(half) for k in range(2)]

    def group_sum(p_mine, p_other):
        q = p_mine + lax.ppermute(p_other, "col", pair)
        far = lax.ppermute(q, "col", ring(2))
        up = lax.ppermute(q, "col", ring(1))
        down = lax.ppermute(q, "col", ring(3))
        mine = (q + far) + (up + down)
        return mine, lax.ppermute(mine, "col", pair)

    block = jax.ShapeDtypeStruct((half, NV, width), F32)
    small = jax.ShapeDtypeStruct((NV, 128), F32)

    spread = jnp.broadcast_to(sources[None], (rows_n,) + sources.shape)
    gathered = lax.all_to_all(spread, "row", 0, 0, tiled=True)
    p_mine, p_other = call(
        dipole_kernel,
        (block, block),
        2,
        2,
        [pltpu.VMEM((rows_n + 1, NV, width), BF16), pltpu.VMEM((cols_n, NV, width), F32)],
    )(d_cin, d_rout, gathered, dipole_tiles)
    z = group_sum(p_mine, p_other)

    zero = jnp.zeros(block.shape, F32)
    q, q_old, z_old = (zero, zero), (zero, zero), zero
    state = jnp.zeros(small.shape, F32)
    diagonal = energies[None, :]
    states, basis = [], []
    for step in range(DEGREE):
        payload = call(
            back_kernel,
            jax.ShapeDtypeStruct((rows_n, 3, NV, width), F32),
            3,
            5,
            [pltpu.VMEM((cols_n + 1, 2 * NV, width), BF16)],
        )(place, h_rin, h_cout, *z, *q, h_tiles)
        gathered = lax.all_to_all(payload, "row", 0, 0, tiled=True)
        p_mine, p_other, qn_mine, qn_other, state = call(
            functools.partial(direct_kernel, step > 1),
            (block, block, block, block, small),
            3,
            11,
            [pltpu.VMEM((rows_n + 1, 2 * NV, width), BF16), pltpu.VMEM((cols_n, NV, width), F32)],
        )(place, h_cin, h_rout, gathered, h_tiles, diagonal, *z, *q, *q_old, z_old, state)
        states.append(state)
        basis.append(qn_mine)
        z_old = z[0]
        q, q_old = (qn_mine, qn_other), q
        z = group_sum(p_mine, p_other)

    wide = jax.ShapeDtypeStruct((SHIFTS * NV, width), F32)
    answer, partial, last, aux = call(
        finish_kernel,
        (wide, wide, small, jax.ShapeDtypeStruct((7, NV, 128), F32)),
        1,
        2 * DEGREE,
    )(place, *states, *basis)
    residual, dots = call(
        tail_kernel,
        (wide, jax.ShapeDtypeStruct((rows_n, NV, 128), F32)),
        1,
        6,
    )(place, *z, *q, partial, last)
    dots = lax.all_to_all(dots, "row", 0, 0, tiled=True)
    checks = call(check_kernel, jax.ShapeDtypeStruct((ITERS, SHIFTS, NV), F32), 0, 2)(dots, aux)
    return answer, residual, checks.reshape(ITERS, SHIFTS * NV)


def solution(mesh):
    both = ("row", "col")
    return jax.shard_map(
        body,
        mesh=mesh,
        in_specs=(
            P(None, both),
            P(both, None, None),
            P(both),
            P(both),
            P(both),
            P(both),
            P(both, None, None),
            P(both),
            P(both),
            P(both),
        ),
        out_specs=(P(None, both), P(None, both), P()),
        check_vma=False,
    )
```

time: 1330 us -> 252 us (0.19)
  waiting for transfers between devices: 727 us -> 64.6 us
  blocking collectives: 441 us -> 92.1 us
  matrix products: 72.6 us -> 0 us
  starting transfers between devices: 1.26 us -> 58 us
  local copies, waits for them, and re-layouts: 41.9 us -> 8.65 us
  Pallas kernels: 0 us -> 24.1 us
  other arithmetic: 18.1 us -> 0.93 us
  between operations: 16.5 us -> 2.17 us
    reduce_scatter x13 -> x0, waiting for transfers between devices: 622 us -> none  [the longest x6 396 us: hamiltonian(): lax.psum_scatter(back_total.reshape(half, -1), 'row', scatter_dimension=1...]
    psum x5 -> x0, blocking collectives: 327 us -> none  [the longest x3 193 us: square_sums(): return lax.psum(jnp.sum(residual * residual, axis=1), ('row', 'col'))]
    all_gather x7 -> x0, blocking collectives: 114 us -> none  [the longest x6 94.7 us: hamiltonian(): lax.all_gather(stacked, 'col', axis=1, tiled=True)]
    all_gather x6 -> x0, waiting for transfers between devices: 105 us -> none  [hamiltonian(): lax.all_gather(stacked, 'row', axis=1, tiled=True)]
    all_to_all x0 -> x6, blocking collectives: none -> 92.1 us  [the longest x5 82.2 us: body(): gathered = lax.all_to_all(payload, 'row', 0, 0, tiled=True)]
    dot_general x26 -> x0, matrix products: 72.6 us -> none  [the longest x6 22.1 us: direct_terms(): jnp.einsum('vts,tks->tvk', picked_columns, tiles, preferred_element_type=...]
    ppermute x0 -> x35, starting transfers between devices: none -> 46.8 us  [the longest x7 17.6 us: group_sum(): down = lax.ppermute(q, 'col', ring(3))]
    ppermute x0 -> x35, waiting for transfers between devices: none -> 46.3 us  [the longest x7 34.2 us: group_sum(): up = lax.ppermute(q, 'col', ring(1))]
  transfers between devices with their start and end apart: 19 -> 37, of which waited for: 19 -> 28; matrix products, arithmetic and copies ran while one was open for 8% -> 0% of each run, Pallas kernels for 0% -> 0%
where the time goes in v1:
time: 252 us; the launch traced here: 251 us
  blocking collectives  92.1 us (37%)
  waiting for transfers between devices  64.6 us (26%)
  starting transfers between devices  58 us (23%)
  Pallas kernels  24.1 us (10%)
  local copies, waits for them, and re-layouts  8.65 us (3%)
    all_to_all x5, blocking collectives, body(): gathered = lax.all_to_all(payload, 'row', 0, 0, tiled=True)  82.2 us
    ppermute x7, waiting for transfers between devices, group_sum(): up = lax.ppermute(q, 'col', ring(1))  34.2 us
    ppermute x7, starting transfers between devices, group_sum(): down = lax.ppermute(q, 'col', ring(3))  17.6 us
    ppermute x7, starting transfers between devices, group_sum(): q = p_mine + lax.ppermute(p_other, 'col', pair)  14.1 us
    all_to_all x1, waiting for transfers between devices, body(): gathered = lax.all_to_all(payload, 'row', 0, 0, tiled=True)  12.7 us
    pallas_call x6, Pallas kernels, body(): call(functools.partial(direct_kernel, step > 1), (block, block, block, bl...  11.3 us
    all_to_all x1, blocking collectives, body(): dots = lax.all_to_all(dots, 'row', 0, 0, tiled=True)  9.83 us
    pallas_call x6, Pallas kernels, body(): call(back_kernel, jax.ShapeDtypeStruct((rows_n, 3, NV, width), F32), 3, 5...  9.2 us
  transfers between devices with their start and end apart: 37, of which 28 were waited for; matrix products, arithmetic and copies ran while one was open for 0% of the time, Pallas kernels for 0%

profile of v1, /device:TPU:1, one launch (start us, length us, event | category | flops | bytes accessed | tf_op | source)
XLA Modules:
  0.0 250.5 jit_solution(17167652758128688889)
XLA Ops:
  2.0 7.6 %all-to-all-start = ((bf16[16,16,256]{2,1,0:T(8,128)(2,1)}), bf16[16,16,256]{2,1,0:T(8,128)(2,1)S(1)}, u32[]{:S(2)}, u32[]{:S(2)}) async-start(bf16[16,16,256]{2,1,0:T(8,128)(2,1)} %broadcast_in_dim.25), calls=%async_computation | async-start | bytes 262144 | tf_op jit(solution)/shard_map/all_to_all | solution.py:275
  11.0 5.5 %all-to-all-done.gathered = bf16[16,16,256]{2,1,0:T(8,128)(2,1)S(1)} async-done(((bf16[16,16,256]{2,1,0:T(8,128)(2,1)}), bf16[16,16,256]{2,1,0:T(8,128)(2,1)S(1)}, u32[]{:S(2)}, u32[]{:S(2)}) %all-to-all-start) | async-done | bytes 131104 | tf_op jit(solution)/shard_map/all_to_all | solution.py:275
  23.4 3.8 %collective-permute-start.3 = (f32[4,16,256]{2,1,0:T(8,128)S(1)}, f32[4,16,256]{2,1,0:T(8,128)S(1)}, u32[]{:S(2)}, u32[]{:S(2)}) collective-permute-start(f32[4,16,256]{2,1,0:T(8,128)S(1)} %add.112), channel_id=1, source_target_pairs={{0,6},{1,7},{2,0},{3,1},{4,2},{5,3},{6,4},{7,5},{8,14},{9,15},{10,... | collective-permute-start | bytes 196616 | tf_op jit(solution)/shard_map/ppermute | solution.py:267
  29.2 4.2 %collective-permute-done.2 = f32[4,16,256]{2,1,0:T(8,128)S(1)} collective-permute-done((f32[4,16,256]{2,1,0:T(8,128)S(1)}, f32[4,16,256]{2,1,0:T(8,128)S(1)}, u32[]{:S(2)}, u32[]{:S(2)}) %collective-permute-start.2) | collective-permute-done | bytes 65568 | tf_op jit(solution)/shard_map/ppermute | solution.py:266
  37.5 2.3 shard_map.122
  39.8 3.6 %all-to-all-start.1 = ((f32[16,3,16,256]{3,2,1,0:T(8,128)}), f32[16,3,16,256]{3,2,1,0:T(8,128)S(1)}, u32[]{:S(2)}, u32[]{:S(2)}) async-start(f32[16,3,16,256]{3,2,1,0:T(8,128)} %shard_map.122), calls=%async_computation.1 | async-start | bytes 1572864 | tf_op jit(solution)/shard_map/all_to_all | solution.py:298
  43.5 12.7 %all-to-all-done.1.gathered = f32[16,3,16,256]{3,2,1,0:T(8,128)S(1)} async-done(((f32[16,3,16,256]{3,2,1,0:T(8,128)}), f32[16,3,16,256]{3,2,1,0:T(8,128)S(1)}, u32[]{:S(2)}, u32[]{:S(2)}) %all-to-all-start.1) | async-done | bytes 786464 | tf_op jit(solution)/shard_map/all_to_all | solution.py:298
  60.3 2.8 %collective-permute-start.5 = (f32[4,16,256]{2,1,0:T(8,128)S(1)}, f32[4,16,256]{2,1,0:T(8,128)S(1)}, u32[]{:S(2)}, u32[]{:S(2)}) collective-permute-start(f32[4,16,256]{2,1,0:T(8,128)S(1)} %get-tuple-element.45), channel_id=1, source_target_pairs={{0,1},{1,0},{2,3},{3,2},{4,5},{5,4},{6,7},{7,6},{8,9},{9,8},{10,11... | collective-permute-start | bytes 196616 | tf_op jit(solution)/shard_map/ppermute | solution.py:264
  67.7 5.0 %collective-permute-done.7 = f32[4,16,256]{2,1,0:T(8,128)S(1)} collective-permute-done((f32[4,16,256]{2,1,0:T(8,128)S(1)}, f32[4,16,256]{2,1,0:T(8,128)S(1)}, u32[]{:S(2)}, u32[]{:S(2)}) %collective-permute-start.7) | collective-permute-done | bytes 65568 | tf_op jit(solution)/shard_map/ppermute | solution.py:266
  75.9 16.4 %all_to_all.40.gathered = f32[16,3,16,256]{3,2,1,0:T(8,128)S(1)} all-to-all(f32[16,3,16,256]{3,2,1,0:T(8,128)S(1)} %shard_map.124), channel_id=1, replica_groups=mesh['row'=16,'col'=8] {'row'}, dimensions={0} | all-to-all | bytes 1572864 | tf_op jit(solution)/shard_map/all_to_all | solution.py:298
  100.5 5.0 %collective-permute-done.12 = f32[4,16,256]{2,1,0:T(8,128)S(1)} collective-permute-done((f32[4,16,256]{2,1,0:T(8,128)S(1)}, f32[4,16,256]{2,1,0:T(8,128)S(1)}, u32[]{:S(2)}, u32[]{:S(2)}) %collective-permute-start.12) | collective-permute-done | bytes 65568 | tf_op jit(solution)/shard_map/ppermute | solution.py:266
  108.7 16.5 %all_to_all.41.gathered = f32[16,3,16,256]{3,2,1,0:T(8,128)S(1)} all-to-all(f32[16,3,16,256]{3,2,1,0:T(8,128)S(1)} %shard_map.126), channel_id=1, replica_groups=mesh['row'=16,'col'=8] {'row'}, dimensions={0} | all-to-all | bytes 1572864 | tf_op jit(solution)/shard_map/all_to_all | solution.py:298
  129.8 2.3 collective-permute-start.18
  133.4 5.0 %collective-permute-done.17 = f32[4,16,256]{2,1,0:T(8,128)S(1)} collective-permute-done((f32[4,16,256]{2,1,0:T(8,128)S(1)}, f32[4,16,256]{2,1,0:T(8,128)S(1)}, u32[]{:S(2)}, u32[]{:S(2)}) %collective-permute-start.17) | collective-permute-done | bytes 65568 | tf_op jit(solution)/shard_map/ppermute | solution.py:266
  141.6 16.5 %all_to_all.42.gathered = f32[16,3,16,256]{3,2,1,0:T(8,128)S(1)} all-to-all(f32[16,3,16,256]{3,2,1,0:T(8,128)S(1)} %shard_map.128), channel_id=1, replica_groups=mesh['row'=16,'col'=8] {'row'}, dimensions={0} | all-to-all | bytes 1572864 | tf_op jit(solution)/shard_map/all_to_all | solution.py:298
  162.7 2.3 collective-permute-start.23
  166.4 5.0 %collective-permute-done.22 = f32[4,16,256]{2,1,0:T(8,128)S(1)} collective-permute-done((f32[4,16,256]{2,1,0:T(8,128)S(1)}, f32[4,16,256]{2,1,0:T(8,128)S(1)}, u32[]{:S(2)}, u32[]{:S(2)}) %collective-permute-start.22) | collective-permute-done | bytes 65568 | tf_op jit(solution)/shard_map/ppermute | solution.py:266
  174.6 16.5 %all_to_all.43.gathered = f32[16,3,16,256]{3,2,1,0:T(8,128)S(1)} all-to-all(f32[16,3,16,256]{3,2,1,0:T(8,128)S(1)} %shard_map.130), channel_id=1, replica_groups=mesh['row'=16,'col'=8] {'row'}, dimensions={0} | all-to-all | bytes 1572864 | tf_op jit(solution)/shard_map/all_to_all | solution.py:298
  195.7 2.3 collective-permute-start.28
  199.3 5.0 %collective-permute-done.27 = f32[4,16,256]{2,1,0:T(8,128)S(1)} collective-permute-done((f32[4,16,256]{2,1,0:T(8,128)S(1)}, f32[4,16,256]{2,1,0:T(8,128)S(1)}, u32[]{:S(2)}, u32[]{:S(2)}) %collective-permute-start.27) | collective-permute-done | bytes 65568 | tf_op jit(solution)/shard_map/ppermute | solution.py:266
  207.5 16.5 %all_to_all.44.gathered = f32[16,3,16,256]{3,2,1,0:T(8,128)S(1)} all-to-all(f32[16,3,16,256]{3,2,1,0:T(8,128)S(1)} %shard_map.132), channel_id=1, replica_groups=mesh['row'=16,'col'=8] {'row'}, dimensions={0} | all-to-all | bytes 1572864 | tf_op jit(solution)/shard_map/all_to_all | solution.py:298
  228.6 2.3 collective-permute-start.33
  232.2 5.0 %collective-permute-done.32 = f32[4,16,256]{2,1,0:T(8,128)S(1)} collective-permute-done((f32[4,16,256]{2,1,0:T(8,128)S(1)}, f32[4,16,256]{2,1,0:T(8,128)S(1)}, u32[]{:S(2)}, u32[]{:S(2)}) %collective-permute-start.32) | collective-permute-done | bytes 65568 | tf_op jit(solution)/shard_map/ppermute | solution.py:266
  239.9 9.8 %all_to_all.45.gathered = f32[16,16,128]{2,1,0:T(8,128)S(1)} all-to-all(f32[16,16,128]{2,1,0:T(8,128)S(1)} %get-tuple-element.77), channel_id=1, replica_groups=mesh['row'=16,'col'=8] {'row'}, dimensions={0} | all-to-all | bytes 262144 | tf_op jit(solution)/shard_map/all_to_all | solution.py:325
  (107 shorter events, 74.5 us)
Async XLA Ops:
  2.0 14.4 %all-to-all-start = ((bf16[16,16,256]{2,1,0:T(8,128)(2,1)}), bf16[16,16,256]{2,1,0:T(8,128)(2,1)S(1)}, u32[]{:S(2)}, u32[]{:S(2)}) async-start(bf16[16,16,256]{2,1,0:T(8,128)(2,1)} %broadcast_in_dim.25), calls=%async_computation | async-start | bytes 262144 | tf_op jit(solution)/shard_map/all_to_all | solution.py:275
  23.4 5.8 %collective-permute-start.3 = (f32[4,16,256]{2,1,0:T(8,128)S(1)}, f32[4,16,256]{2,1,0:T(8,128)S(1)}, u32[]{:S(2)}, u32[]{:S(2)}) collective-permute-start(f32[4,16,256]{2,1,0:T(8,128)S(1)} %add.112), channel_id=1, source_target_pairs={{0,6},{1,7},{2,0},{3,1},{4,2},{5,3},{6,4},{7,5},{8,14},{9,15},{10,... | collective-permute-start | bytes 196616 | tf_op jit(solution)/shard_map/ppermute | solution.py:267
  27.2 6.2 %collective-permute-start.2 = (f32[4,16,256]{2,1,0:T(8,128)S(1)}, f32[4,16,256]{2,1,0:T(8,128)S(1)}, u32[]{:S(2)}, u32[]{:S(2)}) collective-permute-start(f32[4,16,256]{2,1,0:T(8,128)S(1)} %add.112), channel_id=1, source_target_pairs={{0,2},{1,3},{2,4},{3,5},{4,6},{5,7},{6,0},{7,1},{8,10},{9,11},{10,... | collective-permute-start | bytes 196616 | tf_op jit(solution)/shard_map/ppermute | solution.py:266
  27.2 6.2 %collective-permute-start.1 = (f32[4,16,256]{2,1,0:T(8,128)S(1)}, f32[4,16,256]{2,1,0:T(8,128)S(1)}, u32[]{:S(2)}, u32[]{:S(2)}) collective-permute-start(f32[4,16,256]{2,1,0:T(8,128)S(1)} %add.112), channel_id=1, source_target_pairs={{0,4},{1,5},{2,6},{3,7},{4,0},{5,1},{6,2},{7,3},{8,12},{9,13},{10,... | collective-permute-start | bytes 196616 | tf_op jit(solution)/shard_map/ppermute | solution.py:265
  39.8 16.4 %all-to-all-start.1 = ((f32[16,3,16,256]{3,2,1,0:T(8,128)}), f32[16,3,16,256]{3,2,1,0:T(8,128)S(1)}, u32[]{:S(2)}, u32[]{:S(2)}) async-start(f32[16,3,16,256]{3,2,1,0:T(8,128)} %shard_map.122), calls=%async_computation.1 | async-start | bytes 1572864 | tf_op jit(solution)/shard_map/all_to_all | solution.py:298
  60.3 3.8 %collective-permute-start.5 = (f32[4,16,256]{2,1,0:T(8,128)S(1)}, f32[4,16,256]{2,1,0:T(8,128)S(1)}, u32[]{:S(2)}, u32[]{:S(2)}) collective-permute-start(f32[4,16,256]{2,1,0:T(8,128)S(1)} %get-tuple-element.45), channel_id=1, source_target_pairs={{0,1},{1,0},{2,3},{3,2},{4,5},{5,4},{6,7},{7,6},{8,9},{9,8},{10,11... | collective-permute-start | bytes 196616 | tf_op jit(solution)/shard_map/ppermute | solution.py:264
  64.0 3.6 %collective-permute-start.8 = (f32[4,16,256]{2,1,0:T(8,128)S(1)}, f32[4,16,256]{2,1,0:T(8,128)S(1)}, u32[]{:S(2)}, u32[]{:S(2)}) collective-permute-start(f32[4,16,256]{2,1,0:T(8,128)S(1)} %add.116), channel_id=1, source_target_pairs={{0,6},{1,7},{2,0},{3,1},{4,2},{5,3},{6,4},{7,5},{8,14},{9,15},{10,... | collective-permute-start | bytes 196616 | tf_op jit(solution)/shard_map/ppermute | solution.py:267
  66.3 6.3 %collective-permute-start.7 = (f32[4,16,256]{2,1,0:T(8,128)S(1)}, f32[4,16,256]{2,1,0:T(8,128)S(1)}, u32[]{:S(2)}, u32[]{:S(2)}) collective-permute-start(f32[4,16,256]{2,1,0:T(8,128)S(1)} %add.116), channel_id=1, source_target_pairs={{0,2},{1,3},{2,4},{3,5},{4,6},{5,7},{6,0},{7,1},{8,10},{9,11},{10,... | collective-permute-start | bytes 196616 | tf_op jit(solution)/shard_map/ppermute | solution.py:266
  66.3 6.3 %collective-permute-start.6 = (f32[4,16,256]{2,1,0:T(8,128)S(1)}, f32[4,16,256]{2,1,0:T(8,128)S(1)}, u32[]{:S(2)}, u32[]{:S(2)}) collective-permute-start(f32[4,16,256]{2,1,0:T(8,128)S(1)} %add.116), channel_id=1, source_target_pairs={{0,4},{1,5},{2,6},{3,7},{4,0},{5,1},{6,2},{7,3},{8,12},{9,13},{10,... | collective-permute-start | bytes 196616 | tf_op jit(solution)/shard_map/ppermute | solution.py:265
  96.9 3.6 %collective-permute-start.13 = (f32[4,16,256]{2,1,0:T(8,128)S(1)}, f32[4,16,256]{2,1,0:T(8,128)S(1)}, u32[]{:S(2)}, u32[]{:S(2)}) collective-permute-start(f32[4,16,256]{2,1,0:T(8,128)S(1)} %add.120), channel_id=1, source_target_pairs={{0,6},{1,7},{2,0},{3,1},{4,2},{5,3},{6,4},{7,5},{8,14},{9,15},{10,... | collective-permute-start | bytes 196616 | tf_op jit(solution)/shard_map/ppermute | solution.py:267
  99.2 6.3 %collective-permute-start.12 = (f32[4,16,256]{2,1,0:T(8,128)S(1)}, f32[4,16,256]{2,1,0:T(8,128)S(1)}, u32[]{:S(2)}, u32[]{:S(2)}) collective-permute-start(f32[4,16,256]{2,1,0:T(8,128)S(1)} %add.120), channel_id=1, source_target_pairs={{0,2},{1,3},{2,4},{3,5},{4,6},{5,7},{6,0},{7,1},{8,10},{9,11},{10,... | collective-permute-start | bytes 196616 | tf_op jit(solution)/shard_map/ppermute | solution.py:266
  99.2 6.3 %collective-permute-start.11 = (f32[4,16,256]{2,1,0:T(8,128)S(1)}, f32[4,16,256]{2,1,0:T(8,128)S(1)}, u32[]{:S(2)}, u32[]{:S(2)}) collective-permute-start(f32[4,16,256]{2,1,0:T(8,128)S(1)} %add.120), channel_id=1, source_target_pairs={{0,4},{1,5},{2,6},{3,7},{4,0},{5,1},{6,2},{7,3},{8,12},{9,13},{10,... | collective-permute-start | bytes 196616 | tf_op jit(solution)/shard_map/ppermute | solution.py:265
  129.8 3.6 %collective-permute-start.18 = (f32[4,16,256]{2,1,0:T(8,128)S(1)}, f32[4,16,256]{2,1,0:T(8,128)S(1)}, u32[]{:S(2)}, u32[]{:S(2)}) collective-permute-start(f32[4,16,256]{2,1,0:T(8,128)S(1)} %add.124), channel_id=1, source_target_pairs={{0,6},{1,7},{2,0},{3,1},{4,2},{5,3},{6,4},{7,5},{8,14},{9,15},{10,... | collective-permute-start | bytes 196616 | tf_op jit(solution)/shard_map/ppermute | solution.py:267
  132.1 6.3 %collective-permute-start.17 = (f32[4,16,256]{2,1,0:T(8,128)S(1)}, f32[4,16,256]{2,1,0:T(8,128)S(1)}, u32[]{:S(2)}, u32[]{:S(2)}) collective-permute-start(f32[4,16,256]{2,1,0:T(8,128)S(1)} %add.124), channel_id=1, source_target_pairs={{0,2},{1,3},{2,4},{3,5},{4,6},{5,7},{6,0},{7,1},{8,10},{9,11},{10,... | collective-permute-start | bytes 196616 | tf_op jit(solution)/shard_map/ppermute | solution.py:266
  132.1 6.3 %collective-permute-start.16 = (f32[4,16,256]{2,1,0:T(8,128)S(1)}, f32[4,16,256]{2,1,0:T(8,128)S(1)}, u32[]{:S(2)}, u32[]{:S(2)}) collective-permute-start(f32[4,16,256]{2,1,0:T(8,128)S(1)} %add.124), channel_id=1, source_target_pairs={{0,4},{1,5},{2,6},{3,7},{4,0},{5,1},{6,2},{7,3},{8,12},{9,13},{10,... | collective-permute-start | bytes 196616 | tf_op jit(solution)/shard_map/ppermute | solution.py:265
  162.7 3.6 %collective-permute-start.23 = (f32[4,16,256]{2,1,0:T(8,128)S(1)}, f32[4,16,256]{2,1,0:T(8,128)S(1)}, u32[]{:S(2)}, u32[]{:S(2)}) collective-permute-start(f32[4,16,256]{2,1,0:T(8,128)S(1)} %add.128), channel_id=1, source_target_pairs={{0,6},{1,7},{2,0},{3,1},{4,2},{5,3},{6,4},{7,5},{8,14},{9,15},{10,... | collective-permute-start | bytes 196616 | tf_op jit(solution)/shard_map/ppermute | solution.py:267
  165.0 6.3 %collective-permute-start.22 = (f32[4,16,256]{2,1,0:T(8,128)S(1)}, f32[4,16,256]{2,1,0:T(8,128)S(1)}, u32[]{:S(2)}, u32[]{:S(2)}) collective-permute-start(f32[4,16,256]{2,1,0:T(8,128)S(1)} %add.128), channel_id=1, source_target_pairs={{0,2},{1,3},{2,4},{3,5},{4,6},{5,7},{6,0},{7,1},{8,10},{9,11},{10,... | collective-permute-start | bytes 196616 | tf_op jit(solution)/shard_map/ppermute | solution.py:266
  165.1 6.3 %collective-permute-start.21 = (f32[4,16,256]{2,1,0:T(8,128)S(1)}, f32[4,16,256]{2,1,0:T(8,128)S(1)}, u32[]{:S(2)}, u32[]{:S(2)}) collective-permute-start(f32[4,16,256]{2,1,0:T(8,128)S(1)} %add.128), channel_id=1, source_target_pairs={{0,4},{1,5},{2,6},{3,7},{4,0},{5,1},{6,2},{7,3},{8,12},{9,13},{10,... | collective-permute-start | bytes 196616 | tf_op jit(solution)/shard_map/ppermute | solution.py:265
  195.7 3.6 %collective-permute-start.28 = (f32[4,16,256]{2,1,0:T(8,128)S(1)}, f32[4,16,256]{2,1,0:T(8,128)S(1)}, u32[]{:S(2)}, u32[]{:S(2)}) collective-permute-start(f32[4,16,256]{2,1,0:T(8,128)S(1)} %add.132), channel_id=1, source_target_pairs={{0,6},{1,7},{2,0},{3,1},{4,2},{5,3},{6,4},{7,5},{8,14},{9,15},{10,... | collective-permute-start | bytes 196616 | tf_op jit(solution)/shard_map/ppermute | solution.py:267
  198.0 6.3 %collective-permute-start.27 = (f32[4,16,256]{2,1,0:T(8,128)S(1)}, f32[4,16,256]{2,1,0:T(8,128)S(1)}, u32[]{:S(2)}, u32[]{:S(2)}) collective-permute-start(f32[4,16,256]{2,1,0:T(8,128)S(1)} %add.132), channel_id=1, source_target_pairs={{0,2},{1,3},{2,4},{3,5},{4,6},{5,7},{6,0},{7,1},{8,10},{9,11},{10,... | collective-permute-start | bytes 196616 | tf_op jit(solution)/shard_map/ppermute | solution.py:266
  198.0 6.3 %collective-permute-start.26 = (f32[4,16,256]{2,1,0:T(8,128)S(1)}, f32[4,16,256]{2,1,0:T(8,128)S(1)}, u32[]{:S(2)}, u32[]{:S(2)}) collective-permute-start(f32[4,16,256]{2,1,0:T(8,128)S(1)} %add.132), channel_id=1, source_target_pairs={{0,4},{1,5},{2,6},{3,7},{4,0},{5,1},{6,2},{7,3},{8,12},{9,13},{10,... | collective-permute-start | bytes 196616 | tf_op jit(solution)/shard_map/ppermute | solution.py:265
  228.6 3.6 %collective-permute-start.33 = (f32[4,16,256]{2,1,0:T(8,128)S(1)}, f32[4,16,256]{2,1,0:T(8,128)S(1)}, u32[]{:S(2)}, u32[]{:S(2)}) collective-permute-start(f32[4,16,256]{2,1,0:T(8,128)S(1)} %add.136), channel_id=1, source_target_pairs={{0,6},{1,7},{2,0},{3,1},{4,2},{5,3},{6,4},{7,5},{8,14},{9,15},{10,... | collective-permute-start | bytes 196616 | tf_op jit(solution)/shard_map/ppermute | solution.py:267
  230.9 6.3 %collective-permute-start.32 = (f32[4,16,256]{2,1,0:T(8,128)S(1)}, f32[4,16,256]{2,1,0:T(8,128)S(1)}, u32[]{:S(2)}, u32[]{:S(2)}) collective-permute-start(f32[4,16,256]{2,1,0:T(8,128)S(1)} %add.136), channel_id=1, source_target_pairs={{0,2},{1,3},{2,4},{3,5},{4,6},{5,7},{6,0},{7,1},{8,10},{9,11},{10,... | collective-permute-start | bytes 196616 | tf_op jit(solution)/shard_map/ppermute | solution.py:266
  230.9 6.3 %collective-permute-start.31 = (f32[4,16,256]{2,1,0:T(8,128)S(1)}, f32[4,16,256]{2,1,0:T(8,128)S(1)}, u32[]{:S(2)}, u32[]{:S(2)}) collective-permute-start(f32[4,16,256]{2,1,0:T(8,128)S(1)} %add.136), channel_id=1, source_target_pairs={{0,4},{1,5},{2,6},{3,7},{4,0},{5,1},{6,2},{7,3},{8,12},{9,13},{10,... | collective-permute-start | bytes 196616 | tf_op jit(solution)/shard_map/ppermute | solution.py:265
  (20 other events, 156.2 us)

commit v2 on v1

v2 whole, which is shorter than its diff:
```python
import functools

import jax
import jax.numpy as jnp
from jax import lax
from jax.experimental import pallas as pl
from jax.experimental.pallas import tpu as pltpu
from jax.sharding import PartitionSpec as P


NV = 16
SHIFTS = 4
ITERS = 3
EPSILON = 1e-06
DEGREE = 2 * ITERS
FLOOR = 0.1
LANES = 128
CHUNKS = 8
F32 = jnp.float32
BF16 = jnp.bfloat16

PLACE_Z, PLACE_ROW, SLOTS = 0, 1, 8
D_FROM, D_TO, DIRECT_FROM, DIRECT_TO, BACK_FROM, BACK_TO = range(6)
ALPHA, BETA, GAMMA, TOTAL, CENTRE, NEXT, GRAM = 0, 1, 2, 3, 4, 5, 8

VM = pl.BlockSpec(memory_space=pltpu.VMEM)
HBM = pl.BlockSpec(memory_space=pltpu.HBM)
SM = pl.BlockSpec(memory_space=pltpu.SMEM)


def call(kernel, out_shape, n_smem, n_vmem, scratch=()):
    return pl.pallas_call(
        kernel,
        out_shape=out_shape,
        in_specs=[SM] * n_smem + [VM] * n_vmem,
        out_specs=jax.tree.map(lambda _: VM, out_shape),
        scratch_shapes=list(scratch),
        compiler_params=pltpu.CompilerParams(vmem_limit_bytes=24 << 20),
    )


def split_into(target, index, value):
    upper = value.astype(BF16)
    target[index, :NV] = upper
    target[index, NV:] = (value - upper.astype(F32)).astype(BF16)


def wide_of(stack, first, parts):
    return jnp.concatenate([stack[first + i * NV : first + (i + 1) * NV] for i in range(parts)], axis=1)


def entry(table, kind, t, slots):
    return table[SLOTS + kind * slots + t]


def row_sum(*blocks):
    total = None
    for a in blocks:
        for i in range(a.shape[0]):
            total = a[i] if total is None else total + a[i]
    return total


def slab_sum(mine, other):
    return jnp.sum(row_sum(mine), axis=-1, keepdims=True) + jnp.sum(row_sum(other), axis=-1, keepdims=True)


def slab_dot(a, b):
    return slab_sum(a[0] * b[0], a[1] * b[1])


def pack(parts):
    lane = lax.broadcasted_iota(jnp.int32, (8, LANES), 1)
    out = jnp.zeros((8, LANES), F32)
    for i, part in enumerate(parts):
        out = jnp.where(lane == i, part[:8], out)
        out = jnp.where(lane == i + LANES // 2, part[8:], out)
    return out


def unpack(dots, i):
    j = i + LANES // 2
    return jnp.concatenate([dots[:, i : i + 1], dots[:, j : j + 1]], axis=0)


def lanes_of(parts, shape):
    lane = lax.broadcasted_iota(jnp.int32, shape, 1)
    out = jnp.zeros(shape, F32)
    for i, part in parts.items():
        out = jnp.where(lane == i, part, out)
    return out


def load_slab(mine, other):
    if len(mine.shape) == 3:
        return mine[...], other[...]
    parts = 2
    half = mine.shape[0] // (parts * NV)
    return tuple(jnp.stack([wide_of(ref, b * parts * NV, parts) for b in range(half)]) for ref in (mine, other))


def dipole_kernel(table, gathered, energies_hbm, tiles_hbm, p_mine, p_other, xs, acc, energies, tiles, sems):
    slots = tiles.shape[0]
    step = slots // CHUNKS
    copies = [
        pltpu.make_async_copy(tiles_hbm.at[pl.ds(c * step, step)], tiles.at[pl.ds(c * step, step)], sems.at[c])
        for c in range(CHUNKS)
    ]
    copies.append(pltpu.make_async_copy(energies_hbm, energies, sems.at[CHUNKS]))
    for copy in copies:
        copy.start()
    groups = gathered.shape[0]
    half = acc.shape[0] // 2
    for i in range(groups):
        xs[i] = gathered[i]
    xs[groups] = jnp.zeros(xs.shape[1:], BF16)
    acc[...] = jnp.zeros(acc.shape, F32)
    for t in range(tiles.shape[0]):
        if t % step == 0:
            copies[t // step].wait()
        x = xs[entry(table, D_FROM, t, slots)]
        res = lax.dot_general(x, tiles[t], (((1,), (1,)), ((), ())), preferred_element_type=F32)
        acc[entry(table, D_TO, t, slots)] += res
    copies[CHUNKS].wait()
    parts = acc.shape[2] // LANES
    for b in range(half):
        for i in range(parts):
            span = slice((b * parts + i) * NV, (b * parts + i + 1) * NV)
            p_mine[span] = acc[b, :, i * LANES : (i + 1) * LANES]
            p_other[span] = acc[half + b, :, i * LANES : (i + 1) * LANES]
    total = jnp.broadcast_to(jnp.sum(energies[...], axis=1, keepdims=True), (8, LANES))
    p_mine[half * parts * NV :] = total
    p_other[half * parts * NV :] = total


def back_kernel(table, z_mine, z_other, *refs):
    tiles, out, ys = refs[-3:]
    qs = [(refs[i], refs[i + 1]) for i in range(0, len(refs) - 3, 2)]
    z = load_slab(z_mine, z_other)
    half = z[0].shape[0]
    slots = tiles.shape[0]
    for i in range(half):
        split_into(ys, i, z[0][i])
        split_into(ys, half + i, z[1][i])
    ys[2 * half] = jnp.zeros(ys.shape[1:], BF16)
    if qs:
        q = [(m[...], o[...]) for m, o in qs]
        dots = [slab_dot(z, z), slab_dot(z, q[-1]), slab_dot(z, q[-2]) if len(q) > 1 else None, slab_sum(*q[-1])]
        dots = [jnp.zeros((NV, 1), F32) if d is None else d for d in dots]
        dots += [slab_dot(q[-1], other) for other in q]
    else:
        centre = z_mine[-8:, 0:1]
        dots = [slab_dot(z, z), jnp.concatenate([centre, centre], axis=0)]
    dots = pack(dots)
    if len(z_mine.shape) == 3:
        own = z_mine[table[PLACE_Z]]
    else:
        own = z[0][0]
        for i in range(1, half):
            own = jnp.where(table[PLACE_Z] == i, z[0][i], own)
    parts = own.shape[1] // LANES
    for p in range(out.shape[0]):
        for i in range(parts):
            out[p, i * NV : (i + 1) * NV] = own[:, i * LANES : (i + 1) * LANES]
            out[p, (parts + i) * NV : (parts + i + 1) * NV] = jnp.zeros((NV, LANES), F32)
        out[p, 2 * parts * NV :] = dots
    for t in range(tiles.shape[0]):
        y = ys[entry(table, BACK_FROM, t, slots)]
        res = jnp.dot(y, tiles[t], preferred_element_type=F32)
        res = res[:NV] + res[NV:]
        peer = entry(table, BACK_TO, t, slots)
        for i in range(parts):
            out[peer, (parts + i) * NV : (parts + i + 1) * NV] += res[:, i * LANES : (i + 1) * LANES]


def direct_kernel(states_n, step, table, gathered, tiles, energies, z_mine, z_other, *refs):
    p_mine, p_other, qn_mine, qn_other, state_out, xs, acc = refs[-7:]
    extra = list(refs[:-7])
    groups = gathered.shape[0]
    half = p_mine.shape[0]
    slots = tiles.shape[0]
    parts = acc.shape[2] // LANES
    for i in range(groups):
        split_into(xs, i, wide_of(gathered[i], 0, parts))
    xs[groups] = jnp.zeros(xs.shape[1:], BF16)
    acc[...] = jnp.zeros(acc.shape, F32)
    for t in range(tiles.shape[0]):
        x = xs[entry(table, DIRECT_FROM, t, slots)]
        res = lax.dot_general(x, tiles[t], (((1,), (1,)), ((), ())), preferred_element_type=F32)
        acc[entry(table, DIRECT_TO, t, slots)] += res[:NV] + res[NV:]
    rest = gathered[0, parts * NV :]
    for i in range(1, groups):
        rest = rest + gathered[i, parts * NV :]
    back = wide_of(rest, 0, parts)
    dots = rest[parts * NV :]
    norm = unpack(dots, 0)
    z = load_slab(z_mine, z_other)
    own = wide_of(gathered[table[PLACE_ROW]], 0, parts)
    lanes = {}
    if step == 0:
        centre = unpack(dots, 1) * (1.0 / states_n)
        beta = jnp.sqrt(norm + 1e-30)
        scale = 1.0 / beta
        qn = [z[0] * scale, z[1] * scale]
        local = (energies[...] - centre) * own + back
    else:
        state = extra[0][...]
        q = (extra[1][...], extra[2][...])
        centre = state[:, CENTRE : CENTRE + 1]
        size = unpack(dots, 3 + step)
        alpha = unpack(dots, 1) / size
        square = norm - alpha * alpha * size
        qn = [z[0] - alpha * q[0], z[1] - alpha * q[1]]
        local = (energies[...] - centre) * own + back - alpha * own
        lanes.update({ALPHA: alpha, TOTAL: unpack(dots, 3)})
        lanes.update({GRAM + i: unpack(dots, 4 + i) for i in range(step)})
        if step > 1:
            old = (extra[3][...], extra[4][...])
            z_old = extra[5]
            size_old = state[:, GRAM + step - 2 : GRAM + step - 1]
            gamma = unpack(dots, 2) / size_old
            square = square - gamma * gamma * size_old
            qn = [a - gamma * b for a, b in zip(qn, old)]
            local = local - gamma * wide_of(z_old[table[PLACE_ROW]], 0, parts)
            lanes[GAMMA] = gamma
        beta_square = jnp.maximum(square, FLOOR * FLOOR * norm) + 1e-30
        beta = jnp.sqrt(beta_square)
        scale = 1.0 / beta
        qn = [a * scale for a in qn]
        lanes[NEXT] = jnp.maximum(square, 0.0) / beta_square
    lanes.update({BETA: beta, CENTRE: centre})
    state_out[...] = lanes_of(lanes, state_out.shape)
    qn_mine[...] = qn[0]
    qn_other[...] = qn[1]
    acc[table[PLACE_Z]] += local
    p_mine[...] = acc[:half] * scale
    p_other[...] = acc[half:] * scale


def apply_h(coefs, alphas, betas, gammas, shift):
    out = [None] * (DEGREE + 1)

    def add(j, value):
        out[j] = value if out[j] is None else out[j] + value

    for j, c in enumerate(coefs):
        if c is None:
            continue
        if j + 1 < DEGREE:
            add(j + 1, betas[j + 1] * c)
            add(j, (alphas[j] - shift) * c)
            if j:
                add(j - 1, gammas[j] * c)
        else:
            add(j, -shift * c)
            add(DEGREE, c)
    return out


def vec(op, *vectors):
    return [op(*[0.0 if e is None else e for e in es]) if any(e is not None for e in es) else None for es in zip(*vectors)]


def total_of(terms):
    return functools.reduce(lambda x, y: x + y, terms)


def finish_kernel(table, *refs):
    states, qs, z_mine = refs[:DEGREE], refs[DEGREE : 2 * DEGREE], refs[2 * DEGREE]
    solution_out, residual_out, aux_out = refs[2 * DEGREE + 1 :]
    shape = aux_out.shape[1:]
    full = [s[...] for s in states]
    spread = lambda step, i: jnp.broadcast_to(full[step][:, i : i + 1], shape)
    lane = lax.broadcasted_iota(jnp.int32, shape, 1)
    shift = -2.0 + 4.0 * (lane.astype(F32) + 0.5) / SHIFTS - spread(0, CENTRE)
    alphas = [spread(j + 1, ALPHA) for j in range(DEGREE - 1)]
    gammas = [None] + [spread(j + 1, GAMMA) for j in range(1, DEGREE - 1)]
    betas = [spread(j, BETA) for j in range(DEGREE)]
    sums = [spread(j + 1, TOTAL) for j in range(DEGREE - 1)]
    gram = [[spread(j + 1, GRAM + i) for i in range(j + 1)] for j in range(DEGREE - 1)]
    gram.append([None] * (DEGREE - 1) + [spread(DEGREE - 1, NEXT)])

    def inner(a, b):
        terms = []
        for j, x in enumerate(a[:DEGREE]):
            for i, y in enumerate(b[:DEGREE]):
                g = gram[max(i, j)][min(i, j)]
                if x is not None and y is not None and g is not None:
                    terms.append(x * (g * y))
        return total_of(terms)

    residual = [betas[0]] + [None] * DEGREE
    direction = list(residual)
    answer = [None] * (DEGREE + 1)
    norm_now = inner(residual, residual)
    for index in range(ITERS):
        inside = apply_h(direction, alphas, betas, gammas, shift)
        image = vec(lambda x, y: x + y, apply_h(inside, alphas, betas, gammas, shift), direction)
        curvature = inner(inside, inside) + inner(direction, direction)
        alpha = norm_now / curvature
        image_sum = total_of([c * s for c, s in zip(image, sums) if c is not None])
        image_square = inner(image, image)
        if index + 1 < ITERS:
            aux_out[index] = image_sum / jnp.sqrt(image_square + EPSILON)
        answer = vec(lambda x, d: x + alpha * d, answer, direction)
        residual = vec(lambda x, d: x - alpha * d, residual, image)
        if index + 1 < ITERS:
            norm_next = inner(residual, residual)
            ratio = norm_next / norm_now
            direction = vec(lambda x, d: x + ratio * d, residual, direction)
            norm_now = norm_next
    aux_out[ITERS - 1] = image_sum
    aux_out[ITERS] = image_square
    for i, c in enumerate(image):
        aux_out[ITERS + 1 + i] = c
    own = [q[table[PLACE_Z]] for q in qs] + [z_mine[table[PLACE_Z]]]
    for k in range(SHIFTS):
        rows = slice(k * NV, (k + 1) * NV)
        solution_out[rows] = total_of([c[:, k : k + 1] * b for c, b in zip(answer, own) if c is not None])
        residual_out[rows] = total_of([c[:, k : k + 1] * b for c, b in zip(residual, own)])


def dots_kernel(*refs):
    arrays, dots_out = [r[...] for r in refs[:-1]], refs[-1]
    z, *q = [(arrays[i], arrays[i + 1]) for i in range(0, len(arrays), 2)]
    dots = pack([slab_dot(z, z), slab_sum(*z), slab_sum(*q[-1])] + [slab_dot(z, b) for b in q])
    for p in range(dots_out.shape[0]):
        dots_out[p] = dots


def check_kernel(gathered, aux, out):
    dots = gathered[0]
    for i in range(1, gathered.shape[0]):
        dots = dots + gathered[i]
    norm, total, total_q = (unpack(dots, i) for i in range(3))
    image = [aux[ITERS + 1 + i] for i in range(DEGREE + 1)]
    last = image[DEGREE]
    image_sum = aux[ITERS - 1] + image[DEGREE - 1] * total_q + last * total
    cross = total_of([image[i] * unpack(dots, 3 + i) for i in range(DEGREE)])
    image_square = aux[ITERS] + last * (2.0 * cross + last * norm)
    checks = [aux[i] for i in range(ITERS - 1)] + [image_sum / jnp.sqrt(image_square + EPSILON)]
    for i, row in enumerate(checks):
        flipped = jnp.transpose(row)
        for k in range(SHIFTS):
            out[i : i + 1, k * NV : (k + 1) * NV] = flipped[k : k + 1]


def body(
    sources,
    dipole_tiles,
    dipole_rows,
    dipole_columns,
    dipole_count,
    energies,
    h_tiles,
    tile_rows,
    tile_columns,
    tile_count,
):
    width = sources.shape[1]
    rows_n = lax.axis_size("row")
    cols_n = lax.axis_size("col")
    half = cols_n // 2
    col = lax.axis_index("col")
    parity = col & 1
    slots = tile_rows.shape[0]

    def slot_lists(rows, columns, count):
        live = jnp.arange(slots, dtype=jnp.int32) < count[0]
        position = ((rows & 1) ^ parity) * half + (rows >> 1)
        return [jnp.where(live, columns, rows_n), position, jnp.where(live, position, cols_n), columns]

    spot = jnp.arange(SLOTS, dtype=jnp.int32)
    spot = jnp.where(spot == PLACE_Z, col >> 1, lax.axis_index("row"))
    table = jnp.concatenate(
        [spot]
        + slot_lists(dipole_rows, dipole_columns, dipole_count)[:2]
        + slot_lists(tile_rows, tile_columns, tile_count)
    ).astype(jnp.int32)

    pair = [(i, i ^ 1) for i in range(cols_n)]
    ring = lambda d: [(2 * z + k, 2 * ((z + d) % half) + k) for z in range(half) for k in range(2)]

    def group_sum(p_mine, p_other):
        q = p_mine + lax.ppermute(p_other, "col", pair)
        moved = []
        for d in (2, 1, 3):
            moved.append(lax.ppermute(q, "col", ring(d)))
        mine = (q + moved[0]) + (moved[1] + moved[2])
        return mine, lax.ppermute(mine, "col", pair)

    block = jax.ShapeDtypeStruct((half, NV, width), F32)
    stack = jax.ShapeDtypeStruct((half * NV * width // LANES + 8, LANES), F32)
    small = jax.ShapeDtypeStruct((NV, LANES), F32)
    diagonal = energies[None]

    spread = jnp.broadcast_to(sources[None], (rows_n,) + sources.shape)
    gathered = lax.all_to_all(spread, "row", 0, 0, tiled=True)
    p_mine, p_other = pl.pallas_call(
        dipole_kernel,
        out_shape=(stack, stack),
        in_specs=[SM, VM, HBM, HBM],
        out_specs=(VM, VM),
        scratch_shapes=[
            pltpu.VMEM((rows_n + 1, NV, width), BF16),
            pltpu.VMEM((cols_n, NV, width), F32),
            pltpu.VMEM(diagonal.shape, F32),
            pltpu.VMEM(dipole_tiles.shape, BF16),
            pltpu.SemaphoreType.DMA((CHUNKS + 1,)),
        ],
        compiler_params=pltpu.CompilerParams(vmem_limit_bytes=24 << 20),
    )(table, gathered, *(pltpu.with_memory_space_constraint(a, pltpu.HBM) for a in (diagonal, dipole_tiles)))
    z = group_sum(p_mine, p_other)

    states, basis, received = [], [], []
    for step in range(DEGREE):
        pairs = [array for q in basis for array in q]
        payload = call(
            back_kernel,
            jax.ShapeDtypeStruct((rows_n, 2 * NV * width // LANES + 8, LANES), F32),
            1,
            3 + len(pairs),
            [pltpu.VMEM((cols_n + 1, 2 * NV, width), BF16)],
        )(table, *z, *pairs, h_tiles)
        received.append(lax.all_to_all(payload, "row", 0, 0, tiled=True))
        extra = []
        if step > 0:
            extra = [states[-1], *basis[-1]]
        if step > 1:
            extra += [*basis[-2], received[-2]]
        p_mine, p_other, qn_mine, qn_other, state = call(
            functools.partial(direct_kernel, float(rows_n * cols_n * width), step),
            (block, block, block, block, small),
            1,
            5 + len(extra),
            [pltpu.VMEM((rows_n + 1, 2 * NV, width), BF16), pltpu.VMEM((cols_n, NV, width), F32)],
        )(table, received[-1], h_tiles, diagonal, *z, *extra)
        states.append(state)
        basis.append((qn_mine, qn_other))
        z = group_sum(p_mine, p_other)

    pairs = [array for q in basis for array in q]
    dots = call(dots_kernel, jax.ShapeDtypeStruct((rows_n, 8, LANES), F32), 0, 2 + len(pairs))(*z, *pairs)
    dots = lax.all_to_all(dots, "row", 0, 0, tiled=True)
    result = jax.ShapeDtypeStruct((SHIFTS * NV, width), F32)
    answer, residual, aux = call(
        finish_kernel,
        (result, result, jax.ShapeDtypeStruct((ITERS + 2 + DEGREE, NV, LANES), F32)),
        1,
        2 * DEGREE + 1,
    )(table, *states, *[q[0] for q in basis], z[0])
    checks = call(check_kernel, jax.ShapeDtypeStruct((ITERS, SHIFTS * NV), F32), 0, 2)(dots, aux)
    return answer, residual, checks


def solution(mesh):
    both = ("row", "col")
    return jax.shard_map(
        body,
        mesh=mesh,
        in_specs=(
            P(None, both),
            P(both, None, None),
            P(both),
            P(both),
            P(both),
            P(both),
            P(both, None, None),
            P(both),
            P(both),
            P(both),
        ),
        out_specs=(P(None, both), P(None, both), P()),
        check_vma=False,
    )
```

time: 252 us -> 233 us (0.925)
  waiting for transfers between devices: 64.6 us -> 55.6 us
  local copies, waits for them, and re-layouts: 8.65 us -> 2.09 us
  blocking collectives: 92.1 us -> 86.9 us
  Pallas kernels: 24.1 us -> 27.3 us
    all_to_all x1, waiting for transfers between devices: 12.7 us -> 4.75 us  [body(): dots = lax.all_to_all(dots, 'row', 0, 0, tiled=True)]
    unnamed x14 -> x4, local copies, waits for them, and re-layouts: 6.58 us -> 0.01 us
    all_to_all x6, blocking collectives: 92.1 us -> 86.9 us  [body(): received.append(lax.all_to_all(payload, 'row', 0, 0, tiled=True))]
    pallas_call x16, Pallas kernels: 24.1 us -> 27.3 us  [the longest x6 11.4 us: body(): call(functools.partial(direct_kernel, float(rows_n * cols_n * width), ste...]
    all_to_all x1, waiting for transfers between devices: 5.52 us -> 2.83 us  [body(): gathered = lax.all_to_all(spread, 'row', 0, 0, tiled=True)]
  transfers between devices with their start and end apart: 37 -> 37, of which waited for: 28 -> 30; matrix products, arithmetic and copies ran while one was open for 0% -> 1% of each run, Pallas kernels for 0% -> 1%
where the time goes in v2:
time: 233 us; the launch traced here: 232 us
  blocking collectives  86.9 us (37%)
  starting transfers between devices  56.2 us (24%)
  waiting for transfers between devices  55.6 us (24%)
  Pallas kernels  27.3 us (12%)
    all_to_all x6, blocking collectives, body(): received.append(lax.all_to_all(payload, 'row', 0, 0, tiled=True))  86.9 us
    ppermute x21, waiting for transfers between devices, group_sum(): moved.append(lax.ppermute(q, 'col', ring(d)))  35.4 us
    ppermute x21, starting transfers between devices, group_sum(): moved.append(lax.ppermute(q, 'col', ring(d)))  26.4 us
    ppermute x7, starting transfers between devices, group_sum(): q = p_mine + lax.ppermute(p_other, 'col', pair)  12.5 us
    pallas_call x6, Pallas kernels, body(): call(functools.partial(direct_kernel, float(rows_n * cols_n * width), ste...  11.4 us
    pallas_call x6, Pallas kernels, body(): call(back_kernel, jax.ShapeDtypeStruct((rows_n, 2 * NV * width // LANES +...  8.43 us
    all_to_all x1, starting transfers between devices, body(): gathered = lax.all_to_all(spread, 'row', 0, 0, tiled=True)  7.57 us
    ppermute x7, waiting for transfers between devices, group_sum(): return (mine, lax.ppermute(mine, 'col', pair))  6.32 us
  transfers between devices with their start and end apart: 37, of which 30 were waited for; matrix products, arithmetic and copies ran while one was open for 1% of the time, Pallas kernels for 1%

profile of v2, /device:TPU:1, one launch (start us, length us, event | category | flops | bytes accessed | tf_op | source)
XLA Modules:
  0.0 232.5 jit_solution(8277090745466712076)
XLA Ops:
  2.0 7.6 %all-to-all-start = ((bf16[16,16,256]{2,1,0:T(8,128)(2,1)}), bf16[16,16,256]{2,1,0:T(8,128)(2,1)S(1)}, u32[]{:S(2)}, u32[]{:S(2)}) async-start(bf16[16,16,256]{2,1,0:T(8,128)(2,1)} %broadcast_in_dim.29), calls=%async_computation | async-start | bytes 262144 | tf_op jit(solution)/shard_map/all_to_all | solution.py:398
  13.6 2.8 %all-to-all-done.gathered = bf16[16,16,256]{2,1,0:T(8,128)(2,1)S(1)} async-done(((bf16[16,16,256]{2,1,0:T(8,128)(2,1)}), bf16[16,16,256]{2,1,0:T(8,128)(2,1)S(1)}, u32[]{:S(2)}, u32[]{:S(2)}) %all-to-all-start) | async-done | bytes 131104 | tf_op jit(solution)/shard_map/all_to_all | solution.py:398
  16.4 4.1 %shard_map.121 = (f32[136,128]{1,0:T(8,128)S(1)}, f32[136,128]{1,0:T(8,128)S(1)}) custom-call(s32[200]{0:T(256)S(1)} %concatenate.3.table, bf16[16,16,256]{2,1,0:T(8,128)(2,1)S(1)} %all-to-all-done.gathered, f32[1,256]{1,0:T(1,128)} %bitcast.6, bf16[32,256,256]{2,1,0:T(8,128)(2,1)} %tiles_hbm.1), custom_call_target="tpu_custom_call" | custom-call | tf_op jit(solution)/shard_map/pallas_call | solution.py:399
  23.5 3.8 %collective-permute-start.3 = (f32[136,128]{1,0:T(8,128)S(1)}, f32[136,128]{1,0:T(8,128)S(1)}, u32[]{:S(2)}, u32[]{:S(2)}) collective-permute-start(f32[136,128]{1,0:T(8,128)S(1)} %add.92), channel_id=1, source_target_pairs={{0,6},{1,7},{2,0},{3,1},{4,2},{5,3},{6,4},{7,5},{8,14},{9,15},{10,... | collective-permute-start | bytes 208904 | tf_op jit(solution)/shard_map/ppermute | solution.py:388
  28.7 5.0 %collective-permute-done.2 = f32[136,128]{1,0:T(8,128)S(1)} collective-permute-done((f32[136,128]{1,0:T(8,128)S(1)}, f32[136,128]{1,0:T(8,128)S(1)}, u32[]{:S(2)}, u32[]{:S(2)}) %collective-permute-start.2) | collective-permute-done | bytes 69664 | tf_op jit(solution)/shard_map/ppermute | solution.py:388
  37.0 14.6 %all_to_all.40.gathered = f32[16,72,128]{2,1,0:T(8,128)S(1)} all-to-all(f32[16,72,128]{2,1,0:T(8,128)S(1)} %shard_map.122), channel_id=1, replica_groups=mesh['row'=16,'col'=8] {'row'}, dimensions={0} | all-to-all | bytes 1179648 | tf_op jit(solution)/shard_map/all_to_all | solution.py:425
  59.7 5.0 %collective-permute-done.7 = f32[4,16,256]{2,1,0:T(8,128)S(1)} collective-permute-done((f32[4,16,256]{2,1,0:T(8,128)S(1)}, f32[4,16,256]{2,1,0:T(8,128)S(1)}, u32[]{:S(2)}, u32[]{:S(2)}) %collective-permute-start.7) | collective-permute-done | bytes 65568 | tf_op jit(solution)/shard_map/ppermute | solution.py:388
  67.9 14.5 %all_to_all.41.gathered.refs_5_ = f32[16,72,128]{2,1,0:T(8,128)S(1)} all-to-all(f32[16,72,128]{2,1,0:T(8,128)S(1)} %shard_map.124), channel_id=1, replica_groups=mesh['row'=16,'col'=8] {'row'}, dimensions={0} | all-to-all | bytes 1179648 | tf_op jit(solution)/shard_map/all_to_all | solution.py:425
  86.9 2.3 collective-permute-start.13
  90.5 5.0 %collective-permute-done.12 = f32[4,16,256]{2,1,0:T(8,128)S(1)} collective-permute-done((f32[4,16,256]{2,1,0:T(8,128)S(1)}, f32[4,16,256]{2,1,0:T(8,128)S(1)}, u32[]{:S(2)}, u32[]{:S(2)}) %collective-permute-start.12) | collective-permute-done | bytes 65568 | tf_op jit(solution)/shard_map/ppermute | solution.py:388
  98.7 14.5 %all_to_all.42.gathered.refs_5_ = f32[16,72,128]{2,1,0:T(8,128)S(1)} all-to-all(f32[16,72,128]{2,1,0:T(8,128)S(1)} %shard_map.126), channel_id=1, replica_groups=mesh['row'=16,'col'=8] {'row'}, dimensions={0} | all-to-all | bytes 1179648 | tf_op jit(solution)/shard_map/all_to_all | solution.py:425
  117.8 2.3 collective-permute-start.18
  121.4 5.0 %collective-permute-done.17 = f32[4,16,256]{2,1,0:T(8,128)S(1)} collective-permute-done((f32[4,16,256]{2,1,0:T(8,128)S(1)}, f32[4,16,256]{2,1,0:T(8,128)S(1)}, u32[]{:S(2)}, u32[]{:S(2)}) %collective-permute-start.17) | collective-permute-done | bytes 65568 | tf_op jit(solution)/shard_map/ppermute | solution.py:388
  129.6 14.4 %all_to_all.43.gathered.refs_5_ = f32[16,72,128]{2,1,0:T(8,128)S(1)} all-to-all(f32[16,72,128]{2,1,0:T(8,128)S(1)} %shard_map.128), channel_id=1, replica_groups=mesh['row'=16,'col'=8] {'row'}, dimensions={0} | all-to-all | bytes 1179648 | tf_op jit(solution)/shard_map/all_to_all | solution.py:425
  148.6 2.3 collective-permute-start.23
  152.3 5.0 %collective-permute-done.22 = f32[4,16,256]{2,1,0:T(8,128)S(1)} collective-permute-done((f32[4,16,256]{2,1,0:T(8,128)S(1)}, f32[4,16,256]{2,1,0:T(8,128)S(1)}, u32[]{:S(2)}, u32[]{:S(2)}) %collective-permute-start.22) | collective-permute-done | bytes 65568 | tf_op jit(solution)/shard_map/ppermute | solution.py:388
  160.5 14.5 %all_to_all.44.gathered.refs_5_ = f32[16,72,128]{2,1,0:T(8,128)S(1)} all-to-all(f32[16,72,128]{2,1,0:T(8,128)S(1)} %shard_map.130), channel_id=1, replica_groups=mesh['row'=16,'col'=8] {'row'}, dimensions={0} | all-to-all | bytes 1179648 | tf_op jit(solution)/shard_map/all_to_all | solution.py:425
  179.5 2.3 collective-permute-start.28
  183.1 5.0 %collective-permute-done.27 = f32[4,16,256]{2,1,0:T(8,128)S(1)} collective-permute-done((f32[4,16,256]{2,1,0:T(8,128)S(1)}, f32[4,16,256]{2,1,0:T(8,128)S(1)}, u32[]{:S(2)}, u32[]{:S(2)}) %collective-permute-start.27) | collective-permute-done | bytes 65568 | tf_op jit(solution)/shard_map/ppermute | solution.py:388
  191.4 14.5 %all_to_all.45.gathered = f32[16,72,128]{2,1,0:T(8,128)S(1)} all-to-all(f32[16,72,128]{2,1,0:T(8,128)S(1)} %shard_map.132), channel_id=1, replica_groups=mesh['row'=16,'col'=8] {'row'}, dimensions={0} | all-to-all | bytes 1179648 | tf_op jit(solution)/shard_map/all_to_all | solution.py:425
  210.4 2.3 collective-permute-start.33
  214.0 5.0 %collective-permute-done.32 = f32[4,16,256]{2,1,0:T(8,128)S(1)} collective-permute-done((f32[4,16,256]{2,1,0:T(8,128)S(1)}, f32[4,16,256]{2,1,0:T(8,128)S(1)}, u32[]{:S(2)}, u32[]{:S(2)}) %collective-permute-start.32) | collective-permute-done | bytes 65568 | tf_op jit(solution)/shard_map/ppermute | solution.py:388
  221.6 3.5 %all-to-all-start.7 = ((f32[16,8,128]{2,1,0:T(8,128)}), f32[16,8,128]{2,1,0:T(8,128)S(1)}, u32[]{:S(2)}, u32[]{:S(2)}) async-start(f32[16,8,128]{2,1,0:T(8,128)} %shard_map.135), calls=%async_computation.7 | async-start | bytes 131072 | tf_op jit(solution)/shard_map/all_to_all | solution.py:444
  226.8 4.8 %all-to-all-done.7.gathered = f32[16,8,128]{2,1,0:T(8,128)S(1)} async-done(((f32[16,8,128]{2,1,0:T(8,128)}), f32[16,8,128]{2,1,0:T(8,128)S(1)}, u32[]{:S(2)}, u32[]{:S(2)}) %all-to-all-start.7) | async-done | bytes 65568 | tf_op jit(solution)/shard_map/all_to_all | solution.py:444
  (96 shorter events, 70.5 us)
Async XLA Ops:
  2.0 14.4 %all-to-all-start = ((bf16[16,16,256]{2,1,0:T(8,128)(2,1)}), bf16[16,16,256]{2,1,0:T(8,128)(2,1)S(1)}, u32[]{:S(2)}, u32[]{:S(2)}) async-start(bf16[16,16,256]{2,1,0:T(8,128)(2,1)} %broadcast_in_dim.29), calls=%async_computation | async-start | bytes 262144 | tf_op jit(solution)/shard_map/all_to_all | solution.py:398
  20.5 2.9 %collective-permute-start = (f32[136,128]{1,0:T(8,128)S(1)}, f32[136,128]{1,0:T(8,128)S(1)}, u32[]{:S(2)}, u32[]{:S(2)}) collective-permute-start(f32[136,128]{1,0:T(8,128)S(1)} %get-tuple-element.39), channel_id=1, source_target_pairs={{0,1},{1,0},{2,3},{3,2},{4,5},{5,4},{6,7},{7,6},{8,9},{9,8},{10,11... | collective-permute-start | bytes 208904 | tf_op jit(solution)/shard_map/ppermute | solution.py:385
  23.5 5.2 %collective-permute-start.3 = (f32[136,128]{1,0:T(8,128)S(1)}, f32[136,128]{1,0:T(8,128)S(1)}, u32[]{:S(2)}, u32[]{:S(2)}) collective-permute-start(f32[136,128]{1,0:T(8,128)S(1)} %add.92), channel_id=1, source_target_pairs={{0,6},{1,7},{2,0},{3,1},{4,2},{5,3},{6,4},{7,5},{8,14},{9,15},{10,... | collective-permute-start | bytes 208904 | tf_op jit(solution)/shard_map/ppermute | solution.py:388
  27.3 6.3 %collective-permute-start.2 = (f32[136,128]{1,0:T(8,128)S(1)}, f32[136,128]{1,0:T(8,128)S(1)}, u32[]{:S(2)}, u32[]{:S(2)}) collective-permute-start(f32[136,128]{1,0:T(8,128)S(1)} %add.92), channel_id=1, source_target_pairs={{0,2},{1,3},{2,4},{3,5},{4,6},{5,7},{6,0},{7,1},{8,10},{9,11},{10,... | collective-permute-start | bytes 208904 | tf_op jit(solution)/shard_map/ppermute | solution.py:388
  27.3 6.3 %collective-permute-start.1 = (f32[136,128]{1,0:T(8,128)S(1)}, f32[136,128]{1,0:T(8,128)S(1)}, u32[]{:S(2)}, u32[]{:S(2)}) collective-permute-start(f32[136,128]{1,0:T(8,128)S(1)} %add.92), channel_id=1, source_target_pairs={{0,4},{1,5},{2,6},{3,7},{4,0},{5,1},{6,2},{7,3},{8,12},{9,13},{10,... | collective-permute-start | bytes 208904 | tf_op jit(solution)/shard_map/ppermute | solution.py:388
  56.2 3.5 %collective-permute-start.8 = (f32[4,16,256]{2,1,0:T(8,128)S(1)}, f32[4,16,256]{2,1,0:T(8,128)S(1)}, u32[]{:S(2)}, u32[]{:S(2)}) collective-permute-start(f32[4,16,256]{2,1,0:T(8,128)S(1)} %add.96), channel_id=1, source_target_pairs={{0,6},{1,7},{2,0},{3,1},{4,2},{5,3},{6,4},{7,5},{8,14},{9,15},{10,... | collective-permute-start | bytes 196616 | tf_op jit(solution)/shard_map/ppermute | solution.py:388
  58.4 6.3 %collective-permute-start.7 = (f32[4,16,256]{2,1,0:T(8,128)S(1)}, f32[4,16,256]{2,1,0:T(8,128)S(1)}, u32[]{:S(2)}, u32[]{:S(2)}) collective-permute-start(f32[4,16,256]{2,1,0:T(8,128)S(1)} %add.96), channel_id=1, source_target_pairs={{0,2},{1,3},{2,4},{3,5},{4,6},{5,7},{6,0},{7,1},{8,10},{9,11},{10,... | collective-permute-start | bytes 196616 | tf_op jit(solution)/shard_map/ppermute | solution.py:388
  58.4 6.3 %collective-permute-start.6 = (f32[4,16,256]{2,1,0:T(8,128)S(1)}, f32[4,16,256]{2,1,0:T(8,128)S(1)}, u32[]{:S(2)}, u32[]{:S(2)}) collective-permute-start(f32[4,16,256]{2,1,0:T(8,128)S(1)} %add.96), channel_id=1, source_target_pairs={{0,4},{1,5},{2,6},{3,7},{4,0},{5,1},{6,2},{7,3},{8,12},{9,13},{10,... | collective-permute-start | bytes 196616 | tf_op jit(solution)/shard_map/ppermute | solution.py:388
  86.9 3.6 %collective-permute-start.13 = (f32[4,16,256]{2,1,0:T(8,128)S(1)}, f32[4,16,256]{2,1,0:T(8,128)S(1)}, u32[]{:S(2)}, u32[]{:S(2)}) collective-permute-start(f32[4,16,256]{2,1,0:T(8,128)S(1)} %add.100), channel_id=1, source_target_pairs={{0,6},{1,7},{2,0},{3,1},{4,2},{5,3},{6,4},{7,5},{8,14},{9,15},{10,... | collective-permute-start | bytes 196616 | tf_op jit(solution)/shard_map/ppermute | solution.py:388
  89.2 6.3 %collective-permute-start.12 = (f32[4,16,256]{2,1,0:T(8,128)S(1)}, f32[4,16,256]{2,1,0:T(8,128)S(1)}, u32[]{:S(2)}, u32[]{:S(2)}) collective-permute-start(f32[4,16,256]{2,1,0:T(8,128)S(1)} %add.100), channel_id=1, source_target_pairs={{0,2},{1,3},{2,4},{3,5},{4,6},{5,7},{6,0},{7,1},{8,10},{9,11},{10,... | collective-permute-start | bytes 196616 | tf_op jit(solution)/shard_map/ppermute | solution.py:388
  89.2 6.3 %collective-permute-start.11 = (f32[4,16,256]{2,1,0:T(8,128)S(1)}, f32[4,16,256]{2,1,0:T(8,128)S(1)}, u32[]{:S(2)}, u32[]{:S(2)}) collective-permute-start(f32[4,16,256]{2,1,0:T(8,128)S(1)} %add.100), channel_id=1, source_target_pairs={{0,4},{1,5},{2,6},{3,7},{4,0},{5,1},{6,2},{7,3},{8,12},{9,13},{10,... | collective-permute-start | bytes 196616 | tf_op jit(solution)/shard_map/ppermute | solution.py:388
  117.8 3.6 %collective-permute-start.18 = (f32[4,16,256]{2,1,0:T(8,128)S(1)}, f32[4,16,256]{2,1,0:T(8,128)S(1)}, u32[]{:S(2)}, u32[]{:S(2)}) collective-permute-start(f32[4,16,256]{2,1,0:T(8,128)S(1)} %add.104), channel_id=1, source_target_pairs={{0,6},{1,7},{2,0},{3,1},{4,2},{5,3},{6,4},{7,5},{8,14},{9,15},{10,... | collective-permute-start | bytes 196616 | tf_op jit(solution)/shard_map/ppermute | solution.py:388
  120.1 6.3 %collective-permute-start.17 = (f32[4,16,256]{2,1,0:T(8,128)S(1)}, f32[4,16,256]{2,1,0:T(8,128)S(1)}, u32[]{:S(2)}, u32[]{:S(2)}) collective-permute-start(f32[4,16,256]{2,1,0:T(8,128)S(1)} %add.104), channel_id=1, source_target_pairs={{0,2},{1,3},{2,4},{3,5},{4,6},{5,7},{6,0},{7,1},{8,10},{9,11},{10,... | collective-permute-start | bytes 196616 | tf_op jit(solution)/shard_map/ppermute | solution.py:388
  120.1 6.3 %collective-permute-start.16 = (f32[4,16,256]{2,1,0:T(8,128)S(1)}, f32[4,16,256]{2,1,0:T(8,128)S(1)}, u32[]{:S(2)}, u32[]{:S(2)}) collective-permute-start(f32[4,16,256]{2,1,0:T(8,128)S(1)} %add.104), channel_id=1, source_target_pairs={{0,4},{1,5},{2,6},{3,7},{4,0},{5,1},{6,2},{7,3},{8,12},{9,13},{10,... | collective-permute-start | bytes 196616 | tf_op jit(solution)/shard_map/ppermute | solution.py:388
  148.6 3.6 %collective-permute-start.23 = (f32[4,16,256]{2,1,0:T(8,128)S(1)}, f32[4,16,256]{2,1,0:T(8,128)S(1)}, u32[]{:S(2)}, u32[]{:S(2)}) collective-permute-start(f32[4,16,256]{2,1,0:T(8,128)S(1)} %add.108), channel_id=1, source_target_pairs={{0,6},{1,7},{2,0},{3,1},{4,2},{5,3},{6,4},{7,5},{8,14},{9,15},{10,... | collective-permute-start | bytes 196616 | tf_op jit(solution)/shard_map/ppermute | solution.py:388
  150.9 6.3 %collective-permute-start.22 = (f32[4,16,256]{2,1,0:T(8,128)S(1)}, f32[4,16,256]{2,1,0:T(8,128)S(1)}, u32[]{:S(2)}, u32[]{:S(2)}) collective-permute-start(f32[4,16,256]{2,1,0:T(8,128)S(1)} %add.108), channel_id=1, source_target_pairs={{0,2},{1,3},{2,4},{3,5},{4,6},{5,7},{6,0},{7,1},{8,10},{9,11},{10,... | collective-permute-start | bytes 196616 | tf_op jit(solution)/shard_map/ppermute | solution.py:388
  150.9 6.3 %collective-permute-start.21 = (f32[4,16,256]{2,1,0:T(8,128)S(1)}, f32[4,16,256]{2,1,0:T(8,128)S(1)}, u32[]{:S(2)}, u32[]{:S(2)}) collective-permute-start(f32[4,16,256]{2,1,0:T(8,128)S(1)} %add.108), channel_id=1, source_target_pairs={{0,4},{1,5},{2,6},{3,7},{4,0},{5,1},{6,2},{7,3},{8,12},{9,13},{10,... | collective-permute-start | bytes 196616 | tf_op jit(solution)/shard_map/ppermute | solution.py:388
  179.5 3.6 %collective-permute-start.28 = (f32[4,16,256]{2,1,0:T(8,128)S(1)}, f32[4,16,256]{2,1,0:T(8,128)S(1)}, u32[]{:S(2)}, u32[]{:S(2)}) collective-permute-start(f32[4,16,256]{2,1,0:T(8,128)S(1)} %add.112), channel_id=1, source_target_pairs={{0,6},{1,7},{2,0},{3,1},{4,2},{5,3},{6,4},{7,5},{8,14},{9,15},{10,... | collective-permute-start | bytes 196616 | tf_op jit(solution)/shard_map/ppermute | solution.py:388
  181.8 6.3 %collective-permute-start.27 = (f32[4,16,256]{2,1,0:T(8,128)S(1)}, f32[4,16,256]{2,1,0:T(8,128)S(1)}, u32[]{:S(2)}, u32[]{:S(2)}) collective-permute-start(f32[4,16,256]{2,1,0:T(8,128)S(1)} %add.112), channel_id=1, source_target_pairs={{0,2},{1,3},{2,4},{3,5},{4,6},{5,7},{6,0},{7,1},{8,10},{9,11},{10,... | collective-permute-start | bytes 196616 | tf_op jit(solution)/shard_map/ppermute | solution.py:388
  181.8 6.3 %collective-permute-start.26 = (f32[4,16,256]{2,1,0:T(8,128)S(1)}, f32[4,16,256]{2,1,0:T(8,128)S(1)}, u32[]{:S(2)}, u32[]{:S(2)}) collective-permute-start(f32[4,16,256]{2,1,0:T(8,128)S(1)} %add.112), channel_id=1, source_target_pairs={{0,4},{1,5},{2,6},{3,7},{4,0},{5,1},{6,2},{7,3},{8,12},{9,13},{10,... | collective-permute-start | bytes 196616 | tf_op jit(solution)/shard_map/ppermute | solution.py:388
  210.4 3.6 %collective-permute-start.33 = (f32[4,16,256]{2,1,0:T(8,128)S(1)}, f32[4,16,256]{2,1,0:T(8,128)S(1)}, u32[]{:S(2)}, u32[]{:S(2)}) collective-permute-start(f32[4,16,256]{2,1,0:T(8,128)S(1)} %add.116), channel_id=1, source_target_pairs={{0,6},{1,7},{2,0},{3,1},{4,2},{5,3},{6,4},{7,5},{8,14},{9,15},{10,... | collective-permute-start | bytes 196616 | tf_op jit(solution)/shard_map/ppermute | solution.py:388
  212.7 6.3 %collective-permute-start.32 = (f32[4,16,256]{2,1,0:T(8,128)S(1)}, f32[4,16,256]{2,1,0:T(8,128)S(1)}, u32[]{:S(2)}, u32[]{:S(2)}) collective-permute-start(f32[4,16,256]{2,1,0:T(8,128)S(1)} %add.116), channel_id=1, source_target_pairs={{0,2},{1,3},{2,4},{3,5},{4,6},{5,7},{6,0},{7,1},{8,10},{9,11},{10,... | collective-permute-start | bytes 196616 | tf_op jit(solution)/shard_map/ppermute | solution.py:388
  212.7 6.3 %collective-permute-start.31 = (f32[4,16,256]{2,1,0:T(8,128)S(1)}, f32[4,16,256]{2,1,0:T(8,128)S(1)}, u32[]{:S(2)}, u32[]{:S(2)}) collective-permute-start(f32[4,16,256]{2,1,0:T(8,128)S(1)} %add.116), channel_id=1, source_target_pairs={{0,4},{1,5},{2,6},{3,7},{4,0},{5,1},{6,2},{7,3},{8,12},{9,13},{10,... | collective-permute-start | bytes 196616 | tf_op jit(solution)/shard_map/ppermute | solution.py:388
  221.6 9.9 %all-to-all-start.7 = ((f32[16,8,128]{2,1,0:T(8,128)}), f32[16,8,128]{2,1,0:T(8,128)S(1)}, u32[]{:S(2)}, u32[]{:S(2)}) async-start(f32[16,8,128]{2,1,0:T(8,128)} %shard_map.135), calls=%async_computation.7 | async-start | bytes 131072 | tf_op jit(solution)/shard_map/all_to_all | solution.py:444
  (15 other events, 78.8 us)

commit v3 on v2

--- a/solution.py
+++ b/solution.py
@@ -15,12 +15,18 @@
 DEGREE = 2 * ITERS
 FLOOR = 0.1
 LANES = 128
-CHUNKS = 8
+CHUNKS = 4
 F32 = jnp.float32
 BF16 = jnp.bfloat16
 
-PLACE_Z, PLACE_ROW, SLOTS = 0, 1, 8
+PLACE_Z, SLOTS = 0, 8
 D_FROM, D_TO, DIRECT_FROM, DIRECT_TO, BACK_FROM, BACK_TO = range(6)
+CODE = jnp.int16
+TOP = 32767.0
+FINE = 16.0
+DOTS = 16
+LANE_OWN, LANE_BACK = 14, 15
+DIGIT, DIGIT_LOW = 16384.0, 32768.0
 ALPHA, BETA, GAMMA, TOTAL, CENTRE, NEXT, GRAM = 0, 1, 2, 3, 4, 5, 8
 
 VM = pl.BlockSpec(memory_space=pltpu.VMEM)
@@ -91,12 +97,67 @@
     return out
 
 
+def fine_log(block):
+    peak = jnp.max(jnp.abs(block), axis=-1, keepdims=True)
+    return jnp.ceil(FINE * jnp.log2(jnp.maximum(peak, 1e-30)) + 0.02)
+
+
+def unit_of(fine):
+    return jnp.exp2(fine * (1.0 / FINE)) * (1.0 / TOP)
+
+
+def code_of(value):
+    return jnp.clip(jnp.round(value), -TOP, TOP).astype(jnp.int32).astype(CODE)
+
+
+def value_of(code):
+    return code.astype(jnp.int32).astype(F32)
+
+
+def encode(parts):
+    shape = (NV, LANES)
+    numbers = lanes_of(dict(enumerate(parts)), shape)
+    power = jnp.ceil(jnp.log2(jnp.maximum(jnp.abs(numbers), 1e-30)))
+    digits = numbers * jnp.exp2(-power) * DIGIT
+    first = jnp.round(digits)
+    second = jnp.round((digits - first) * DIGIT_LOW)
+    used = lax.broadcasted_iota(jnp.int32, shape, 1) < DOTS
+    power, first, second = (jnp.where(used, a, 0.0) for a in (power, first, second))
+    return power + pltpu.roll(first, DOTS, 1) + pltpu.roll(second, 2 * DOTS, 1)
+
+
+def decode(tile):
+    first, second = pltpu.roll(tile, LANES - DOTS, 1), pltpu.roll(tile, LANES - 2 * DOTS, 1)
+    return jnp.exp2(tile) * ((first + second * (1.0 / DIGIT_LOW)) * (1.0 / DIGIT))
+
+
+def own_of(table, z_mine, z):
+    if len(z_mine.shape) == 3:
+        return z_mine[table[PLACE_Z]]
+    own = z[0][0]
+    for i in range(1, z[0].shape[0]):
+        own = jnp.where(table[PLACE_Z] == i, z[0][i], own)
+    return own
+
+
 def load_slab(mine, other):
     if len(mine.shape) == 3:
         return mine[...], other[...]
     parts = 2
     half = mine.shape[0] // (parts * NV)
     return tuple(jnp.stack([wide_of(ref, b * parts * NV, parts) for b in range(half)]) for ref in (mine, other))
+
+
+def load_kernel(source, target, sems):
+    step = source.shape[0] // CHUNKS
+    copies = [
+        pltpu.make_async_copy(source.at[pl.ds(c * step, step)], target.at[pl.ds(c * step, step)], sems.at[c])
+        for c in range(CHUNKS)
+    ]
+    for copy in copies:
+        copy.start()
+    for copy in copies:
+        copy.wait()
 
 
 def dipole_kernel(table, gathered, energies_hbm, tiles_hbm, p_mine, p_other, xs, acc, energies, tiles, sems):
@@ -134,8 +195,8 @@
 
 
 def back_kernel(table, z_mine, z_other, *refs):
-    tiles, out, ys = refs[-3:]
-    qs = [(refs[i], refs[i + 1]) for i in range(0, len(refs) - 3, 2)]
+    tiles, out, ys, acc = refs[-4:]
+    qs = [(refs[i], refs[i + 1]) for i in range(0, len(refs) - 4, 2)]
     z = load_slab(z_mine, z_other)
     half = z[0].shape[0]
     slots = tiles.shape[0]
@@ -151,26 +212,25 @@
     else:
         centre = z_mine[-8:, 0:1]
         dots = [slab_dot(z, z), jnp.concatenate([centre, centre], axis=0)]
-    dots = pack(dots)
-    if len(z_mine.shape) == 3:
-        own = z_mine[table[PLACE_Z]]
-    else:
-        own = z[0][0]
-        for i in range(1, half):
-            own = jnp.where(table[PLACE_Z] == i, z[0][i], own)
+    own = own_of(table, z_mine, z)
+    acc[...] = jnp.zeros(acc.shape, F32)
+    for t in range(slots):
+        y = ys[entry(table, BACK_FROM, t, slots)]
+        res = jnp.dot(y, tiles[t], preferred_element_type=F32)
+        acc[entry(table, BACK_TO, t, slots)] += res[:NV] + res[NV:]
     parts = own.shape[1] // LANES
+    lane = lax.broadcasted_iota(jnp.int32, (NV, LANES), 1)
+    fine = fine_log(own)
+    own = code_of(own / unit_of(fine))
+    numbers = jnp.where(lane == LANE_OWN, fine, encode(dots))
     for p in range(out.shape[0]):
+        image = acc[p]
+        fine = fine_log(image)
+        image = code_of(image / unit_of(fine))
         for i in range(parts):
             out[p, i * NV : (i + 1) * NV] = own[:, i * LANES : (i + 1) * LANES]
-            out[p, (parts + i) * NV : (parts + i + 1) * NV] = jnp.zeros((NV, LANES), F32)
-        out[p, 2 * parts * NV :] = dots
-    for t in range(tiles.shape[0]):
-        y = ys[entry(table, BACK_FROM, t, slots)]
-        res = jnp.dot(y, tiles[t], preferred_element_type=F32)
-        res = res[:NV] + res[NV:]
-        peer = entry(table, BACK_TO, t, slots)
-        for i in range(parts):
-            out[peer, (parts + i) * NV : (parts + i + 1) * NV] += res[:, i * LANES : (i + 1) * LANES]
+            out[p, (parts + i) * NV : (parts + i + 1) * NV] = image[:, i * LANES : (i + 1) * LANES]
+        out[p, 2 * parts * NV :] = code_of(jnp.where(lane == LANE_BACK, fine, numbers))
 
 
 def direct_kernel(states_n, step, table, gathered, tiles, energies, z_mine, z_other, *refs):
@@ -180,25 +240,28 @@
     half = p_mine.shape[0]
     slots = tiles.shape[0]
     parts = acc.shape[2] // LANES
+    back = dots = None
     for i in range(groups):
-        split_into(xs, i, wide_of(gathered[i], 0, parts))
+        tile = value_of(gathered[i, 2 * parts * NV :])
+        unit = unit_of(tile)
+        split_into(xs, i, value_of(wide_of(gathered.at[i], 0, parts)) * unit[:, LANE_OWN : LANE_OWN + 1])
+        image = value_of(wide_of(gathered.at[i], parts * NV, parts)) * unit[:, LANE_BACK : LANE_BACK + 1]
+        numbers = decode(tile)
+        back = image if i == 0 else back + image
+        dots = numbers if i == 0 else dots + numbers
     xs[groups] = jnp.zeros(xs.shape[1:], BF16)
     acc[...] = jnp.zeros(acc.shape, F32)
     for t in range(tiles.shape[0]):
         x = xs[entry(table, DIRECT_FROM, t, slots)]
         res = lax.dot_general(x, tiles[t], (((1,), (1,)), ((), ())), preferred_element_type=F32)
         acc[entry(table, DIRECT_TO, t, slots)] += res[:NV] + res[NV:]
-    rest = gathered[0, parts * NV :]
-    for i in range(1, groups):
-        rest = rest + gathered[i, parts * NV :]
-    back = wide_of(rest, 0, parts)
-    dots = rest[parts * NV :]
-    norm = unpack(dots, 0)
+    column = lambda i: dots[:, i : i + 1]
+    norm = column(0)
     z = load_slab(z_mine, z_other)
-    own = wide_of(gathered[table[PLACE_ROW]], 0, parts)
+    own = own_of(table, z_mine, z)
     lanes = {}
     if step == 0:
-        centre = unpack(dots, 1) * (1.0 / states_n)
+        centre = column(1) * (1.0 / states_n)
         beta = jnp.sqrt(norm + 1e-30)
         scale = 1.0 / beta
         qn = [z[0] * scale, z[1] * scale]
@@ -207,21 +270,21 @@
         state = extra[0][...]
         q = (extra[1][...], extra[2][...])
         centre = state[:, CENTRE : CENTRE + 1]
-        size = unpack(dots, 3 + step)
-        alpha = unpack(dots, 1) / size
+        size = column(3 + step)
+        alpha = column(1) / size
         square = norm - alpha * alpha * size
         qn = [z[0] - alpha * q[0], z[1] - alpha * q[1]]
         local = (energies[...] - centre) * own + back - alpha * own
-        lanes.update({ALPHA: alpha, TOTAL: unpack(dots, 3)})
-        lanes.update({GRAM + i: unpack(dots, 4 + i) for i in range(step)})
+        lanes.update({ALPHA: alpha, TOTAL: column(3)})
+        lanes.update({GRAM + i: column(4 + i) for i in range(step)})
         if step > 1:
             old = (extra[3][...], extra[4][...])
             z_old = extra[5]
             size_old = state[:, GRAM + step - 2 : GRAM + step - 1]
-            gamma = unpack(dots, 2) / size_old
+            gamma = column(2) / size_old
             square = square - gamma * gamma * size_old
             qn = [a - gamma * b for a, b in zip(qn, old)]
-            local = local - gamma * wide_of(z_old[table[PLACE_ROW]], 0, parts)
+            local = local - gamma * z_old[table[PLACE_Z]]
             lanes[GAMMA] = gamma
         beta_square = jnp.maximum(square, FLOOR * FLOOR * norm) + 1e-30
         beta = jnp.sqrt(beta_square)
@@ -379,7 +442,7 @@
     ).astype(jnp.int32)
 
     pair = [(i, i ^ 1) for i in range(cols_n)]
-    ring = lambda d: [(2 * z + k, 2 * ((z + d) % half) + k) for z in range(half) for k in range(2)]
+    ring = lambda d: [(2 * z + k, 2 * ((z + (d if k else -d)) % half) + k) for z in range(half) for k in range(2)]
 
     def group_sum(p_mine, p_other):
         q = p_mine + lax.ppermute(p_other, "col", pair)
@@ -410,31 +473,41 @@
         ],
         compiler_params=pltpu.CompilerParams(vmem_limit_bytes=24 << 20),
     )(table, gathered, *(pltpu.with_memory_space_constraint(a, pltpu.HBM) for a in (diagonal, dipole_tiles)))
+    p_mine, h_tiles = lax.optimization_barrier((p_mine, pltpu.with_memory_space_constraint(h_tiles, pltpu.HBM)))
+    h_tiles = pl.pallas_call(
+        load_kernel,
+        out_shape=jax.ShapeDtypeStruct(h_tiles.shape, h_tiles.dtype),
+        in_specs=[HBM],
+        out_specs=VM,
+        scratch_shapes=[pltpu.SemaphoreType.DMA((CHUNKS,))],
+        compiler_params=pltpu.CompilerParams(vmem_limit_bytes=24 << 20),
+    )(h_tiles)
     z = group_sum(p_mine, p_other)
 
-    states, basis, received = [], [], []
+    states, basis, vectors = [], [], []
     for step in range(DEGREE):
         pairs = [array for q in basis for array in q]
         payload = call(
             back_kernel,
-            jax.ShapeDtypeStruct((rows_n, 2 * NV * width // LANES + 8, LANES), F32),
+            jax.ShapeDtypeStruct((rows_n, 2 * NV * width // LANES + NV, LANES), CODE),
             1,
             3 + len(pairs),
-            [pltpu.VMEM((cols_n + 1, 2 * NV, width), BF16)],
+            [pltpu.VMEM((cols_n + 1, 2 * NV, width), BF16), pltpu.VMEM((rows_n, NV, width), F32)],
         )(table, *z, *pairs, h_tiles)
-        received.append(lax.all_to_all(payload, "row", 0, 0, tiled=True))
+        vectors.append(z[0])
+        gathered = lax.all_to_all(payload, "row", 0, 0, tiled=True)
         extra = []
         if step > 0:
             extra = [states[-1], *basis[-1]]
         if step > 1:
-            extra += [*basis[-2], received[-2]]
+            extra += [*basis[-2], vectors[-2]]
         p_mine, p_other, qn_mine, qn_other, state = call(
             functools.partial(direct_kernel, float(rows_n * cols_n * width), step),
             (block, block, block, block, small),
             1,
             5 + len(extra),
             [pltpu.VMEM((rows_n + 1, 2 * NV, width), BF16), pltpu.VMEM((cols_n, NV, width), F32)],
-        )(table, received[-1], h_tiles, diagonal, *z, *extra)
+        )(table, gathered, h_tiles, diagonal, *z, *extra)
         states.append(state)
         basis.append((qn_mine, qn_other))
         z = group_sum(p_mine, p_other)

time: 233 us -> 218 us (0.936)
  blocking collectives: 86.9 us -> 67.1 us
  starting transfers between devices: 56.2 us -> 62.8 us
  waiting for transfers between devices: 55.6 us -> 50.4 us
  Pallas kernels: 27.3 us -> 30.5 us
    all_to_all x6, blocking collectives: 86.9 us -> 67.1 us  [body(): gathered = lax.all_to_all(payload, 'row', 0, 0, tiled=True)]
    ppermute x7, starting transfers between devices: 6.29 us -> 16 us  [group_sum(): return (mine, lax.ppermute(mine, 'col', pair))]
    ppermute x21, starting transfers between devices: 26.4 us -> 20.5 us  [group_sum(): moved.append(lax.ppermute(q, 'col', ring(d)))]
    ppermute x21, waiting for transfers between devices: 35.4 us -> 31.1 us  [group_sum(): moved.append(lax.ppermute(q, 'col', ring(d)))]
    ppermute x7, starting transfers between devices: 12.5 us -> 15.2 us  [group_sum(): q = p_mine + lax.ppermute(p_other, 'col', pair)]
  transfers between devices with their start and end apart: 37 -> 37, of which waited for: 30 -> 29; matrix products, arithmetic and copies ran while one was open for 1% -> 1% of each run, Pallas kernels for 1% -> 2%
where the time goes in v3:
time: 218 us; the launch traced here: 217 us
  blocking collectives  67.1 us (31%)
  starting transfers between devices  62.8 us (29%)
  waiting for transfers between devices  50.4 us (23%)
  Pallas kernels  30.5 us (14%)
  other arithmetic  2.22 us (1%)
    all_to_all x6, blocking collectives, body(): gathered = lax.all_to_all(payload, 'row', 0, 0, tiled=True)  67.1 us
    ppermute x21, waiting for transfers between devices, group_sum(): moved.append(lax.ppermute(q, 'col', ring(d)))  31.1 us
    ppermute x21, starting transfers between devices, group_sum(): moved.append(lax.ppermute(q, 'col', ring(d)))  20.5 us
    ppermute x7, starting transfers between devices, group_sum(): return (mine, lax.ppermute(mine, 'col', pair))  16 us
    ppermute x7, starting transfers between devices, group_sum(): q = p_mine + lax.ppermute(p_other, 'col', pair)  15.2 us
    pallas_call x6, Pallas kernels, body(): call(functools.partial(direct_kernel, float(rows_n * cols_n * width), ste...  11.8 us
    pallas_call x6, Pallas kernels, body(): call(back_kernel, jax.ShapeDtypeStruct((rows_n, 2 * NV * width // LANES +...  9.61 us
    all_to_all x1, starting transfers between devices, body(): gathered = lax.all_to_all(spread, 'row', 0, 0, tiled=True)  7.57 us
  transfers between devices with their start and end apart: 37, of which 29 were waited for; matrix products, arithmetic and copies ran while one was open for 1% of the time, Pallas kernels for 2%

profile of v3, /device:TPU:1, one launch (start us, length us, event | category | flops | bytes accessed | tf_op | source)
XLA Modules:
  0.0 217.3 jit_solution(7242975012788549351)
XLA Ops:
  2.0 7.6 %all-to-all-start = ((bf16[16,16,256]{2,1,0:T(8,128)(2,1)}), bf16[16,16,256]{2,1,0:T(8,128)(2,1)S(1)}, u32[]{:S(2)}, u32[]{:S(2)}) async-start(bf16[16,16,256]{2,1,0:T(8,128)(2,1)} %broadcast_in_dim.29), calls=%async_computation | async-start | bytes 262144 | tf_op jit(solution)/shard_map/all_to_all | solution.py:461
  13.6 2.8 %all-to-all-done.gathered = bf16[16,16,256]{2,1,0:T(8,128)(2,1)S(1)} async-done(((bf16[16,16,256]{2,1,0:T(8,128)(2,1)}), bf16[16,16,256]{2,1,0:T(8,128)(2,1)S(1)}, u32[]{:S(2)}, u32[]{:S(2)}) %all-to-all-start) | async-done | bytes 131104 | tf_op jit(solution)/shard_map/all_to_all | solution.py:461
  16.4 3.5 %shard_map.121 = (f32[136,128]{1,0:T(8,128)S(1)}, f32[136,128]{1,0:T(8,128)S(1)}) custom-call(s32[200]{0:T(256)S(1)} %concatenate.3.table, bf16[16,16,256]{2,1,0:T(8,128)(2,1)S(1)} %all-to-all-done.gathered, f32[1,256]{1,0:T(1,128)} %bitcast.6, bf16[32,256,256]{2,1,0:T(8,128)(2,1)} %tiles_hbm.1), custom_call_target="tpu_custom_call" | custom-call | tf_op jit(solution)/shard_map/pallas_call | solution.py:462
  22.8 3.8 %collective-permute-start.3 = (f32[136,128]{1,0:T(8,128)S(1)}, f32[136,128]{1,0:T(8,128)S(1)}, u32[]{:S(2)}, u32[]{:S(2)}) collective-permute-start(f32[136,128]{1,0:T(8,128)S(1)} %add.92), channel_id=1, source_target_pairs={{0,2},{1,7},{2,4},{3,1},{4,6},{5,3},{6,0},{7,5},{8,10},{9,15},{10,... | collective-permute-start | bytes 208904 | tf_op jit(solution)/shard_map/ppermute | solution.py:451
  28.0 4.8 %collective-permute-done.2 = f32[136,128]{1,0:T(8,128)S(1)} collective-permute-done((f32[136,128]{1,0:T(8,128)S(1)}, f32[136,128]{1,0:T(8,128)S(1)}, u32[]{:S(2)}, u32[]{:S(2)}) %collective-permute-start.2) | collective-permute-done | bytes 69664 | tf_op jit(solution)/shard_map/ppermute | solution.py:451
  37.1 11.3 %all_to_all.40.gathered = s16[16,80,128]{2,1,0:T(8,128)(2,1)S(1)} all-to-all(s16[16,80,128]{2,1,0:T(8,128)(2,1)S(1)} %shard_map.123), channel_id=1, replica_groups=mesh['row'=16,'col'=8] {'row'}, dimensions={0} | all-to-all | bytes 655360 | tf_op jit(solution)/shard_map/all_to_all | solution.py:498
  57.0 3.7 %collective-permute-done.7 = f32[4,16,256]{2,1,0:T(8,128)S(1)} collective-permute-done((f32[4,16,256]{2,1,0:T(8,128)S(1)}, f32[4,16,256]{2,1,0:T(8,128)S(1)}, u32[]{:S(2)}, u32[]{:S(2)}) %collective-permute-start.7) | collective-permute-done | bytes 65568 | tf_op jit(solution)/shard_map/ppermute | solution.py:451
  65.4 11.2 %all_to_all.41.gathered = s16[16,80,128]{2,1,0:T(8,128)(2,1)S(1)} all-to-all(s16[16,80,128]{2,1,0:T(8,128)(2,1)S(1)} %shard_map.125), channel_id=1, replica_groups=mesh['row'=16,'col'=8] {'row'}, dimensions={0} | all-to-all | bytes 655360 | tf_op jit(solution)/shard_map/all_to_all | solution.py:498
  84.9 3.5 %collective-permute-done.12 = f32[4,16,256]{2,1,0:T(8,128)S(1)} collective-permute-done((f32[4,16,256]{2,1,0:T(8,128)S(1)}, f32[4,16,256]{2,1,0:T(8,128)S(1)}, u32[]{:S(2)}, u32[]{:S(2)}) %collective-permute-start.12) | collective-permute-done | bytes 65568 | tf_op jit(solution)/shard_map/ppermute | solution.py:451
  88.4 2.8 %collective-permute-start.14 = (f32[4,16,256]{2,1,0:T(8,128)S(1)}, f32[4,16,256]{2,1,0:T(8,128)S(1)}, u32[]{:S(2)}, u32[]{:S(2)}) collective-permute-start(f32[4,16,256]{2,1,0:T(8,128)S(1)} %add_add_fusion.5.z_mine.refs_5_), channel_id=1, source_target_pairs={{0,1},{1,0},{2,3},{3,2},{4,5},{5,4},{6,7},{7,6},{8,9},{9,8},{10,11... | collective-permute-start | bytes 196616 | tf_op jit(solution)/shard_map/ppermute | solution.py:453
  93.7 11.2 %all_to_all.42.gathered = s16[16,80,128]{2,1,0:T(8,128)(2,1)S(1)} all-to-all(s16[16,80,128]{2,1,0:T(8,128)(2,1)S(1)} %shard_map.127), channel_id=1, replica_groups=mesh['row'=16,'col'=8] {'row'}, dimensions={0} | all-to-all | bytes 655360 | tf_op jit(solution)/shard_map/all_to_all | solution.py:498
  113.4 3.6 %collective-permute-done.17 = f32[4,16,256]{2,1,0:T(8,128)S(1)} collective-permute-done((f32[4,16,256]{2,1,0:T(8,128)S(1)}, f32[4,16,256]{2,1,0:T(8,128)S(1)}, u32[]{:S(2)}, u32[]{:S(2)}) %collective-permute-start.17) | collective-permute-done | bytes 65568 | tf_op jit(solution)/shard_map/ppermute | solution.py:451
  117.0 2.7 %collective-permute-start.19 = (f32[4,16,256]{2,1,0:T(8,128)S(1)}, f32[4,16,256]{2,1,0:T(8,128)S(1)}, u32[]{:S(2)}, u32[]{:S(2)}) collective-permute-start(f32[4,16,256]{2,1,0:T(8,128)S(1)} %add_add_fusion.4.z_mine.refs_5_), channel_id=1, source_target_pairs={{0,1},{1,0},{2,3},{3,2},{4,5},{5,4},{6,7},{7,6},{8,9},{9,8},{10,11... | collective-permute-start | bytes 196616 | tf_op jit(solution)/shard_map/ppermute | solution.py:453
  122.2 11.2 %all_to_all.43.gathered = s16[16,80,128]{2,1,0:T(8,128)(2,1)S(1)} all-to-all(s16[16,80,128]{2,1,0:T(8,128)(2,1)S(1)} %shard_map.129), channel_id=1, replica_groups=mesh['row'=16,'col'=8] {'row'}, dimensions={0} | all-to-all | bytes 655360 | tf_op jit(solution)/shard_map/all_to_all | solution.py:498
  141.7 3.7 %collective-permute-done.22 = f32[4,16,256]{2,1,0:T(8,128)S(1)} collective-permute-done((f32[4,16,256]{2,1,0:T(8,128)S(1)}, f32[4,16,256]{2,1,0:T(8,128)S(1)}, u32[]{:S(2)}, u32[]{:S(2)}) %collective-permute-start.22) | collective-permute-done | bytes 65568 | tf_op jit(solution)/shard_map/ppermute | solution.py:451
  145.4 2.6 %collective-permute-start.24 = (f32[4,16,256]{2,1,0:T(8,128)S(1)}, f32[4,16,256]{2,1,0:T(8,128)S(1)}, u32[]{:S(2)}, u32[]{:S(2)}) collective-permute-start(f32[4,16,256]{2,1,0:T(8,128)S(1)} %add_add_fusion.3.z_mine.refs_5_), channel_id=1, source_target_pairs={{0,1},{1,0},{2,3},{3,2},{4,5},{5,4},{6,7},{7,6},{8,9},{9,8},{10,11... | collective-permute-start | bytes 196616 | tf_op jit(solution)/shard_map/ppermute | solution.py:453
  150.6 11.2 %all_to_all.44.gathered = s16[16,80,128]{2,1,0:T(8,128)(2,1)S(1)} all-to-all(s16[16,80,128]{2,1,0:T(8,128)(2,1)S(1)} %shard_map.131), channel_id=1, replica_groups=mesh['row'=16,'col'=8] {'row'}, dimensions={0} | all-to-all | bytes 655360 | tf_op jit(solution)/shard_map/all_to_all | solution.py:498
  170.0 3.7 %collective-permute-done.27 = f32[4,16,256]{2,1,0:T(8,128)S(1)} collective-permute-done((f32[4,16,256]{2,1,0:T(8,128)S(1)}, f32[4,16,256]{2,1,0:T(8,128)S(1)}, u32[]{:S(2)}, u32[]{:S(2)}) %collective-permute-start.27) | collective-permute-done | bytes 65568 | tf_op jit(solution)/shard_map/ppermute | solution.py:451
  173.8 2.6 %collective-permute-start.29 = (f32[4,16,256]{2,1,0:T(8,128)S(1)}, f32[4,16,256]{2,1,0:T(8,128)S(1)}, u32[]{:S(2)}, u32[]{:S(2)}) collective-permute-start(f32[4,16,256]{2,1,0:T(8,128)S(1)} %add_add_fusion.2.z_mine), channel_id=1, source_target_pairs={{0,1},{1,0},{2,3},{3,2},{4,5},{5,4},{6,7},{7,6},{8,9},{9,8},{10,11... | collective-permute-start | bytes 196616 | tf_op jit(solution)/shard_map/ppermute | solution.py:453
  178.9 11.2 %all_to_all.45.gathered = s16[16,80,128]{2,1,0:T(8,128)(2,1)S(1)} all-to-all(s16[16,80,128]{2,1,0:T(8,128)(2,1)S(1)} %shard_map.133), channel_id=1, replica_groups=mesh['row'=16,'col'=8] {'row'}, dimensions={0} | all-to-all | bytes 655360 | tf_op jit(solution)/shard_map/all_to_all | solution.py:498
  198.4 3.7 %collective-permute-done.32 = f32[4,16,256]{2,1,0:T(8,128)S(1)} collective-permute-done((f32[4,16,256]{2,1,0:T(8,128)S(1)}, f32[4,16,256]{2,1,0:T(8,128)S(1)}, u32[]{:S(2)}, u32[]{:S(2)}) %collective-permute-start.32) | collective-permute-done | bytes 65568 | tf_op jit(solution)/shard_map/ppermute | solution.py:451
  202.1 2.6 %collective-permute-start.34 = (f32[4,16,256]{2,1,0:T(8,128)S(1)}, f32[4,16,256]{2,1,0:T(8,128)S(1)}, u32[]{:S(2)}, u32[]{:S(2)}) collective-permute-start(f32[4,16,256]{2,1,0:T(8,128)S(1)} %add_add_fusion.1.refs_12_.refs_0_), channel_id=1, source_target_pairs={{0,1},{1,0},{2,3},{3,2},{4,5},{5,4},{6,7},{7,6},{8,9},{9,8},{10,11... | collective-permute-start | bytes 196616 | tf_op jit(solution)/shard_map/ppermute | solution.py:453
  206.4 3.5 %all-to-all-start.7 = ((f32[16,8,128]{2,1,0:T(8,128)}), f32[16,8,128]{2,1,0:T(8,128)S(1)}, u32[]{:S(2)}, u32[]{:S(2)}) async-start(f32[16,8,128]{2,1,0:T(8,128)} %shard_map.136), calls=%async_computation.7 | async-start | bytes 131072 | tf_op jit(solution)/shard_map/all_to_all | solution.py:517
  211.6 4.8 %all-to-all-done.7.gathered = f32[16,8,128]{2,1,0:T(8,128)S(1)} async-done(((f32[16,8,128]{2,1,0:T(8,128)}), f32[16,8,128]{2,1,0:T(8,128)S(1)}, u32[]{:S(2)}, u32[]{:S(2)}) %all-to-all-start.7) | async-done | bytes 65568 | tf_op jit(solution)/shard_map/all_to_all | solution.py:517
  (95 shorter events, 82.0 us)
Async XLA Ops:
  2.0 14.4 %all-to-all-start = ((bf16[16,16,256]{2,1,0:T(8,128)(2,1)}), bf16[16,16,256]{2,1,0:T(8,128)(2,1)S(1)}, u32[]{:S(2)}, u32[]{:S(2)}) async-start(bf16[16,16,256]{2,1,0:T(8,128)(2,1)} %broadcast_in_dim.29), calls=%async_computation | async-start | bytes 262144 | tf_op jit(solution)/shard_map/all_to_all | solution.py:461
  22.8 5.2 %collective-permute-start.3 = (f32[136,128]{1,0:T(8,128)S(1)}, f32[136,128]{1,0:T(8,128)S(1)}, u32[]{:S(2)}, u32[]{:S(2)}) collective-permute-start(f32[136,128]{1,0:T(8,128)S(1)} %add.92), channel_id=1, source_target_pairs={{0,2},{1,7},{2,4},{3,1},{4,6},{5,3},{6,0},{7,5},{8,10},{9,15},{10,... | collective-permute-start | bytes 208904 | tf_op jit(solution)/shard_map/ppermute | solution.py:451
  26.7 6.1 %collective-permute-start.2 = (f32[136,128]{1,0:T(8,128)S(1)}, f32[136,128]{1,0:T(8,128)S(1)}, u32[]{:S(2)}, u32[]{:S(2)}) collective-permute-start(f32[136,128]{1,0:T(8,128)S(1)} %add.92), channel_id=1, source_target_pairs={{0,6},{1,3},{2,0},{3,5},{4,2},{5,7},{6,4},{7,1},{8,14},{9,11},{10,... | collective-permute-start | bytes 208904 | tf_op jit(solution)/shard_map/ppermute | solution.py:451
  26.7 6.1 %collective-permute-start.1 = (f32[136,128]{1,0:T(8,128)S(1)}, f32[136,128]{1,0:T(8,128)S(1)}, u32[]{:S(2)}, u32[]{:S(2)}) collective-permute-start(f32[136,128]{1,0:T(8,128)S(1)} %add.92), channel_id=1, source_target_pairs={{0,4},{1,5},{2,6},{3,7},{4,0},{5,1},{6,2},{7,3},{8,12},{9,13},{10,... | collective-permute-start | bytes 208904 | tf_op jit(solution)/shard_map/ppermute | solution.py:451
  53.4 3.6 %collective-permute-start.8 = (f32[4,16,256]{2,1,0:T(8,128)S(1)}, f32[4,16,256]{2,1,0:T(8,128)S(1)}, u32[]{:S(2)}, u32[]{:S(2)}) collective-permute-start(f32[4,16,256]{2,1,0:T(8,128)S(1)} %add.96), channel_id=1, source_target_pairs={{0,2},{1,7},{2,4},{3,1},{4,6},{5,3},{6,0},{7,5},{8,10},{9,15},{10,... | collective-permute-start | bytes 196616 | tf_op jit(solution)/shard_map/ppermute | solution.py:451
  55.7 5.0 %collective-permute-start.7 = (f32[4,16,256]{2,1,0:T(8,128)S(1)}, f32[4,16,256]{2,1,0:T(8,128)S(1)}, u32[]{:S(2)}, u32[]{:S(2)}) collective-permute-start(f32[4,16,256]{2,1,0:T(8,128)S(1)} %add.96), channel_id=1, source_target_pairs={{0,6},{1,3},{2,0},{3,5},{4,2},{5,7},{6,4},{7,1},{8,14},{9,11},{10,... | collective-permute-start | bytes 196616 | tf_op jit(solution)/shard_map/ppermute | solution.py:451
  55.7 5.0 %collective-permute-start.6 = (f32[4,16,256]{2,1,0:T(8,128)S(1)}, f32[4,16,256]{2,1,0:T(8,128)S(1)}, u32[]{:S(2)}, u32[]{:S(2)}) collective-permute-start(f32[4,16,256]{2,1,0:T(8,128)S(1)} %add.96), channel_id=1, source_target_pairs={{0,4},{1,5},{2,6},{3,7},{4,0},{5,1},{6,2},{7,3},{8,12},{9,13},{10,... | collective-permute-start | bytes 196616 | tf_op jit(solution)/shard_map/ppermute | solution.py:451
  83.3 5.0 %collective-permute-start.12 = (f32[4,16,256]{2,1,0:T(8,128)S(1)}, f32[4,16,256]{2,1,0:T(8,128)S(1)}, u32[]{:S(2)}, u32[]{:S(2)}) collective-permute-start(f32[4,16,256]{2,1,0:T(8,128)S(1)} %add.100), channel_id=1, source_target_pairs={{0,6},{1,3},{2,0},{3,5},{4,2},{5,7},{6,4},{7,1},{8,14},{9,11},{10,... | collective-permute-start | bytes 196616 | tf_op jit(solution)/shard_map/ppermute | solution.py:451
  83.3 5.0 %collective-permute-start.11 = (f32[4,16,256]{2,1,0:T(8,128)S(1)}, f32[4,16,256]{2,1,0:T(8,128)S(1)}, u32[]{:S(2)}, u32[]{:S(2)}) collective-permute-start(f32[4,16,256]{2,1,0:T(8,128)S(1)} %add.100), channel_id=1, source_target_pairs={{0,4},{1,5},{2,6},{3,7},{4,0},{5,1},{6,2},{7,3},{8,12},{9,13},{10,... | collective-permute-start | bytes 196616 | tf_op jit(solution)/shard_map/ppermute | solution.py:451
  88.4 3.7 %collective-permute-start.14 = (f32[4,16,256]{2,1,0:T(8,128)S(1)}, f32[4,16,256]{2,1,0:T(8,128)S(1)}, u32[]{:S(2)}, u32[]{:S(2)}) collective-permute-start(f32[4,16,256]{2,1,0:T(8,128)S(1)} %add_add_fusion.5.z_mine.refs_5_), channel_id=1, source_target_pairs={{0,1},{1,0},{2,3},{3,2},{4,5},{5,4},{6,7},{7,6},{8,9},{9,8},{10,11... | collective-permute-start | bytes 196616 | tf_op jit(solution)/shard_map/ppermute | solution.py:453
  110.0 3.4 %collective-permute-start.18 = (f32[4,16,256]{2,1,0:T(8,128)S(1)}, f32[4,16,256]{2,1,0:T(8,128)S(1)}, u32[]{:S(2)}, u32[]{:S(2)}) collective-permute-start(f32[4,16,256]{2,1,0:T(8,128)S(1)} %add.104), channel_id=1, source_target_pairs={{0,2},{1,7},{2,4},{3,1},{4,6},{5,3},{6,0},{7,5},{8,10},{9,15},{10,... | collective-permute-start | bytes 196616 | tf_op jit(solution)/shard_map/ppermute | solution.py:451
  111.2 5.8 %collective-permute-start.17 = (f32[4,16,256]{2,1,0:T(8,128)S(1)}, f32[4,16,256]{2,1,0:T(8,128)S(1)}, u32[]{:S(2)}, u32[]{:S(2)}) collective-permute-start(f32[4,16,256]{2,1,0:T(8,128)S(1)} %add.104), channel_id=1, source_target_pairs={{0,6},{1,3},{2,0},{3,5},{4,2},{5,7},{6,4},{7,1},{8,14},{9,11},{10,... | collective-permute-start | bytes 196616 | tf_op jit(solution)/shard_map/ppermute | solution.py:451
  111.7 5.3 %collective-permute-start.16 = (f32[4,16,256]{2,1,0:T(8,128)S(1)}, f32[4,16,256]{2,1,0:T(8,128)S(1)}, u32[]{:S(2)}, u32[]{:S(2)}) collective-permute-start(f32[4,16,256]{2,1,0:T(8,128)S(1)} %add.104), channel_id=1, source_target_pairs={{0,4},{1,5},{2,6},{3,7},{4,0},{5,1},{6,2},{7,3},{8,12},{9,13},{10,... | collective-permute-start | bytes 196616 | tf_op jit(solution)/shard_map/ppermute | solution.py:451
  117.0 3.6 %collective-permute-start.19 = (f32[4,16,256]{2,1,0:T(8,128)S(1)}, f32[4,16,256]{2,1,0:T(8,128)S(1)}, u32[]{:S(2)}, u32[]{:S(2)}) collective-permute-start(f32[4,16,256]{2,1,0:T(8,128)S(1)} %add_add_fusion.4.z_mine.refs_5_), channel_id=1, source_target_pairs={{0,1},{1,0},{2,3},{3,2},{4,5},{5,4},{6,7},{7,6},{8,9},{9,8},{10,11... | collective-permute-start | bytes 196616 | tf_op jit(solution)/shard_map/ppermute | solution.py:453
  139.4 6.0 %collective-permute-start.22 = (f32[4,16,256]{2,1,0:T(8,128)S(1)}, f32[4,16,256]{2,1,0:T(8,128)S(1)}, u32[]{:S(2)}, u32[]{:S(2)}) collective-permute-start(f32[4,16,256]{2,1,0:T(8,128)S(1)} %add.108), channel_id=1, source_target_pairs={{0,6},{1,3},{2,0},{3,5},{4,2},{5,7},{6,4},{7,1},{8,14},{9,11},{10,... | collective-permute-start | bytes 196616 | tf_op jit(solution)/shard_map/ppermute | solution.py:451
  140.0 5.4 %collective-permute-start.21 = (f32[4,16,256]{2,1,0:T(8,128)S(1)}, f32[4,16,256]{2,1,0:T(8,128)S(1)}, u32[]{:S(2)}, u32[]{:S(2)}) collective-permute-start(f32[4,16,256]{2,1,0:T(8,128)S(1)} %add.108), channel_id=1, source_target_pairs={{0,4},{1,5},{2,6},{3,7},{4,0},{5,1},{6,2},{7,3},{8,12},{9,13},{10,... | collective-permute-start | bytes 196616 | tf_op jit(solution)/shard_map/ppermute | solution.py:451
  145.4 3.5 %collective-permute-start.24 = (f32[4,16,256]{2,1,0:T(8,128)S(1)}, f32[4,16,256]{2,1,0:T(8,128)S(1)}, u32[]{:S(2)}, u32[]{:S(2)}) collective-permute-start(f32[4,16,256]{2,1,0:T(8,128)S(1)} %add_add_fusion.3.z_mine.refs_5_), channel_id=1, source_target_pairs={{0,1},{1,0},{2,3},{3,2},{4,5},{5,4},{6,7},{7,6},{8,9},{9,8},{10,11... | collective-permute-start | bytes 196616 | tf_op jit(solution)/shard_map/ppermute | solution.py:453
  167.8 6.0 %collective-permute-start.27 = (f32[4,16,256]{2,1,0:T(8,128)S(1)}, f32[4,16,256]{2,1,0:T(8,128)S(1)}, u32[]{:S(2)}, u32[]{:S(2)}) collective-permute-start(f32[4,16,256]{2,1,0:T(8,128)S(1)} %add.112), channel_id=1, source_target_pairs={{0,6},{1,3},{2,0},{3,5},{4,2},{5,7},{6,4},{7,1},{8,14},{9,11},{10,... | collective-permute-start | bytes 196616 | tf_op jit(solution)/shard_map/ppermute | solution.py:451
  168.4 5.3 %collective-permute-start.26 = (f32[4,16,256]{2,1,0:T(8,128)S(1)}, f32[4,16,256]{2,1,0:T(8,128)S(1)}, u32[]{:S(2)}, u32[]{:S(2)}) collective-permute-start(f32[4,16,256]{2,1,0:T(8,128)S(1)} %add.112), channel_id=1, source_target_pairs={{0,4},{1,5},{2,6},{3,7},{4,0},{5,1},{6,2},{7,3},{8,12},{9,13},{10,... | collective-permute-start | bytes 196616 | tf_op jit(solution)/shard_map/ppermute | solution.py:451
  173.8 3.5 %collective-permute-start.29 = (f32[4,16,256]{2,1,0:T(8,128)S(1)}, f32[4,16,256]{2,1,0:T(8,128)S(1)}, u32[]{:S(2)}, u32[]{:S(2)}) collective-permute-start(f32[4,16,256]{2,1,0:T(8,128)S(1)} %add_add_fusion.2.z_mine), channel_id=1, source_target_pairs={{0,1},{1,0},{2,3},{3,2},{4,5},{5,4},{6,7},{7,6},{8,9},{9,8},{10,11... | collective-permute-start | bytes 196616 | tf_op jit(solution)/shard_map/ppermute | solution.py:453
  196.1 6.0 %collective-permute-start.32 = (f32[4,16,256]{2,1,0:T(8,128)S(1)}, f32[4,16,256]{2,1,0:T(8,128)S(1)}, u32[]{:S(2)}, u32[]{:S(2)}) collective-permute-start(f32[4,16,256]{2,1,0:T(8,128)S(1)} %add.116), channel_id=1, source_target_pairs={{0,6},{1,3},{2,0},{3,5},{4,2},{5,7},{6,4},{7,1},{8,14},{9,11},{10,... | collective-permute-start | bytes 196616 | tf_op jit(solution)/shard_map/ppermute | solution.py:451
  196.7 5.3 %collective-permute-start.31 = (f32[4,16,256]{2,1,0:T(8,128)S(1)}, f32[4,16,256]{2,1,0:T(8,128)S(1)}, u32[]{:S(2)}, u32[]{:S(2)}) collective-permute-start(f32[4,16,256]{2,1,0:T(8,128)S(1)} %add.116), channel_id=1, source_target_pairs={{0,4},{1,5},{2,6},{3,7},{4,0},{5,1},{6,2},{7,3},{8,12},{9,13},{10,... | collective-permute-start | bytes 196616 | tf_op jit(solution)/shard_map/ppermute | solution.py:451
  202.1 3.5 %collective-permute-start.34 = (f32[4,16,256]{2,1,0:T(8,128)S(1)}, f32[4,16,256]{2,1,0:T(8,128)S(1)}, u32[]{:S(2)}, u32[]{:S(2)}) collective-permute-start(f32[4,16,256]{2,1,0:T(8,128)S(1)} %add_add_fusion.1.refs_12_.refs_0_), channel_id=1, source_target_pairs={{0,1},{1,0},{2,3},{3,2},{4,5},{5,4},{6,7},{7,6},{8,9},{9,8},{10,11... | collective-permute-start | bytes 196616 | tf_op jit(solution)/shard_map/ppermute | solution.py:453
  206.4 9.9 %all-to-all-start.7 = ((f32[16,8,128]{2,1,0:T(8,128)}), f32[16,8,128]{2,1,0:T(8,128)S(1)}, u32[]{:S(2)}, u32[]{:S(2)}) async-start(f32[16,8,128]{2,1,0:T(8,128)} %shard_map.136), calls=%async_computation.7 | async-start | bytes 131072 | tf_op jit(solution)/shard_map/all_to_all | solution.py:517
  (14 other events, 52.9 us)

commit v4 on v3

--- a/solution.py
+++ b/solution.py
@@ -114,14 +114,19 @@
     return code.astype(jnp.int32).astype(F32)
 
 
+def put(tile, i, value):
+    lane = lax.broadcasted_iota(jnp.int32, tile.shape, 1)
+    tile = jnp.where(lane == i, value[:8], tile)
+    return jnp.where(lane == i + LANES // 2, value[8:], tile)
+
+
 def encode(parts):
-    shape = (NV, LANES)
-    numbers = lanes_of(dict(enumerate(parts)), shape)
+    numbers = pack(parts)
     power = jnp.ceil(jnp.log2(jnp.maximum(jnp.abs(numbers), 1e-30)))
     digits = numbers * jnp.exp2(-power) * DIGIT
     first = jnp.round(digits)
     second = jnp.round((digits - first) * DIGIT_LOW)
-    used = lax.broadcasted_iota(jnp.int32, shape, 1) < DOTS
+    used = (lax.broadcasted_iota(jnp.int32, numbers.shape, 1) & (LANES // 2 - 1)) < DOTS
     power, first, second = (jnp.where(used, a, 0.0) for a in (power, first, second))
     return power + pltpu.roll(first, DOTS, 1) + pltpu.roll(second, 2 * DOTS, 1)
 
@@ -219,10 +224,9 @@
         res = jnp.dot(y, tiles[t], preferred_element_type=F32)
         acc[entry(table, BACK_TO, t, slots)] += res[:NV] + res[NV:]
     parts = own.shape[1] // LANES
-    lane = lax.broadcasted_iota(jnp.int32, (NV, LANES), 1)
     fine = fine_log(own)
     own = code_of(own / unit_of(fine))
-    numbers = jnp.where(lane == LANE_OWN, fine, encode(dots))
+    numbers = put(encode(dots), LANE_OWN, fine)
     for p in range(out.shape[0]):
         image = acc[p]
         fine = fine_log(image)
@@ -230,7 +234,7 @@
         for i in range(parts):
             out[p, i * NV : (i + 1) * NV] = own[:, i * LANES : (i + 1) * LANES]
             out[p, (parts + i) * NV : (parts + i + 1) * NV] = image[:, i * LANES : (i + 1) * LANES]
-        out[p, 2 * parts * NV :] = code_of(jnp.where(lane == LANE_BACK, fine, numbers))
+        out[p, 2 * parts * NV :] = code_of(put(numbers, LANE_BACK, fine))
 
 
 def direct_kernel(states_n, step, table, gathered, tiles, energies, z_mine, z_other, *refs):
@@ -244,8 +248,8 @@
     for i in range(groups):
         tile = value_of(gathered[i, 2 * parts * NV :])
         unit = unit_of(tile)
-        split_into(xs, i, value_of(wide_of(gathered.at[i], 0, parts)) * unit[:, LANE_OWN : LANE_OWN + 1])
-        image = value_of(wide_of(gathered.at[i], parts * NV, parts)) * unit[:, LANE_BACK : LANE_BACK + 1]
+        split_into(xs, i, value_of(wide_of(gathered.at[i], 0, parts)) * unpack(unit, LANE_OWN))
+        image = value_of(wide_of(gathered.at[i], parts * NV, parts)) * unpack(unit, LANE_BACK)
         numbers = decode(tile)
         back = image if i == 0 else back + image
         dots = numbers if i == 0 else dots + numbers
@@ -255,7 +259,7 @@
         x = xs[entry(table, DIRECT_FROM, t, slots)]
         res = lax.dot_general(x, tiles[t], (((1,), (1,)), ((), ())), preferred_element_type=F32)
         acc[entry(table, DIRECT_TO, t, slots)] += res[:NV] + res[NV:]
-    column = lambda i: dots[:, i : i + 1]
+    column = functools.partial(unpack, dots)
     norm = column(0)
     z = load_slab(z_mine, z_other)
     own = own_of(table, z_mine, z)
@@ -489,7 +493,7 @@
         pairs = [array for q in basis for array in q]
         payload = call(
             back_kernel,
-            jax.ShapeDtypeStruct((rows_n, 2 * NV * width // LANES + NV, LANES), CODE),
+            jax.ShapeDtypeStruct((rows_n, 2 * NV * width // LANES + 8, LANES), CODE),
             1,
             3 + len(pairs),
             [pltpu.VMEM((cols_n + 1, 2 * NV, width), BF16), pltpu.VMEM((rows_n, NV, width), F32)],

time: 218 us -> 216 us (level)
  no operation moved by 1% of the time
where the time goes in v4:
time: 216 us; the launch traced here: 215 us
  blocking collectives  65.7 us (30%)
  starting transfers between devices  62.1 us (29%)
  waiting for transfers between devices  50.4 us (23%)
  Pallas kernels  30.8 us (14%)
  other arithmetic  2.22 us (1%)
  between operations  2.16 us (1%)
    all_to_all x6, blocking collectives, body(): gathered = lax.all_to_all(payload, 'row', 0, 0, tiled=True)  65.7 us
    ppermute x21, waiting for transfers between devices, group_sum(): moved.append(lax.ppermute(q, 'col', ring(d)))  31.1 us
    ppermute x21, starting transfers between devices, group_sum(): moved.append(lax.ppermute(q, 'col', ring(d)))  20.5 us
    ppermute x7, starting transfers between devices, group_sum(): return (mine, lax.ppermute(mine, 'col', pair))  16 us
    ppermute x7, starting transfers between devices, group_sum(): q = p_mine + lax.ppermute(p_other, 'col', pair)  14.5 us
    pallas_call x6, Pallas kernels, body(): call(functools.partial(direct_kernel, float(rows_n * cols_n * width), ste...  12.1 us
    pallas_call x6, Pallas kernels, body(): call(back_kernel, jax.ShapeDtypeStruct((rows_n, 2 * NV * width // LANES +...  9.58 us
    all_to_all x1, starting transfers between devices, body(): gathered = lax.all_to_all(spread, 'row', 0, 0, tiled=True)  7.57 us
  transfers between devices with their start and end apart: 37, of which 29 were waited for; matrix products, arithmetic and copies ran while one was open for 1% of the time, Pallas kernels for 2%

profile of v4, /device:TPU:1, one launch (start us, length us, event | category | flops | bytes accessed | tf_op | source)
XLA Modules:
  0.0 215.5 jit_solution(15885712114651484005)
XLA Ops:
  2.0 7.6 %all-to-all-start = ((bf16[16,16,256]{2,1,0:T(8,128)(2,1)}), bf16[16,16,256]{2,1,0:T(8,128)(2,1)S(1)}, u32[]{:S(2)}, u32[]{:S(2)}) async-start(bf16[16,16,256]{2,1,0:T(8,128)(2,1)} %broadcast_in_dim.29), calls=%async_computation | async-start | bytes 262144 | tf_op jit(solution)/shard_map/all_to_all | solution.py:465
  13.6 2.8 %all-to-all-done.gathered = bf16[16,16,256]{2,1,0:T(8,128)(2,1)S(1)} async-done(((bf16[16,16,256]{2,1,0:T(8,128)(2,1)}), bf16[16,16,256]{2,1,0:T(8,128)(2,1)S(1)}, u32[]{:S(2)}, u32[]{:S(2)}) %all-to-all-start) | async-done | bytes 131104 | tf_op jit(solution)/shard_map/all_to_all | solution.py:465
  16.4 3.5 %shard_map.121 = (f32[136,128]{1,0:T(8,128)S(1)}, f32[136,128]{1,0:T(8,128)S(1)}) custom-call(s32[200]{0:T(256)S(1)} %concatenate.3.table, bf16[16,16,256]{2,1,0:T(8,128)(2,1)S(1)} %all-to-all-done.gathered, f32[1,256]{1,0:T(1,128)} %bitcast.6, bf16[32,256,256]{2,1,0:T(8,128)(2,1)} %tiles_hbm.1), custom_call_target="tpu_custom_call" | custom-call | tf_op jit(solution)/shard_map/pallas_call | solution.py:466
  22.8 3.8 %collective-permute-start.3 = (f32[136,128]{1,0:T(8,128)S(1)}, f32[136,128]{1,0:T(8,128)S(1)}, u32[]{:S(2)}, u32[]{:S(2)}) collective-permute-start(f32[136,128]{1,0:T(8,128)S(1)} %add.92), channel_id=1, source_target_pairs={{0,2},{1,7},{2,4},{3,1},{4,6},{5,3},{6,0},{7,5},{8,10},{9,15},{10,... | collective-permute-start | bytes 208904 | tf_op jit(solution)/shard_map/ppermute | solution.py:455
  28.0 4.8 %collective-permute-done.2 = f32[136,128]{1,0:T(8,128)S(1)} collective-permute-done((f32[136,128]{1,0:T(8,128)S(1)}, f32[136,128]{1,0:T(8,128)S(1)}, u32[]{:S(2)}, u32[]{:S(2)}) %collective-permute-start.2) | collective-permute-done | bytes 69664 | tf_op jit(solution)/shard_map/ppermute | solution.py:455
  37.1 11.1 %all_to_all.40.gathered = s16[16,72,128]{2,1,0:T(8,128)(2,1)S(1)} all-to-all(s16[16,72,128]{2,1,0:T(8,128)(2,1)S(1)} %shard_map.123), channel_id=1, replica_groups=mesh['row'=16,'col'=8] {'row'}, dimensions={0} | all-to-all | bytes 589824 | tf_op jit(solution)/shard_map/all_to_all | solution.py:502
  56.7 3.7 %collective-permute-done.7 = f32[4,16,256]{2,1,0:T(8,128)S(1)} collective-permute-done((f32[4,16,256]{2,1,0:T(8,128)S(1)}, f32[4,16,256]{2,1,0:T(8,128)S(1)}, u32[]{:S(2)}, u32[]{:S(2)}) %collective-permute-start.7) | collective-permute-done | bytes 65568 | tf_op jit(solution)/shard_map/ppermute | solution.py:455
  65.1 10.9 %all_to_all.41.gathered = s16[16,72,128]{2,1,0:T(8,128)(2,1)S(1)} all-to-all(s16[16,72,128]{2,1,0:T(8,128)(2,1)S(1)} %shard_map.125), channel_id=1, replica_groups=mesh['row'=16,'col'=8] {'row'}, dimensions={0} | all-to-all | bytes 589824 | tf_op jit(solution)/shard_map/all_to_all | solution.py:502
  84.3 3.5 %collective-permute-done.12 = f32[4,16,256]{2,1,0:T(8,128)S(1)} collective-permute-done((f32[4,16,256]{2,1,0:T(8,128)S(1)}, f32[4,16,256]{2,1,0:T(8,128)S(1)}, u32[]{:S(2)}, u32[]{:S(2)}) %collective-permute-start.12) | collective-permute-done | bytes 65568 | tf_op jit(solution)/shard_map/ppermute | solution.py:455
  87.8 2.8 %collective-permute-start.14 = (f32[4,16,256]{2,1,0:T(8,128)S(1)}, f32[4,16,256]{2,1,0:T(8,128)S(1)}, u32[]{:S(2)}, u32[]{:S(2)}) collective-permute-start(f32[4,16,256]{2,1,0:T(8,128)S(1)} %add_add_fusion.5.z_mine.refs_5_), channel_id=1, source_target_pairs={{0,1},{1,0},{2,3},{3,2},{4,5},{5,4},{6,7},{7,6},{8,9},{9,8},{10,11... | collective-permute-start | bytes 196616 | tf_op jit(solution)/shard_map/ppermute | solution.py:457
  93.1 10.9 %all_to_all.42.gathered = s16[16,72,128]{2,1,0:T(8,128)(2,1)S(1)} all-to-all(s16[16,72,128]{2,1,0:T(8,128)(2,1)S(1)} %shard_map.127), channel_id=1, replica_groups=mesh['row'=16,'col'=8] {'row'}, dimensions={0} | all-to-all | bytes 589824 | tf_op jit(solution)/shard_map/all_to_all | solution.py:502
  112.5 3.6 %collective-permute-done.17 = f32[4,16,256]{2,1,0:T(8,128)S(1)} collective-permute-done((f32[4,16,256]{2,1,0:T(8,128)S(1)}, f32[4,16,256]{2,1,0:T(8,128)S(1)}, u32[]{:S(2)}, u32[]{:S(2)}) %collective-permute-start.17) | collective-permute-done | bytes 65568 | tf_op jit(solution)/shard_map/ppermute | solution.py:455
  116.2 2.7 %collective-permute-start.19 = (f32[4,16,256]{2,1,0:T(8,128)S(1)}, f32[4,16,256]{2,1,0:T(8,128)S(1)}, u32[]{:S(2)}, u32[]{:S(2)}) collective-permute-start(f32[4,16,256]{2,1,0:T(8,128)S(1)} %add_add_fusion.4.z_mine.refs_5_), channel_id=1, source_target_pairs={{0,1},{1,0},{2,3},{3,2},{4,5},{5,4},{6,7},{7,6},{8,9},{9,8},{10,11... | collective-permute-start | bytes 196616 | tf_op jit(solution)/shard_map/ppermute | solution.py:457
  121.3 10.9 %all_to_all.43.gathered = s16[16,72,128]{2,1,0:T(8,128)(2,1)S(1)} all-to-all(s16[16,72,128]{2,1,0:T(8,128)(2,1)S(1)} %shard_map.129), channel_id=1, replica_groups=mesh['row'=16,'col'=8] {'row'}, dimensions={0} | all-to-all | bytes 589824 | tf_op jit(solution)/shard_map/all_to_all | solution.py:502
  140.5 3.7 %collective-permute-done.22 = f32[4,16,256]{2,1,0:T(8,128)S(1)} collective-permute-done((f32[4,16,256]{2,1,0:T(8,128)S(1)}, f32[4,16,256]{2,1,0:T(8,128)S(1)}, u32[]{:S(2)}, u32[]{:S(2)}) %collective-permute-start.22) | collective-permute-done | bytes 65568 | tf_op jit(solution)/shard_map/ppermute | solution.py:455
  144.2 2.6 %collective-permute-start.24 = (f32[4,16,256]{2,1,0:T(8,128)S(1)}, f32[4,16,256]{2,1,0:T(8,128)S(1)}, u32[]{:S(2)}, u32[]{:S(2)}) collective-permute-start(f32[4,16,256]{2,1,0:T(8,128)S(1)} %add_add_fusion.3.z_mine.refs_5_), channel_id=1, source_target_pairs={{0,1},{1,0},{2,3},{3,2},{4,5},{5,4},{6,7},{7,6},{8,9},{9,8},{10,11... | collective-permute-start | bytes 196616 | tf_op jit(solution)/shard_map/ppermute | solution.py:457
  149.4 10.9 %all_to_all.44.gathered = s16[16,72,128]{2,1,0:T(8,128)(2,1)S(1)} all-to-all(s16[16,72,128]{2,1,0:T(8,128)(2,1)S(1)} %shard_map.131), channel_id=1, replica_groups=mesh['row'=16,'col'=8] {'row'}, dimensions={0} | all-to-all | bytes 589824 | tf_op jit(solution)/shard_map/all_to_all | solution.py:502
  168.5 3.7 %collective-permute-done.27 = f32[4,16,256]{2,1,0:T(8,128)S(1)} collective-permute-done((f32[4,16,256]{2,1,0:T(8,128)S(1)}, f32[4,16,256]{2,1,0:T(8,128)S(1)}, u32[]{:S(2)}, u32[]{:S(2)}) %collective-permute-start.27) | collective-permute-done | bytes 65568 | tf_op jit(solution)/shard_map/ppermute | solution.py:455
  172.3 2.6 %collective-permute-start.29 = (f32[4,16,256]{2,1,0:T(8,128)S(1)}, f32[4,16,256]{2,1,0:T(8,128)S(1)}, u32[]{:S(2)}, u32[]{:S(2)}) collective-permute-start(f32[4,16,256]{2,1,0:T(8,128)S(1)} %add_add_fusion.2.z_mine), channel_id=1, source_target_pairs={{0,1},{1,0},{2,3},{3,2},{4,5},{5,4},{6,7},{7,6},{8,9},{9,8},{10,11... | collective-permute-start | bytes 196616 | tf_op jit(solution)/shard_map/ppermute | solution.py:457
  177.4 10.9 %all_to_all.45.gathered = s16[16,72,128]{2,1,0:T(8,128)(2,1)S(1)} all-to-all(s16[16,72,128]{2,1,0:T(8,128)(2,1)S(1)} %shard_map.133), channel_id=1, replica_groups=mesh['row'=16,'col'=8] {'row'}, dimensions={0} | all-to-all | bytes 589824 | tf_op jit(solution)/shard_map/all_to_all | solution.py:502
  196.6 3.7 %collective-permute-done.32 = f32[4,16,256]{2,1,0:T(8,128)S(1)} collective-permute-done((f32[4,16,256]{2,1,0:T(8,128)S(1)}, f32[4,16,256]{2,1,0:T(8,128)S(1)}, u32[]{:S(2)}, u32[]{:S(2)}) %collective-permute-start.32) | collective-permute-done | bytes 65568 | tf_op jit(solution)/shard_map/ppermute | solution.py:455
  200.3 2.6 %collective-permute-start.34 = (f32[4,16,256]{2,1,0:T(8,128)S(1)}, f32[4,16,256]{2,1,0:T(8,128)S(1)}, u32[]{:S(2)}, u32[]{:S(2)}) collective-permute-start(f32[4,16,256]{2,1,0:T(8,128)S(1)} %add_add_fusion.1.refs_12_.refs_0_), channel_id=1, source_target_pairs={{0,1},{1,0},{2,3},{3,2},{4,5},{5,4},{6,7},{7,6},{8,9},{9,8},{10,11... | collective-permute-start | bytes 196616 | tf_op jit(solution)/shard_map/ppermute | solution.py:457
  204.6 3.5 %all-to-all-start.7 = ((f32[16,8,128]{2,1,0:T(8,128)}), f32[16,8,128]{2,1,0:T(8,128)S(1)}, u32[]{:S(2)}, u32[]{:S(2)}) async-start(f32[16,8,128]{2,1,0:T(8,128)} %shard_map.136), calls=%async_computation.7 | async-start | bytes 131072 | tf_op jit(solution)/shard_map/all_to_all | solution.py:521
  209.8 4.8 %all-to-all-done.7.gathered = f32[16,8,128]{2,1,0:T(8,128)S(1)} async-done(((f32[16,8,128]{2,1,0:T(8,128)}), f32[16,8,128]{2,1,0:T(8,128)S(1)}, u32[]{:S(2)}, u32[]{:S(2)}) %all-to-all-start.7) | async-done | bytes 65568 | tf_op jit(solution)/shard_map/all_to_all | solution.py:521
  (95 shorter events, 81.6 us)
Async XLA Ops:
  2.0 14.4 %all-to-all-start = ((bf16[16,16,256]{2,1,0:T(8,128)(2,1)}), bf16[16,16,256]{2,1,0:T(8,128)(2,1)S(1)}, u32[]{:S(2)}, u32[]{:S(2)}) async-start(bf16[16,16,256]{2,1,0:T(8,128)(2,1)} %broadcast_in_dim.29), calls=%async_computation | async-start | bytes 262144 | tf_op jit(solution)/shard_map/all_to_all | solution.py:465
  22.8 5.2 %collective-permute-start.3 = (f32[136,128]{1,0:T(8,128)S(1)}, f32[136,128]{1,0:T(8,128)S(1)}, u32[]{:S(2)}, u32[]{:S(2)}) collective-permute-start(f32[136,128]{1,0:T(8,128)S(1)} %add.92), channel_id=1, source_target_pairs={{0,2},{1,7},{2,4},{3,1},{4,6},{5,3},{6,0},{7,5},{8,10},{9,15},{10,... | collective-permute-start | bytes 208904 | tf_op jit(solution)/shard_map/ppermute | solution.py:455
  26.7 6.1 %collective-permute-start.2 = (f32[136,128]{1,0:T(8,128)S(1)}, f32[136,128]{1,0:T(8,128)S(1)}, u32[]{:S(2)}, u32[]{:S(2)}) collective-permute-start(f32[136,128]{1,0:T(8,128)S(1)} %add.92), channel_id=1, source_target_pairs={{0,6},{1,3},{2,0},{3,5},{4,2},{5,7},{6,4},{7,1},{8,14},{9,11},{10,... | collective-permute-start | bytes 208904 | tf_op jit(solution)/shard_map/ppermute | solution.py:455
  26.7 6.1 %collective-permute-start.1 = (f32[136,128]{1,0:T(8,128)S(1)}, f32[136,128]{1,0:T(8,128)S(1)}, u32[]{:S(2)}, u32[]{:S(2)}) collective-permute-start(f32[136,128]{1,0:T(8,128)S(1)} %add.92), channel_id=1, source_target_pairs={{0,4},{1,5},{2,6},{3,7},{4,0},{5,1},{6,2},{7,3},{8,12},{9,13},{10,... | collective-permute-start | bytes 208904 | tf_op jit(solution)/shard_map/ppermute | solution.py:455
  53.1 3.6 %collective-permute-start.8 = (f32[4,16,256]{2,1,0:T(8,128)S(1)}, f32[4,16,256]{2,1,0:T(8,128)S(1)}, u32[]{:S(2)}, u32[]{:S(2)}) collective-permute-start(f32[4,16,256]{2,1,0:T(8,128)S(1)} %add.96), channel_id=1, source_target_pairs={{0,2},{1,7},{2,4},{3,1},{4,6},{5,3},{6,0},{7,5},{8,10},{9,15},{10,... | collective-permute-start | bytes 196616 | tf_op jit(solution)/shard_map/ppermute | solution.py:455
  55.4 5.0 %collective-permute-start.7 = (f32[4,16,256]{2,1,0:T(8,128)S(1)}, f32[4,16,256]{2,1,0:T(8,128)S(1)}, u32[]{:S(2)}, u32[]{:S(2)}) collective-permute-start(f32[4,16,256]{2,1,0:T(8,128)S(1)} %add.96), channel_id=1, source_target_pairs={{0,6},{1,3},{2,0},{3,5},{4,2},{5,7},{6,4},{7,1},{8,14},{9,11},{10,... | collective-permute-start | bytes 196616 | tf_op jit(solution)/shard_map/ppermute | solution.py:455
  55.4 5.0 %collective-permute-start.6 = (f32[4,16,256]{2,1,0:T(8,128)S(1)}, f32[4,16,256]{2,1,0:T(8,128)S(1)}, u32[]{:S(2)}, u32[]{:S(2)}) collective-permute-start(f32[4,16,256]{2,1,0:T(8,128)S(1)} %add.96), channel_id=1, source_target_pairs={{0,4},{1,5},{2,6},{3,7},{4,0},{5,1},{6,2},{7,3},{8,12},{9,13},{10,... | collective-permute-start | bytes 196616 | tf_op jit(solution)/shard_map/ppermute | solution.py:455
  82.7 5.0 %collective-permute-start.12 = (f32[4,16,256]{2,1,0:T(8,128)S(1)}, f32[4,16,256]{2,1,0:T(8,128)S(1)}, u32[]{:S(2)}, u32[]{:S(2)}) collective-permute-start(f32[4,16,256]{2,1,0:T(8,128)S(1)} %add.100), channel_id=1, source_target_pairs={{0,6},{1,3},{2,0},{3,5},{4,2},{5,7},{6,4},{7,1},{8,14},{9,11},{10,... | collective-permute-start | bytes 196616 | tf_op jit(solution)/shard_map/ppermute | solution.py:455
  82.7 5.0 %collective-permute-start.11 = (f32[4,16,256]{2,1,0:T(8,128)S(1)}, f32[4,16,256]{2,1,0:T(8,128)S(1)}, u32[]{:S(2)}, u32[]{:S(2)}) collective-permute-start(f32[4,16,256]{2,1,0:T(8,128)S(1)} %add.100), channel_id=1, source_target_pairs={{0,4},{1,5},{2,6},{3,7},{4,0},{5,1},{6,2},{7,3},{8,12},{9,13},{10,... | collective-permute-start | bytes 196616 | tf_op jit(solution)/shard_map/ppermute | solution.py:455
  87.8 3.7 %collective-permute-start.14 = (f32[4,16,256]{2,1,0:T(8,128)S(1)}, f32[4,16,256]{2,1,0:T(8,128)S(1)}, u32[]{:S(2)}, u32[]{:S(2)}) collective-permute-start(f32[4,16,256]{2,1,0:T(8,128)S(1)} %add_add_fusion.5.z_mine.refs_5_), channel_id=1, source_target_pairs={{0,1},{1,0},{2,3},{3,2},{4,5},{5,4},{6,7},{7,6},{8,9},{9,8},{10,11... | collective-permute-start | bytes 196616 | tf_op jit(solution)/shard_map/ppermute | solution.py:457
  109.1 3.4 %collective-permute-start.18 = (f32[4,16,256]{2,1,0:T(8,128)S(1)}, f32[4,16,256]{2,1,0:T(8,128)S(1)}, u32[]{:S(2)}, u32[]{:S(2)}) collective-permute-start(f32[4,16,256]{2,1,0:T(8,128)S(1)} %add.104), channel_id=1, source_target_pairs={{0,2},{1,7},{2,4},{3,1},{4,6},{5,3},{6,0},{7,5},{8,10},{9,15},{10,... | collective-permute-start | bytes 196616 | tf_op jit(solution)/shard_map/ppermute | solution.py:455
  110.3 5.9 %collective-permute-start.17 = (f32[4,16,256]{2,1,0:T(8,128)S(1)}, f32[4,16,256]{2,1,0:T(8,128)S(1)}, u32[]{:S(2)}, u32[]{:S(2)}) collective-permute-start(f32[4,16,256]{2,1,0:T(8,128)S(1)} %add.104), channel_id=1, source_target_pairs={{0,6},{1,3},{2,0},{3,5},{4,2},{5,7},{6,4},{7,1},{8,14},{9,11},{10,... | collective-permute-start | bytes 196616 | tf_op jit(solution)/shard_map/ppermute | solution.py:455
  110.8 5.3 %collective-permute-start.16 = (f32[4,16,256]{2,1,0:T(8,128)S(1)}, f32[4,16,256]{2,1,0:T(8,128)S(1)}, u32[]{:S(2)}, u32[]{:S(2)}) collective-permute-start(f32[4,16,256]{2,1,0:T(8,128)S(1)} %add.104), channel_id=1, source_target_pairs={{0,4},{1,5},{2,6},{3,7},{4,0},{5,1},{6,2},{7,3},{8,12},{9,13},{10,... | collective-permute-start | bytes 196616 | tf_op jit(solution)/shard_map/ppermute | solution.py:455
  116.2 3.6 %collective-permute-start.19 = (f32[4,16,256]{2,1,0:T(8,128)S(1)}, f32[4,16,256]{2,1,0:T(8,128)S(1)}, u32[]{:S(2)}, u32[]{:S(2)}) collective-permute-start(f32[4,16,256]{2,1,0:T(8,128)S(1)} %add_add_fusion.4.z_mine.refs_5_), channel_id=1, source_target_pairs={{0,1},{1,0},{2,3},{3,2},{4,5},{5,4},{6,7},{7,6},{8,9},{9,8},{10,11... | collective-permute-start | bytes 196616 | tf_op jit(solution)/shard_map/ppermute | solution.py:457
  138.2 6.0 %collective-permute-start.22 = (f32[4,16,256]{2,1,0:T(8,128)S(1)}, f32[4,16,256]{2,1,0:T(8,128)S(1)}, u32[]{:S(2)}, u32[]{:S(2)}) collective-permute-start(f32[4,16,256]{2,1,0:T(8,128)S(1)} %add.108), channel_id=1, source_target_pairs={{0,6},{1,3},{2,0},{3,5},{4,2},{5,7},{6,4},{7,1},{8,14},{9,11},{10,... | collective-permute-start | bytes 196616 | tf_op jit(solution)/shard_map/ppermute | solution.py:455
  138.9 5.4 %collective-permute-start.21 = (f32[4,16,256]{2,1,0:T(8,128)S(1)}, f32[4,16,256]{2,1,0:T(8,128)S(1)}, u32[]{:S(2)}, u32[]{:S(2)}) collective-permute-start(f32[4,16,256]{2,1,0:T(8,128)S(1)} %add.108), channel_id=1, source_target_pairs={{0,4},{1,5},{2,6},{3,7},{4,0},{5,1},{6,2},{7,3},{8,12},{9,13},{10,... | collective-permute-start | bytes 196616 | tf_op jit(solution)/shard_map/ppermute | solution.py:455
  144.2 3.5 %collective-permute-start.24 = (f32[4,16,256]{2,1,0:T(8,128)S(1)}, f32[4,16,256]{2,1,0:T(8,128)S(1)}, u32[]{:S(2)}, u32[]{:S(2)}) collective-permute-start(f32[4,16,256]{2,1,0:T(8,128)S(1)} %add_add_fusion.3.z_mine.refs_5_), channel_id=1, source_target_pairs={{0,1},{1,0},{2,3},{3,2},{4,5},{5,4},{6,7},{7,6},{8,9},{9,8},{10,11... | collective-permute-start | bytes 196616 | tf_op jit(solution)/shard_map/ppermute | solution.py:457
  166.3 6.0 %collective-permute-start.27 = (f32[4,16,256]{2,1,0:T(8,128)S(1)}, f32[4,16,256]{2,1,0:T(8,128)S(1)}, u32[]{:S(2)}, u32[]{:S(2)}) collective-permute-start(f32[4,16,256]{2,1,0:T(8,128)S(1)} %add.112), channel_id=1, source_target_pairs={{0,6},{1,3},{2,0},{3,5},{4,2},{5,7},{6,4},{7,1},{8,14},{9,11},{10,... | collective-permute-start | bytes 196616 | tf_op jit(solution)/shard_map/ppermute | solution.py:455
  166.9 5.3 %collective-permute-start.26 = (f32[4,16,256]{2,1,0:T(8,128)S(1)}, f32[4,16,256]{2,1,0:T(8,128)S(1)}, u32[]{:S(2)}, u32[]{:S(2)}) collective-permute-start(f32[4,16,256]{2,1,0:T(8,128)S(1)} %add.112), channel_id=1, source_target_pairs={{0,4},{1,5},{2,6},{3,7},{4,0},{5,1},{6,2},{7,3},{8,12},{9,13},{10,... | collective-permute-start | bytes 196616 | tf_op jit(solution)/shard_map/ppermute | solution.py:455
  172.3 3.5 %collective-permute-start.29 = (f32[4,16,256]{2,1,0:T(8,128)S(1)}, f32[4,16,256]{2,1,0:T(8,128)S(1)}, u32[]{:S(2)}, u32[]{:S(2)}) collective-permute-start(f32[4,16,256]{2,1,0:T(8,128)S(1)} %add_add_fusion.2.z_mine), channel_id=1, source_target_pairs={{0,1},{1,0},{2,3},{3,2},{4,5},{5,4},{6,7},{7,6},{8,9},{9,8},{10,11... | collective-permute-start | bytes 196616 | tf_op jit(solution)/shard_map/ppermute | solution.py:457
  194.3 6.0 %collective-permute-start.32 = (f32[4,16,256]{2,1,0:T(8,128)S(1)}, f32[4,16,256]{2,1,0:T(8,128)S(1)}, u32[]{:S(2)}, u32[]{:S(2)}) collective-permute-start(f32[4,16,256]{2,1,0:T(8,128)S(1)} %add.116), channel_id=1, source_target_pairs={{0,6},{1,3},{2,0},{3,5},{4,2},{5,7},{6,4},{7,1},{8,14},{9,11},{10,... | collective-permute-start | bytes 196616 | tf_op jit(solution)/shard_map/ppermute | solution.py:455
  194.9 5.3 %collective-permute-start.31 = (f32[4,16,256]{2,1,0:T(8,128)S(1)}, f32[4,16,256]{2,1,0:T(8,128)S(1)}, u32[]{:S(2)}, u32[]{:S(2)}) collective-permute-start(f32[4,16,256]{2,1,0:T(8,128)S(1)} %add.116), channel_id=1, source_target_pairs={{0,4},{1,5},{2,6},{3,7},{4,0},{5,1},{6,2},{7,3},{8,12},{9,13},{10,... | collective-permute-start | bytes 196616 | tf_op jit(solution)/shard_map/ppermute | solution.py:455
  200.3 3.5 %collective-permute-start.34 = (f32[4,16,256]{2,1,0:T(8,128)S(1)}, f32[4,16,256]{2,1,0:T(8,128)S(1)}, u32[]{:S(2)}, u32[]{:S(2)}) collective-permute-start(f32[4,16,256]{2,1,0:T(8,128)S(1)} %add_add_fusion.1.refs_12_.refs_0_), channel_id=1, source_target_pairs={{0,1},{1,0},{2,3},{3,2},{4,5},{5,4},{6,7},{7,6},{8,9},{9,8},{10,11... | collective-permute-start | bytes 196616 | tf_op jit(solution)/shard_map/ppermute | solution.py:457
  204.6 9.9 %all-to-all-start.7 = ((f32[16,8,128]{2,1,0:T(8,128)}), f32[16,8,128]{2,1,0:T(8,128)S(1)}, u32[]{:S(2)}, u32[]{:S(2)}) async-start(f32[16,8,128]{2,1,0:T(8,128)} %shard_map.136), calls=%async_computation.7 | async-start | bytes 131072 | tf_op jit(solution)/shard_map/all_to_all | solution.py:521
  (14 other events, 52.0 us)

commit v5 on v4

--- a/solution.py
+++ b/solution.py
@@ -153,7 +153,7 @@
     return tuple(jnp.stack([wide_of(ref, b * parts * NV, parts) for b in range(half)]) for ref in (mine, other))
 
 
-def load_kernel(source, target, sems):
+def load_kernel(source, target, flipped, sems):
     step = source.shape[0] // CHUNKS
     copies = [
         pltpu.make_async_copy(source.at[pl.ds(c * step, step)], target.at[pl.ds(c * step, step)], sems.at[c])
@@ -161,8 +161,10 @@
     ]
     for copy in copies:
         copy.start()
-    for copy in copies:
+    for c, copy in enumerate(copies):
         copy.wait()
+        for t in range(c * step, (c + 1) * step):
+            flipped[t] = jnp.transpose(target[t])
 
 
 def dipole_kernel(table, gathered, energies_hbm, tiles_hbm, p_mine, p_other, xs, acc, energies, tiles, sems):
@@ -257,7 +259,7 @@
     acc[...] = jnp.zeros(acc.shape, F32)
     for t in range(tiles.shape[0]):
         x = xs[entry(table, DIRECT_FROM, t, slots)]
-        res = lax.dot_general(x, tiles[t], (((1,), (1,)), ((), ())), preferred_element_type=F32)
+        res = jnp.dot(x, tiles[t], preferred_element_type=F32)
         acc[entry(table, DIRECT_TO, t, slots)] += res[:NV] + res[NV:]
     column = functools.partial(unpack, dots)
     norm = column(0)
@@ -478,11 +480,11 @@
         compiler_params=pltpu.CompilerParams(vmem_limit_bytes=24 << 20),
     )(table, gathered, *(pltpu.with_memory_space_constraint(a, pltpu.HBM) for a in (diagonal, dipole_tiles)))
     p_mine, h_tiles = lax.optimization_barrier((p_mine, pltpu.with_memory_space_constraint(h_tiles, pltpu.HBM)))
-    h_tiles = pl.pallas_call(
+    h_tiles, h_flipped = pl.pallas_call(
         load_kernel,
-        out_shape=jax.ShapeDtypeStruct(h_tiles.shape, h_tiles.dtype),
+        out_shape=(jax.ShapeDtypeStruct(h_tiles.shape, h_tiles.dtype),) * 2,
         in_specs=[HBM],
-        out_specs=VM,
+        out_specs=(VM, VM),
         scratch_shapes=[pltpu.SemaphoreType.DMA((CHUNKS,))],
         compiler_params=pltpu.CompilerParams(vmem_limit_bytes=24 << 20),
     )(h_tiles)
@@ -511,7 +513,7 @@
             1,
             5 + len(extra),
             [pltpu.VMEM((rows_n + 1, 2 * NV, width), BF16), pltpu.VMEM((cols_n, NV, width), F32)],
-        )(table, gathered, h_tiles, diagonal, *z, *extra)
+        )(table, gathered, h_flipped, diagonal, *z, *extra)
         states.append(state)
         basis.append((qn_mine, qn_other))
         z = group_sum(p_mine, p_other)

time: 216 us -> 214 us (level)
  Pallas kernels: 30.8 us -> 28.4 us
    pallas_call x6, Pallas kernels: 12.1 us -> 9.34 us  [body(): call(functools.partial(direct_kernel, float(rows_n * cols_n * width), ste...]
where the time goes in v5:
time: 214 us; the launch traced here: 213 us
  blocking collectives  65.7 us (31%)
  starting transfers between devices  61.9 us (29%)
  waiting for transfers between devices  50.4 us (24%)
  Pallas kernels  28.4 us (13%)
  other arithmetic  2.22 us (1%)
  between operations  2.16 us (1%)
    all_to_all x6, blocking collectives, body(): gathered = lax.all_to_all(payload, 'row', 0, 0, tiled=True)  65.7 us
    ppermute x21, waiting for transfers between devices, group_sum(): moved.append(lax.ppermute(q, 'col', ring(d)))  31.1 us
    ppermute x21, starting transfers between devices, group_sum(): moved.append(lax.ppermute(q, 'col', ring(d)))  20.4 us
    ppermute x7, starting transfers between devices, group_sum(): return (mine, lax.ppermute(mine, 'col', pair))  16 us
    ppermute x7, starting transfers between devices, group_sum(): q = p_mine + lax.ppermute(p_other, 'col', pair)  14.5 us
    pallas_call x6, Pallas kernels, body(): call(back_kernel, jax.ShapeDtypeStruct((rows_n, 2 * NV * width // LANES +...  9.58 us
    pallas_call x6, Pallas kernels, body(): call(functools.partial(direct_kernel, float(rows_n * cols_n * width), ste...  9.34 us
    all_to_all x1, starting transfers between devices, body(): gathered = lax.all_to_all(spread, 'row', 0, 0, tiled=True)  7.57 us
  transfers between devices with their start and end apart: 37, of which 29 were waited for; matrix products, arithmetic and copies ran while one was open for 1% of the time, Pallas kernels for 2%

profile of v5, /device:TPU:1, one launch (start us, length us, event | category | flops | bytes accessed | tf_op | source)
XLA Modules:
  0.0 212.9 jit_solution(1821737186224754189)
XLA Ops:
  2.0 7.6 %all-to-all-start = ((bf16[16,16,256]{2,1,0:T(8,128)(2,1)}), bf16[16,16,256]{2,1,0:T(8,128)(2,1)S(1)}, u32[]{:S(2)}, u32[]{:S(2)}) async-start(bf16[16,16,256]{2,1,0:T(8,128)(2,1)} %broadcast_in_dim.29), calls=%async_computation | async-start | bytes 262144 | tf_op jit(solution)/shard_map/all_to_all | solution.py:467
  13.6 2.8 %all-to-all-done.gathered = bf16[16,16,256]{2,1,0:T(8,128)(2,1)S(1)} async-done(((bf16[16,16,256]{2,1,0:T(8,128)(2,1)}), bf16[16,16,256]{2,1,0:T(8,128)(2,1)S(1)}, u32[]{:S(2)}, u32[]{:S(2)}) %all-to-all-start) | async-done | bytes 131104 | tf_op jit(solution)/shard_map/all_to_all | solution.py:467
  16.4 3.5 %shard_map.121 = (f32[136,128]{1,0:T(8,128)S(1)}, f32[136,128]{1,0:T(8,128)S(1)}) custom-call(s32[200]{0:T(256)S(1)} %concatenate.3.table, bf16[16,16,256]{2,1,0:T(8,128)(2,1)S(1)} %all-to-all-done.gathered, f32[1,256]{1,0:T(1,128)} %bitcast.6, bf16[32,256,256]{2,1,0:T(8,128)(2,1)} %tiles_hbm.1), custom_call_target="tpu_custom_call" | custom-call | tf_op jit(solution)/shard_map/pallas_call | solution.py:468
  22.8 3.8 %collective-permute-start.3 = (f32[136,128]{1,0:T(8,128)S(1)}, f32[136,128]{1,0:T(8,128)S(1)}, u32[]{:S(2)}, u32[]{:S(2)}) collective-permute-start(f32[136,128]{1,0:T(8,128)S(1)} %add.92), channel_id=1, source_target_pairs={{0,2},{1,7},{2,4},{3,1},{4,6},{5,3},{6,0},{7,5},{8,10},{9,15},{10,... | collective-permute-start | bytes 208904 | tf_op jit(solution)/shard_map/ppermute | solution.py:457
  28.0 4.8 %collective-permute-done.2 = f32[136,128]{1,0:T(8,128)S(1)} collective-permute-done((f32[136,128]{1,0:T(8,128)S(1)}, f32[136,128]{1,0:T(8,128)S(1)}, u32[]{:S(2)}, u32[]{:S(2)}) %collective-permute-start.2) | collective-permute-done | bytes 69664 | tf_op jit(solution)/shard_map/ppermute | solution.py:457
  37.5 11.1 %all_to_all.40.gathered = s16[16,72,128]{2,1,0:T(8,128)(2,1)S(1)} all-to-all(s16[16,72,128]{2,1,0:T(8,128)(2,1)S(1)} %shard_map.123), channel_id=1, replica_groups=mesh['row'=16,'col'=8] {'row'}, dimensions={0} | all-to-all | bytes 589824 | tf_op jit(solution)/shard_map/all_to_all | solution.py:504
  56.6 3.7 %collective-permute-done.7 = f32[4,16,256]{2,1,0:T(8,128)S(1)} collective-permute-done((f32[4,16,256]{2,1,0:T(8,128)S(1)}, f32[4,16,256]{2,1,0:T(8,128)S(1)}, u32[]{:S(2)}, u32[]{:S(2)}) %collective-permute-start.7) | collective-permute-done | bytes 65568 | tf_op jit(solution)/shard_map/ppermute | solution.py:457
  65.0 10.9 %all_to_all.41.gathered = s16[16,72,128]{2,1,0:T(8,128)(2,1)S(1)} all-to-all(s16[16,72,128]{2,1,0:T(8,128)(2,1)S(1)} %shard_map.125), channel_id=1, replica_groups=mesh['row'=16,'col'=8] {'row'}, dimensions={0} | all-to-all | bytes 589824 | tf_op jit(solution)/shard_map/all_to_all | solution.py:504
  83.7 3.5 %collective-permute-done.12 = f32[4,16,256]{2,1,0:T(8,128)S(1)} collective-permute-done((f32[4,16,256]{2,1,0:T(8,128)S(1)}, f32[4,16,256]{2,1,0:T(8,128)S(1)}, u32[]{:S(2)}, u32[]{:S(2)}) %collective-permute-start.12) | collective-permute-done | bytes 65568 | tf_op jit(solution)/shard_map/ppermute | solution.py:457
  87.2 2.8 %collective-permute-start.14 = (f32[4,16,256]{2,1,0:T(8,128)S(1)}, f32[4,16,256]{2,1,0:T(8,128)S(1)}, u32[]{:S(2)}, u32[]{:S(2)}) collective-permute-start(f32[4,16,256]{2,1,0:T(8,128)S(1)} %add_add_fusion.5.z_mine.refs_5_), channel_id=1, source_target_pairs={{0,1},{1,0},{2,3},{3,2},{4,5},{5,4},{6,7},{7,6},{8,9},{9,8},{10,11... | collective-permute-start | bytes 196616 | tf_op jit(solution)/shard_map/ppermute | solution.py:459
  92.5 10.9 %all_to_all.42.gathered = s16[16,72,128]{2,1,0:T(8,128)(2,1)S(1)} all-to-all(s16[16,72,128]{2,1,0:T(8,128)(2,1)S(1)} %shard_map.127), channel_id=1, replica_groups=mesh['row'=16,'col'=8] {'row'}, dimensions={0} | all-to-all | bytes 589824 | tf_op jit(solution)/shard_map/all_to_all | solution.py:504
  111.3 3.6 %collective-permute-done.17 = f32[4,16,256]{2,1,0:T(8,128)S(1)} collective-permute-done((f32[4,16,256]{2,1,0:T(8,128)S(1)}, f32[4,16,256]{2,1,0:T(8,128)S(1)}, u32[]{:S(2)}, u32[]{:S(2)}) %collective-permute-start.17) | collective-permute-done | bytes 65568 | tf_op jit(solution)/shard_map/ppermute | solution.py:457
  114.9 2.7 %collective-permute-start.19 = (f32[4,16,256]{2,1,0:T(8,128)S(1)}, f32[4,16,256]{2,1,0:T(8,128)S(1)}, u32[]{:S(2)}, u32[]{:S(2)}) collective-permute-start(f32[4,16,256]{2,1,0:T(8,128)S(1)} %add_add_fusion.4.z_mine.refs_5_), channel_id=1, source_target_pairs={{0,1},{1,0},{2,3},{3,2},{4,5},{5,4},{6,7},{7,6},{8,9},{9,8},{10,11... | collective-permute-start | bytes 196616 | tf_op jit(solution)/shard_map/ppermute | solution.py:459
  120.1 10.9 %all_to_all.43.gathered = s16[16,72,128]{2,1,0:T(8,128)(2,1)S(1)} all-to-all(s16[16,72,128]{2,1,0:T(8,128)(2,1)S(1)} %shard_map.129), channel_id=1, replica_groups=mesh['row'=16,'col'=8] {'row'}, dimensions={0} | all-to-all | bytes 589824 | tf_op jit(solution)/shard_map/all_to_all | solution.py:504
  138.8 3.7 %collective-permute-done.22 = f32[4,16,256]{2,1,0:T(8,128)S(1)} collective-permute-done((f32[4,16,256]{2,1,0:T(8,128)S(1)}, f32[4,16,256]{2,1,0:T(8,128)S(1)}, u32[]{:S(2)}, u32[]{:S(2)}) %collective-permute-start.22) | collective-permute-done | bytes 65568 | tf_op jit(solution)/shard_map/ppermute | solution.py:457
  142.5 2.6 %collective-permute-start.24 = (f32[4,16,256]{2,1,0:T(8,128)S(1)}, f32[4,16,256]{2,1,0:T(8,128)S(1)}, u32[]{:S(2)}, u32[]{:S(2)}) collective-permute-start(f32[4,16,256]{2,1,0:T(8,128)S(1)} %add_add_fusion.3.z_mine.refs_5_), channel_id=1, source_target_pairs={{0,1},{1,0},{2,3},{3,2},{4,5},{5,4},{6,7},{7,6},{8,9},{9,8},{10,11... | collective-permute-start | bytes 196616 | tf_op jit(solution)/shard_map/ppermute | solution.py:459
  147.7 10.9 %all_to_all.44.gathered = s16[16,72,128]{2,1,0:T(8,128)(2,1)S(1)} all-to-all(s16[16,72,128]{2,1,0:T(8,128)(2,1)S(1)} %shard_map.131), channel_id=1, replica_groups=mesh['row'=16,'col'=8] {'row'}, dimensions={0} | all-to-all | bytes 589824 | tf_op jit(solution)/shard_map/all_to_all | solution.py:504
  166.4 3.7 %collective-permute-done.27 = f32[4,16,256]{2,1,0:T(8,128)S(1)} collective-permute-done((f32[4,16,256]{2,1,0:T(8,128)S(1)}, f32[4,16,256]{2,1,0:T(8,128)S(1)}, u32[]{:S(2)}, u32[]{:S(2)}) %collective-permute-start.27) | collective-permute-done | bytes 65568 | tf_op jit(solution)/shard_map/ppermute | solution.py:457
  170.1 2.6 %collective-permute-start.29 = (f32[4,16,256]{2,1,0:T(8,128)S(1)}, f32[4,16,256]{2,1,0:T(8,128)S(1)}, u32[]{:S(2)}, u32[]{:S(2)}) collective-permute-start(f32[4,16,256]{2,1,0:T(8,128)S(1)} %add_add_fusion.2.z_mine), channel_id=1, source_target_pairs={{0,1},{1,0},{2,3},{3,2},{4,5},{5,4},{6,7},{7,6},{8,9},{9,8},{10,11... | collective-permute-start | bytes 196616 | tf_op jit(solution)/shard_map/ppermute | solution.py:459
  175.3 10.9 %all_to_all.45.gathered = s16[16,72,128]{2,1,0:T(8,128)(2,1)S(1)} all-to-all(s16[16,72,128]{2,1,0:T(8,128)(2,1)S(1)} %shard_map.133), channel_id=1, replica_groups=mesh['row'=16,'col'=8] {'row'}, dimensions={0} | all-to-all | bytes 589824 | tf_op jit(solution)/shard_map/all_to_all | solution.py:504
  194.0 3.7 %collective-permute-done.32 = f32[4,16,256]{2,1,0:T(8,128)S(1)} collective-permute-done((f32[4,16,256]{2,1,0:T(8,128)S(1)}, f32[4,16,256]{2,1,0:T(8,128)S(1)}, u32[]{:S(2)}, u32[]{:S(2)}) %collective-permute-start.32) | collective-permute-done | bytes 65568 | tf_op jit(solution)/shard_map/ppermute | solution.py:457
  197.7 2.6 %collective-permute-start.34 = (f32[4,16,256]{2,1,0:T(8,128)S(1)}, f32[4,16,256]{2,1,0:T(8,128)S(1)}, u32[]{:S(2)}, u32[]{:S(2)}) collective-permute-start(f32[4,16,256]{2,1,0:T(8,128)S(1)} %add_add_fusion.1.refs_12_.refs_0_), channel_id=1, source_target_pairs={{0,1},{1,0},{2,3},{3,2},{4,5},{5,4},{6,7},{7,6},{8,9},{9,8},{10,11... | collective-permute-start | bytes 196616 | tf_op jit(solution)/shard_map/ppermute | solution.py:459
  202.0 3.5 %all-to-all-start.7 = ((f32[16,8,128]{2,1,0:T(8,128)}), f32[16,8,128]{2,1,0:T(8,128)S(1)}, u32[]{:S(2)}, u32[]{:S(2)}) async-start(f32[16,8,128]{2,1,0:T(8,128)} %shard_map.136), calls=%async_computation.7 | async-start | bytes 131072 | tf_op jit(solution)/shard_map/all_to_all | solution.py:523
  207.2 4.8 %all-to-all-done.7.gathered = f32[16,8,128]{2,1,0:T(8,128)S(1)} async-done(((f32[16,8,128]{2,1,0:T(8,128)}), f32[16,8,128]{2,1,0:T(8,128)S(1)}, u32[]{:S(2)}, u32[]{:S(2)}) %all-to-all-start.7) | async-done | bytes 65568 | tf_op jit(solution)/shard_map/all_to_all | solution.py:523
  (95 shorter events, 79.0 us)
Async XLA Ops:
  2.0 14.4 %all-to-all-start = ((bf16[16,16,256]{2,1,0:T(8,128)(2,1)}), bf16[16,16,256]{2,1,0:T(8,128)(2,1)S(1)}, u32[]{:S(2)}, u32[]{:S(2)}) async-start(bf16[16,16,256]{2,1,0:T(8,128)(2,1)} %broadcast_in_dim.29), calls=%async_computation | async-start | bytes 262144 | tf_op jit(solution)/shard_map/all_to_all | solution.py:467
  22.8 5.2 %collective-permute-start.3 = (f32[136,128]{1,0:T(8,128)S(1)}, f32[136,128]{1,0:T(8,128)S(1)}, u32[]{:S(2)}, u32[]{:S(2)}) collective-permute-start(f32[136,128]{1,0:T(8,128)S(1)} %add.92), channel_id=1, source_target_pairs={{0,2},{1,7},{2,4},{3,1},{4,6},{5,3},{6,0},{7,5},{8,10},{9,15},{10,... | collective-permute-start | bytes 208904 | tf_op jit(solution)/shard_map/ppermute | solution.py:457
  26.7 6.1 %collective-permute-start.2 = (f32[136,128]{1,0:T(8,128)S(1)}, f32[136,128]{1,0:T(8,128)S(1)}, u32[]{:S(2)}, u32[]{:S(2)}) collective-permute-start(f32[136,128]{1,0:T(8,128)S(1)} %add.92), channel_id=1, source_target_pairs={{0,6},{1,3},{2,0},{3,5},{4,2},{5,7},{6,4},{7,1},{8,14},{9,11},{10,... | collective-permute-start | bytes 208904 | tf_op jit(solution)/shard_map/ppermute | solution.py:457
  26.7 6.1 %collective-permute-start.1 = (f32[136,128]{1,0:T(8,128)S(1)}, f32[136,128]{1,0:T(8,128)S(1)}, u32[]{:S(2)}, u32[]{:S(2)}) collective-permute-start(f32[136,128]{1,0:T(8,128)S(1)} %add.92), channel_id=1, source_target_pairs={{0,4},{1,5},{2,6},{3,7},{4,0},{5,1},{6,2},{7,3},{8,12},{9,13},{10,... | collective-permute-start | bytes 208904 | tf_op jit(solution)/shard_map/ppermute | solution.py:457
  53.0 3.6 %collective-permute-start.8 = (f32[4,16,256]{2,1,0:T(8,128)S(1)}, f32[4,16,256]{2,1,0:T(8,128)S(1)}, u32[]{:S(2)}, u32[]{:S(2)}) collective-permute-start(f32[4,16,256]{2,1,0:T(8,128)S(1)} %add.96), channel_id=1, source_target_pairs={{0,2},{1,7},{2,4},{3,1},{4,6},{5,3},{6,0},{7,5},{8,10},{9,15},{10,... | collective-permute-start | bytes 196616 | tf_op jit(solution)/shard_map/ppermute | solution.py:457
  55.3 5.0 %collective-permute-start.7 = (f32[4,16,256]{2,1,0:T(8,128)S(1)}, f32[4,16,256]{2,1,0:T(8,128)S(1)}, u32[]{:S(2)}, u32[]{:S(2)}) collective-permute-start(f32[4,16,256]{2,1,0:T(8,128)S(1)} %add.96), channel_id=1, source_target_pairs={{0,6},{1,3},{2,0},{3,5},{4,2},{5,7},{6,4},{7,1},{8,14},{9,11},{10,... | collective-permute-start | bytes 196616 | tf_op jit(solution)/shard_map/ppermute | solution.py:457
  55.3 5.0 %collective-permute-start.6 = (f32[4,16,256]{2,1,0:T(8,128)S(1)}, f32[4,16,256]{2,1,0:T(8,128)S(1)}, u32[]{:S(2)}, u32[]{:S(2)}) collective-permute-start(f32[4,16,256]{2,1,0:T(8,128)S(1)} %add.96), channel_id=1, source_target_pairs={{0,4},{1,5},{2,6},{3,7},{4,0},{5,1},{6,2},{7,3},{8,12},{9,13},{10,... | collective-permute-start | bytes 196616 | tf_op jit(solution)/shard_map/ppermute | solution.py:457
  80.5 3.2 %collective-permute-start.13 = (f32[4,16,256]{2,1,0:T(8,128)S(1)}, f32[4,16,256]{2,1,0:T(8,128)S(1)}, u32[]{:S(2)}, u32[]{:S(2)}) collective-permute-start(f32[4,16,256]{2,1,0:T(8,128)S(1)} %add.100), channel_id=1, source_target_pairs={{0,2},{1,7},{2,4},{3,1},{4,6},{5,3},{6,0},{7,5},{8,10},{9,15},{10,... | collective-permute-start | bytes 196616 | tf_op jit(solution)/shard_map/ppermute | solution.py:457
  82.1 5.0 %collective-permute-start.12 = (f32[4,16,256]{2,1,0:T(8,128)S(1)}, f32[4,16,256]{2,1,0:T(8,128)S(1)}, u32[]{:S(2)}, u32[]{:S(2)}) collective-permute-start(f32[4,16,256]{2,1,0:T(8,128)S(1)} %add.100), channel_id=1, source_target_pairs={{0,6},{1,3},{2,0},{3,5},{4,2},{5,7},{6,4},{7,1},{8,14},{9,11},{10,... | collective-permute-start | bytes 196616 | tf_op jit(solution)/shard_map/ppermute | solution.py:457
  82.2 5.0 %collective-permute-start.11 = (f32[4,16,256]{2,1,0:T(8,128)S(1)}, f32[4,16,256]{2,1,0:T(8,128)S(1)}, u32[]{:S(2)}, u32[]{:S(2)}) collective-permute-start(f32[4,16,256]{2,1,0:T(8,128)S(1)} %add.100), channel_id=1, source_target_pairs={{0,4},{1,5},{2,6},{3,7},{4,0},{5,1},{6,2},{7,3},{8,12},{9,13},{10,... | collective-permute-start | bytes 196616 | tf_op jit(solution)/shard_map/ppermute | solution.py:457
  87.2 3.7 %collective-permute-start.14 = (f32[4,16,256]{2,1,0:T(8,128)S(1)}, f32[4,16,256]{2,1,0:T(8,128)S(1)}, u32[]{:S(2)}, u32[]{:S(2)}) collective-permute-start(f32[4,16,256]{2,1,0:T(8,128)S(1)} %add_add_fusion.5.z_mine.refs_5_), channel_id=1, source_target_pairs={{0,1},{1,0},{2,3},{3,2},{4,5},{5,4},{6,7},{7,6},{8,9},{9,8},{10,11... | collective-permute-start | bytes 196616 | tf_op jit(solution)/shard_map/ppermute | solution.py:459
  109.0 5.8 %collective-permute-start.17 = (f32[4,16,256]{2,1,0:T(8,128)S(1)}, f32[4,16,256]{2,1,0:T(8,128)S(1)}, u32[]{:S(2)}, u32[]{:S(2)}) collective-permute-start(f32[4,16,256]{2,1,0:T(8,128)S(1)} %add.104), channel_id=1, source_target_pairs={{0,6},{1,3},{2,0},{3,5},{4,2},{5,7},{6,4},{7,1},{8,14},{9,11},{10,... | collective-permute-start | bytes 196616 | tf_op jit(solution)/shard_map/ppermute | solution.py:457
  109.6 5.3 %collective-permute-start.16 = (f32[4,16,256]{2,1,0:T(8,128)S(1)}, f32[4,16,256]{2,1,0:T(8,128)S(1)}, u32[]{:S(2)}, u32[]{:S(2)}) collective-permute-start(f32[4,16,256]{2,1,0:T(8,128)S(1)} %add.104), channel_id=1, source_target_pairs={{0,4},{1,5},{2,6},{3,7},{4,0},{5,1},{6,2},{7,3},{8,12},{9,13},{10,... | collective-permute-start | bytes 196616 | tf_op jit(solution)/shard_map/ppermute | solution.py:457
  114.9 3.6 %collective-permute-start.19 = (f32[4,16,256]{2,1,0:T(8,128)S(1)}, f32[4,16,256]{2,1,0:T(8,128)S(1)}, u32[]{:S(2)}, u32[]{:S(2)}) collective-permute-start(f32[4,16,256]{2,1,0:T(8,128)S(1)} %add_add_fusion.4.z_mine.refs_5_), channel_id=1, source_target_pairs={{0,1},{1,0},{2,3},{3,2},{4,5},{5,4},{6,7},{7,6},{8,9},{9,8},{10,11... | collective-permute-start | bytes 196616 | tf_op jit(solution)/shard_map/ppermute | solution.py:459
  136.5 6.0 %collective-permute-start.22 = (f32[4,16,256]{2,1,0:T(8,128)S(1)}, f32[4,16,256]{2,1,0:T(8,128)S(1)}, u32[]{:S(2)}, u32[]{:S(2)}) collective-permute-start(f32[4,16,256]{2,1,0:T(8,128)S(1)} %add.108), channel_id=1, source_target_pairs={{0,6},{1,3},{2,0},{3,5},{4,2},{5,7},{6,4},{7,1},{8,14},{9,11},{10,... | collective-permute-start | bytes 196616 | tf_op jit(solution)/shard_map/ppermute | solution.py:457
  137.2 5.4 %collective-permute-start.21 = (f32[4,16,256]{2,1,0:T(8,128)S(1)}, f32[4,16,256]{2,1,0:T(8,128)S(1)}, u32[]{:S(2)}, u32[]{:S(2)}) collective-permute-start(f32[4,16,256]{2,1,0:T(8,128)S(1)} %add.108), channel_id=1, source_target_pairs={{0,4},{1,5},{2,6},{3,7},{4,0},{5,1},{6,2},{7,3},{8,12},{9,13},{10,... | collective-permute-start | bytes 196616 | tf_op jit(solution)/shard_map/ppermute | solution.py:457
  142.5 3.5 %collective-permute-start.24 = (f32[4,16,256]{2,1,0:T(8,128)S(1)}, f32[4,16,256]{2,1,0:T(8,128)S(1)}, u32[]{:S(2)}, u32[]{:S(2)}) collective-permute-start(f32[4,16,256]{2,1,0:T(8,128)S(1)} %add_add_fusion.3.z_mine.refs_5_), channel_id=1, source_target_pairs={{0,1},{1,0},{2,3},{3,2},{4,5},{5,4},{6,7},{7,6},{8,9},{9,8},{10,11... | collective-permute-start | bytes 196616 | tf_op jit(solution)/shard_map/ppermute | solution.py:459
  164.1 6.0 %collective-permute-start.27 = (f32[4,16,256]{2,1,0:T(8,128)S(1)}, f32[4,16,256]{2,1,0:T(8,128)S(1)}, u32[]{:S(2)}, u32[]{:S(2)}) collective-permute-start(f32[4,16,256]{2,1,0:T(8,128)S(1)} %add.112), channel_id=1, source_target_pairs={{0,6},{1,3},{2,0},{3,5},{4,2},{5,7},{6,4},{7,1},{8,14},{9,11},{10,... | collective-permute-start | bytes 196616 | tf_op jit(solution)/shard_map/ppermute | solution.py:457
  164.7 5.3 %collective-permute-start.26 = (f32[4,16,256]{2,1,0:T(8,128)S(1)}, f32[4,16,256]{2,1,0:T(8,128)S(1)}, u32[]{:S(2)}, u32[]{:S(2)}) collective-permute-start(f32[4,16,256]{2,1,0:T(8,128)S(1)} %add.112), channel_id=1, source_target_pairs={{0,4},{1,5},{2,6},{3,7},{4,0},{5,1},{6,2},{7,3},{8,12},{9,13},{10,... | collective-permute-start | bytes 196616 | tf_op jit(solution)/shard_map/ppermute | solution.py:457
  170.1 3.5 %collective-permute-start.29 = (f32[4,16,256]{2,1,0:T(8,128)S(1)}, f32[4,16,256]{2,1,0:T(8,128)S(1)}, u32[]{:S(2)}, u32[]{:S(2)}) collective-permute-start(f32[4,16,256]{2,1,0:T(8,128)S(1)} %add_add_fusion.2.z_mine), channel_id=1, source_target_pairs={{0,1},{1,0},{2,3},{3,2},{4,5},{5,4},{6,7},{7,6},{8,9},{9,8},{10,11... | collective-permute-start | bytes 196616 | tf_op jit(solution)/shard_map/ppermute | solution.py:459
  191.7 6.0 %collective-permute-start.32 = (f32[4,16,256]{2,1,0:T(8,128)S(1)}, f32[4,16,256]{2,1,0:T(8,128)S(1)}, u32[]{:S(2)}, u32[]{:S(2)}) collective-permute-start(f32[4,16,256]{2,1,0:T(8,128)S(1)} %add.116), channel_id=1, source_target_pairs={{0,6},{1,3},{2,0},{3,5},{4,2},{5,7},{6,4},{7,1},{8,14},{9,11},{10,... | collective-permute-start | bytes 196616 | tf_op jit(solution)/shard_map/ppermute | solution.py:457
  192.3 5.3 %collective-permute-start.31 = (f32[4,16,256]{2,1,0:T(8,128)S(1)}, f32[4,16,256]{2,1,0:T(8,128)S(1)}, u32[]{:S(2)}, u32[]{:S(2)}) collective-permute-start(f32[4,16,256]{2,1,0:T(8,128)S(1)} %add.116), channel_id=1, source_target_pairs={{0,4},{1,5},{2,6},{3,7},{4,0},{5,1},{6,2},{7,3},{8,12},{9,13},{10,... | collective-permute-start | bytes 196616 | tf_op jit(solution)/shard_map/ppermute | solution.py:457
  197.7 3.5 %collective-permute-start.34 = (f32[4,16,256]{2,1,0:T(8,128)S(1)}, f32[4,16,256]{2,1,0:T(8,128)S(1)}, u32[]{:S(2)}, u32[]{:S(2)}) collective-permute-start(f32[4,16,256]{2,1,0:T(8,128)S(1)} %add_add_fusion.1.refs_12_.refs_0_), channel_id=1, source_target_pairs={{0,1},{1,0},{2,3},{3,2},{4,5},{5,4},{6,7},{7,6},{8,9},{9,8},{10,11... | collective-permute-start | bytes 196616 | tf_op jit(solution)/shard_map/ppermute | solution.py:459
  202.0 9.9 %all-to-all-start.7 = ((f32[16,8,128]{2,1,0:T(8,128)}), f32[16,8,128]{2,1,0:T(8,128)S(1)}, u32[]{:S(2)}, u32[]{:S(2)}) async-start(f32[16,8,128]{2,1,0:T(8,128)} %shard_map.136), calls=%async_computation.7 | async-start | bytes 131072 | tf_op jit(solution)/shard_map/all_to_all | solution.py:523
  (14 other events, 55.4 us)

commit v6 on v5

--- a/solution.py
+++ b/solution.py
@@ -240,8 +240,8 @@
 
 
 def direct_kernel(states_n, step, table, gathered, tiles, energies, z_mine, z_other, *refs):
-    p_mine, p_other, qn_mine, qn_other, state_out, xs, acc = refs[-7:]
-    extra = list(refs[:-7])
+    p_mine, p_other, state_out, xs, acc = refs[-5:]
+    extra = list(refs[:-5])
     groups = gathered.shape[0]
     half = p_mine.shape[0]
     slots = tiles.shape[0]
@@ -270,40 +270,43 @@
         centre = column(1) * (1.0 / states_n)
         beta = jnp.sqrt(norm + 1e-30)
         scale = 1.0 / beta
-        qn = [z[0] * scale, z[1] * scale]
         local = (energies[...] - centre) * own + back
     else:
         state = extra[0][...]
-        q = (extra[1][...], extra[2][...])
         centre = state[:, CENTRE : CENTRE + 1]
         size = column(3 + step)
         alpha = column(1) / size
         square = norm - alpha * alpha * size
-        qn = [z[0] - alpha * q[0], z[1] - alpha * q[1]]
         local = (energies[...] - centre) * own + back - alpha * own
         lanes.update({ALPHA: alpha, TOTAL: column(3)})
         lanes.update({GRAM + i: column(4 + i) for i in range(step)})
         if step > 1:
-            old = (extra[3][...], extra[4][...])
-            z_old = extra[5]
+            z_old = extra[1]
             size_old = state[:, GRAM + step - 2 : GRAM + step - 1]
             gamma = column(2) / size_old
             square = square - gamma * gamma * size_old
-            qn = [a - gamma * b for a, b in zip(qn, old)]
             local = local - gamma * z_old[table[PLACE_Z]]
             lanes[GAMMA] = gamma
         beta_square = jnp.maximum(square, FLOOR * FLOOR * norm) + 1e-30
         beta = jnp.sqrt(beta_square)
         scale = 1.0 / beta
-        qn = [a * scale for a in qn]
         lanes[NEXT] = jnp.maximum(square, 0.0) / beta_square
     lanes.update({BETA: beta, CENTRE: centre})
     state_out[...] = lanes_of(lanes, state_out.shape)
-    qn_mine[...] = qn[0]
-    qn_other[...] = qn[1]
     acc[table[PLACE_Z]] += local
     p_mine[...] = acc[:half] * scale
     p_other[...] = acc[half:] * scale
+
+
+def basis_kernel(state, z_mine, z_other, *refs):
+    qn = load_slab(z_mine, z_other)
+    q, out = refs[:-2], refs[-2:]
+    full = state[...]
+    for i, lane in enumerate((ALPHA, GAMMA)[: len(q) // 2]):
+        qn = [a - full[:, lane : lane + 1] * b[...] for a, b in zip(qn, q[2 * i : 2 * i + 2])]
+    scale = 1.0 / full[:, BETA : BETA + 1]
+    for target, a in zip(out, qn):
+        target[...] = a * scale
 
 
 def apply_h(coefs, alphas, betas, gammas, shift):
@@ -504,18 +507,19 @@
         gathered = lax.all_to_all(payload, "row", 0, 0, tiled=True)
         extra = []
         if step > 0:
-            extra = [states[-1], *basis[-1]]
+            extra = [states[-1]]
         if step > 1:
-            extra += [*basis[-2], vectors[-2]]
-        p_mine, p_other, qn_mine, qn_other, state = call(
+            extra += [vectors[-2]]
+        p_mine, p_other, state = call(
             functools.partial(direct_kernel, float(rows_n * cols_n * width), step),
-            (block, block, block, block, small),
+            (block, block, small),
             1,
             5 + len(extra),
             [pltpu.VMEM((rows_n + 1, 2 * NV, width), BF16), pltpu.VMEM((cols_n, NV, width), F32)],
         )(table, gathered, h_flipped, diagonal, *z, *extra)
         states.append(state)
-        basis.append((qn_mine, qn_other))
+        before = [array for q in basis[:-3:-1] for array in q]
+        basis.append(call(basis_kernel, (block, block), 0, 3 + len(before))(state, *z, *before))
         z = group_sum(p_mine, p_other)
 
     pairs = [array for q in basis for array in q]

time: 214 us -> 214 us (level)
  no operation moved by 1% of the time
where the time goes in v6:
time: 214 us; the launch traced here: 213 us
  blocking collectives  65.7 us (31%)
  starting transfers between devices  61.9 us (29%)
  waiting for transfers between devices  49.8 us (23%)
  Pallas kernels  28.9 us (14%)
  other arithmetic  2.22 us (1%)
  between operations  2.18 us (1%)
    all_to_all x6, blocking collectives, body(): gathered = lax.all_to_all(payload, 'row', 0, 0, tiled=True)  65.7 us
    ppermute x21, waiting for transfers between devices, group_sum(): moved.append(lax.ppermute(q, 'col', ring(d)))  31.1 us
    ppermute x21, starting transfers between devices, group_sum(): moved.append(lax.ppermute(q, 'col', ring(d)))  20.4 us
    ppermute x7, starting transfers between devices, group_sum(): return (mine, lax.ppermute(mine, 'col', pair))  16 us
    ppermute x7, starting transfers between devices, group_sum(): q = p_mine + lax.ppermute(p_other, 'col', pair)  14.5 us
    pallas_call x6, Pallas kernels, body(): call(back_kernel, jax.ShapeDtypeStruct((rows_n, 2 * NV * width // LANES +...  9.56 us
    pallas_call x6, Pallas kernels, body(): call(functools.partial(direct_kernel, float(rows_n * cols_n * width), ste...  9.31 us
    all_to_all x1, starting transfers between devices, body(): gathered = lax.all_to_all(spread, 'row', 0, 0, tiled=True)  7.57 us
  transfers between devices with their start and end apart: 37, of which 29 were waited for; matrix products, arithmetic and copies ran while one was open for 1% of the time, Pallas kernels for 2%

profile of v6, /device:TPU:1, one launch (start us, length us, event | category | flops | bytes accessed | tf_op | source)
XLA Modules:
  0.0 212.9 jit_solution(8220461438330480060)
XLA Ops:
  2.0 7.6 %all-to-all-start = ((bf16[16,16,256]{2,1,0:T(8,128)(2,1)}), bf16[16,16,256]{2,1,0:T(8,128)(2,1)S(1)}, u32[]{:S(2)}, u32[]{:S(2)}) async-start(bf16[16,16,256]{2,1,0:T(8,128)(2,1)} %broadcast_in_dim.29), calls=%async_computation | async-start | bytes 262144 | tf_op jit(solution)/shard_map/all_to_all | solution.py:470
  13.6 2.8 %all-to-all-done.gathered = bf16[16,16,256]{2,1,0:T(8,128)(2,1)S(1)} async-done(((bf16[16,16,256]{2,1,0:T(8,128)(2,1)}), bf16[16,16,256]{2,1,0:T(8,128)(2,1)S(1)}, u32[]{:S(2)}, u32[]{:S(2)}) %all-to-all-start) | async-done | bytes 131104 | tf_op jit(solution)/shard_map/all_to_all | solution.py:470
  16.4 3.5 %shard_map.121 = (f32[136,128]{1,0:T(8,128)S(1)}, f32[136,128]{1,0:T(8,128)S(1)}) custom-call(s32[200]{0:T(256)S(1)} %concatenate.3.table, bf16[16,16,256]{2,1,0:T(8,128)(2,1)S(1)} %all-to-all-done.gathered, f32[1,256]{1,0:T(1,128)} %bitcast.6, bf16[32,256,256]{2,1,0:T(8,128)(2,1)} %tiles_hbm.1), custom_call_target="tpu_custom_call" | custom-call | tf_op jit(solution)/shard_map/pallas_call | solution.py:471
  22.9 3.8 %collective-permute-start.3 = (f32[136,128]{1,0:T(8,128)S(1)}, f32[136,128]{1,0:T(8,128)S(1)}, u32[]{:S(2)}, u32[]{:S(2)}) collective-permute-start(f32[136,128]{1,0:T(8,128)S(1)} %add.92), channel_id=1, source_target_pairs={{0,2},{1,7},{2,4},{3,1},{4,6},{5,3},{6,0},{7,5},{8,10},{9,15},{10,... | collective-permute-start | bytes 208904 | tf_op jit(solution)/shard_map/ppermute | solution.py:460
  28.1 4.8 %collective-permute-done.2 = f32[136,128]{1,0:T(8,128)S(1)} collective-permute-done((f32[136,128]{1,0:T(8,128)S(1)}, f32[136,128]{1,0:T(8,128)S(1)}, u32[]{:S(2)}, u32[]{:S(2)}) %collective-permute-start.2) | collective-permute-done | bytes 69664 | tf_op jit(solution)/shard_map/ppermute | solution.py:460
  37.5 11.1 %all_to_all.40.gathered = s16[16,72,128]{2,1,0:T(8,128)(2,1)S(1)} all-to-all(s16[16,72,128]{2,1,0:T(8,128)(2,1)S(1)} %shard_map.123), channel_id=1, replica_groups=mesh['row'=16,'col'=8] {'row'}, dimensions={0} | all-to-all | bytes 589824 | tf_op jit(solution)/shard_map/all_to_all | solution.py:507
  56.6 3.7 %collective-permute-done.7 = f32[4,16,256]{2,1,0:T(8,128)S(1)} collective-permute-done((f32[4,16,256]{2,1,0:T(8,128)S(1)}, f32[4,16,256]{2,1,0:T(8,128)S(1)}, u32[]{:S(2)}, u32[]{:S(2)}) %collective-permute-start.7) | collective-permute-done | bytes 65568 | tf_op jit(solution)/shard_map/ppermute | solution.py:460
  65.0 10.9 %all_to_all.41.gathered = s16[16,72,128]{2,1,0:T(8,128)(2,1)S(1)} all-to-all(s16[16,72,128]{2,1,0:T(8,128)(2,1)S(1)} %shard_map.126), channel_id=1, replica_groups=mesh['row'=16,'col'=8] {'row'}, dimensions={0} | all-to-all | bytes 589824 | tf_op jit(solution)/shard_map/all_to_all | solution.py:507
  83.7 3.5 %collective-permute-done.12 = f32[4,16,256]{2,1,0:T(8,128)S(1)} collective-permute-done((f32[4,16,256]{2,1,0:T(8,128)S(1)}, f32[4,16,256]{2,1,0:T(8,128)S(1)}, u32[]{:S(2)}, u32[]{:S(2)}) %collective-permute-start.12) | collective-permute-done | bytes 65568 | tf_op jit(solution)/shard_map/ppermute | solution.py:460
  87.2 2.8 %collective-permute-start.14 = (f32[4,16,256]{2,1,0:T(8,128)S(1)}, f32[4,16,256]{2,1,0:T(8,128)S(1)}, u32[]{:S(2)}, u32[]{:S(2)}) collective-permute-start(f32[4,16,256]{2,1,0:T(8,128)S(1)} %add_add_fusion.5.z_mine.refs_1_), channel_id=1, source_target_pairs={{0,1},{1,0},{2,3},{3,2},{4,5},{5,4},{6,7},{7,6},{8,9},{9,8},{10,11... | collective-permute-start | bytes 196616 | tf_op jit(solution)/shard_map/ppermute | solution.py:462
  92.5 10.9 %all_to_all.42.gathered = s16[16,72,128]{2,1,0:T(8,128)(2,1)S(1)} all-to-all(s16[16,72,128]{2,1,0:T(8,128)(2,1)S(1)} %shard_map.129), channel_id=1, replica_groups=mesh['row'=16,'col'=8] {'row'}, dimensions={0} | all-to-all | bytes 589824 | tf_op jit(solution)/shard_map/all_to_all | solution.py:507
  111.3 3.6 %collective-permute-done.17 = f32[4,16,256]{2,1,0:T(8,128)S(1)} collective-permute-done((f32[4,16,256]{2,1,0:T(8,128)S(1)}, f32[4,16,256]{2,1,0:T(8,128)S(1)}, u32[]{:S(2)}, u32[]{:S(2)}) %collective-permute-start.17) | collective-permute-done | bytes 65568 | tf_op jit(solution)/shard_map/ppermute | solution.py:460
  114.9 2.7 %collective-permute-start.19 = (f32[4,16,256]{2,1,0:T(8,128)S(1)}, f32[4,16,256]{2,1,0:T(8,128)S(1)}, u32[]{:S(2)}, u32[]{:S(2)}) collective-permute-start(f32[4,16,256]{2,1,0:T(8,128)S(1)} %add_add_fusion.4.z_mine.refs_1_), channel_id=1, source_target_pairs={{0,1},{1,0},{2,3},{3,2},{4,5},{5,4},{6,7},{7,6},{8,9},{9,8},{10,11... | collective-permute-start | bytes 196616 | tf_op jit(solution)/shard_map/ppermute | solution.py:462
  120.1 10.9 %all_to_all.43.gathered = s16[16,72,128]{2,1,0:T(8,128)(2,1)S(1)} all-to-all(s16[16,72,128]{2,1,0:T(8,128)(2,1)S(1)} %shard_map.132), channel_id=1, replica_groups=mesh['row'=16,'col'=8] {'row'}, dimensions={0} | all-to-all | bytes 589824 | tf_op jit(solution)/shard_map/all_to_all | solution.py:507
  138.8 3.7 %collective-permute-done.22 = f32[4,16,256]{2,1,0:T(8,128)S(1)} collective-permute-done((f32[4,16,256]{2,1,0:T(8,128)S(1)}, f32[4,16,256]{2,1,0:T(8,128)S(1)}, u32[]{:S(2)}, u32[]{:S(2)}) %collective-permute-start.22) | collective-permute-done | bytes 65568 | tf_op jit(solution)/shard_map/ppermute | solution.py:460
  142.5 2.6 %collective-permute-start.24 = (f32[4,16,256]{2,1,0:T(8,128)S(1)}, f32[4,16,256]{2,1,0:T(8,128)S(1)}, u32[]{:S(2)}, u32[]{:S(2)}) collective-permute-start(f32[4,16,256]{2,1,0:T(8,128)S(1)} %add_add_fusion.3.z_mine.refs_1_), channel_id=1, source_target_pairs={{0,1},{1,0},{2,3},{3,2},{4,5},{5,4},{6,7},{7,6},{8,9},{9,8},{10,11... | collective-permute-start | bytes 196616 | tf_op jit(solution)/shard_map/ppermute | solution.py:462
  147.7 10.9 %all_to_all.44.gathered = s16[16,72,128]{2,1,0:T(8,128)(2,1)S(1)} all-to-all(s16[16,72,128]{2,1,0:T(8,128)(2,1)S(1)} %shard_map.135), channel_id=1, replica_groups=mesh['row'=16,'col'=8] {'row'}, dimensions={0} | all-to-all | bytes 589824 | tf_op jit(solution)/shard_map/all_to_all | solution.py:507
  166.4 3.7 %collective-permute-done.27 = f32[4,16,256]{2,1,0:T(8,128)S(1)} collective-permute-done((f32[4,16,256]{2,1,0:T(8,128)S(1)}, f32[4,16,256]{2,1,0:T(8,128)S(1)}, u32[]{:S(2)}, u32[]{:S(2)}) %collective-permute-start.27) | collective-permute-done | bytes 65568 | tf_op jit(solution)/shard_map/ppermute | solution.py:460
  170.1 2.6 %collective-permute-start.29 = (f32[4,16,256]{2,1,0:T(8,128)S(1)}, f32[4,16,256]{2,1,0:T(8,128)S(1)}, u32[]{:S(2)}, u32[]{:S(2)}) collective-permute-start(f32[4,16,256]{2,1,0:T(8,128)S(1)} %add_add_fusion.2.z_mine), channel_id=1, source_target_pairs={{0,1},{1,0},{2,3},{3,2},{4,5},{5,4},{6,7},{7,6},{8,9},{9,8},{10,11... | collective-permute-start | bytes 196616 | tf_op jit(solution)/shard_map/ppermute | solution.py:462
  175.2 10.9 %all_to_all.45.gathered = s16[16,72,128]{2,1,0:T(8,128)(2,1)S(1)} all-to-all(s16[16,72,128]{2,1,0:T(8,128)(2,1)S(1)} %shard_map.138), channel_id=1, replica_groups=mesh['row'=16,'col'=8] {'row'}, dimensions={0} | all-to-all | bytes 589824 | tf_op jit(solution)/shard_map/all_to_all | solution.py:507
  193.9 3.7 %collective-permute-done.32 = f32[4,16,256]{2,1,0:T(8,128)S(1)} collective-permute-done((f32[4,16,256]{2,1,0:T(8,128)S(1)}, f32[4,16,256]{2,1,0:T(8,128)S(1)}, u32[]{:S(2)}, u32[]{:S(2)}) %collective-permute-start.32) | collective-permute-done | bytes 65568 | tf_op jit(solution)/shard_map/ppermute | solution.py:460
  197.7 2.6 %collective-permute-start.34 = (f32[4,16,256]{2,1,0:T(8,128)S(1)}, f32[4,16,256]{2,1,0:T(8,128)S(1)}, u32[]{:S(2)}, u32[]{:S(2)}) collective-permute-start(f32[4,16,256]{2,1,0:T(8,128)S(1)} %add_add_fusion.1.refs_12_.refs_0_), channel_id=1, source_target_pairs={{0,1},{1,0},{2,3},{3,2},{4,5},{5,4},{6,7},{7,6},{8,9},{9,8},{10,11... | collective-permute-start | bytes 196616 | tf_op jit(solution)/shard_map/ppermute | solution.py:462
  202.0 3.5 %all-to-all-start.7 = ((f32[16,8,128]{2,1,0:T(8,128)}), f32[16,8,128]{2,1,0:T(8,128)S(1)}, u32[]{:S(2)}, u32[]{:S(2)}) async-start(f32[16,8,128]{2,1,0:T(8,128)} %shard_map.142), calls=%async_computation.7 | async-start | bytes 131072 | tf_op jit(solution)/shard_map/all_to_all | solution.py:527
  207.2 4.8 %all-to-all-done.7.gathered = f32[16,8,128]{2,1,0:T(8,128)S(1)} async-done(((f32[16,8,128]{2,1,0:T(8,128)}), f32[16,8,128]{2,1,0:T(8,128)S(1)}, u32[]{:S(2)}, u32[]{:S(2)}) %all-to-all-start.7) | async-done | bytes 65568 | tf_op jit(solution)/shard_map/all_to_all | solution.py:527
  (101 shorter events, 79.0 us)
Async XLA Ops:
  2.0 14.4 %all-to-all-start = ((bf16[16,16,256]{2,1,0:T(8,128)(2,1)}), bf16[16,16,256]{2,1,0:T(8,128)(2,1)S(1)}, u32[]{:S(2)}, u32[]{:S(2)}) async-start(bf16[16,16,256]{2,1,0:T(8,128)(2,1)} %broadcast_in_dim.29), calls=%async_computation | async-start | bytes 262144 | tf_op jit(solution)/shard_map/all_to_all | solution.py:470
  22.9 5.2 %collective-permute-start.3 = (f32[136,128]{1,0:T(8,128)S(1)}, f32[136,128]{1,0:T(8,128)S(1)}, u32[]{:S(2)}, u32[]{:S(2)}) collective-permute-start(f32[136,128]{1,0:T(8,128)S(1)} %add.92), channel_id=1, source_target_pairs={{0,2},{1,7},{2,4},{3,1},{4,6},{5,3},{6,0},{7,5},{8,10},{9,15},{10,... | collective-permute-start | bytes 208904 | tf_op jit(solution)/shard_map/ppermute | solution.py:460
  26.7 6.1 %collective-permute-start.2 = (f32[136,128]{1,0:T(8,128)S(1)}, f32[136,128]{1,0:T(8,128)S(1)}, u32[]{:S(2)}, u32[]{:S(2)}) collective-permute-start(f32[136,128]{1,0:T(8,128)S(1)} %add.92), channel_id=1, source_target_pairs={{0,6},{1,3},{2,0},{3,5},{4,2},{5,7},{6,4},{7,1},{8,14},{9,11},{10,... | collective-permute-start | bytes 208904 | tf_op jit(solution)/shard_map/ppermute | solution.py:460
  26.7 6.1 %collective-permute-start.1 = (f32[136,128]{1,0:T(8,128)S(1)}, f32[136,128]{1,0:T(8,128)S(1)}, u32[]{:S(2)}, u32[]{:S(2)}) collective-permute-start(f32[136,128]{1,0:T(8,128)S(1)} %add.92), channel_id=1, source_target_pairs={{0,4},{1,5},{2,6},{3,7},{4,0},{5,1},{6,2},{7,3},{8,12},{9,13},{10,... | collective-permute-start | bytes 208904 | tf_op jit(solution)/shard_map/ppermute | solution.py:460
  53.0 3.6 %collective-permute-start.8 = (f32[4,16,256]{2,1,0:T(8,128)S(1)}, f32[4,16,256]{2,1,0:T(8,128)S(1)}, u32[]{:S(2)}, u32[]{:S(2)}) collective-permute-start(f32[4,16,256]{2,1,0:T(8,128)S(1)} %add.96), channel_id=1, source_target_pairs={{0,2},{1,7},{2,4},{3,1},{4,6},{5,3},{6,0},{7,5},{8,10},{9,15},{10,... | collective-permute-start | bytes 196616 | tf_op jit(solution)/shard_map/ppermute | solution.py:460
  55.3 5.0 %collective-permute-start.7 = (f32[4,16,256]{2,1,0:T(8,128)S(1)}, f32[4,16,256]{2,1,0:T(8,128)S(1)}, u32[]{:S(2)}, u32[]{:S(2)}) collective-permute-start(f32[4,16,256]{2,1,0:T(8,128)S(1)} %add.96), channel_id=1, source_target_pairs={{0,6},{1,3},{2,0},{3,5},{4,2},{5,7},{6,4},{7,1},{8,14},{9,11},{10,... | collective-permute-start | bytes 196616 | tf_op jit(solution)/shard_map/ppermute | solution.py:460
  55.3 5.0 %collective-permute-start.6 = (f32[4,16,256]{2,1,0:T(8,128)S(1)}, f32[4,16,256]{2,1,0:T(8,128)S(1)}, u32[]{:S(2)}, u32[]{:S(2)}) collective-permute-start(f32[4,16,256]{2,1,0:T(8,128)S(1)} %add.96), channel_id=1, source_target_pairs={{0,4},{1,5},{2,6},{3,7},{4,0},{5,1},{6,2},{7,3},{8,12},{9,13},{10,... | collective-permute-start | bytes 196616 | tf_op jit(solution)/shard_map/ppermute | solution.py:460
  80.5 3.2 %collective-permute-start.13 = (f32[4,16,256]{2,1,0:T(8,128)S(1)}, f32[4,16,256]{2,1,0:T(8,128)S(1)}, u32[]{:S(2)}, u32[]{:S(2)}) collective-permute-start(f32[4,16,256]{2,1,0:T(8,128)S(1)} %add.100), channel_id=1, source_target_pairs={{0,2},{1,7},{2,4},{3,1},{4,6},{5,3},{6,0},{7,5},{8,10},{9,15},{10,... | collective-permute-start | bytes 196616 | tf_op jit(solution)/shard_map/ppermute | solution.py:460
  82.2 5.0 %collective-permute-start.12 = (f32[4,16,256]{2,1,0:T(8,128)S(1)}, f32[4,16,256]{2,1,0:T(8,128)S(1)}, u32[]{:S(2)}, u32[]{:S(2)}) collective-permute-start(f32[4,16,256]{2,1,0:T(8,128)S(1)} %add.100), channel_id=1, source_target_pairs={{0,6},{1,3},{2,0},{3,5},{4,2},{5,7},{6,4},{7,1},{8,14},{9,11},{10,... | collective-permute-start | bytes 196616 | tf_op jit(solution)/shard_map/ppermute | solution.py:460
  82.2 5.0 %collective-permute-start.11 = (f32[4,16,256]{2,1,0:T(8,128)S(1)}, f32[4,16,256]{2,1,0:T(8,128)S(1)}, u32[]{:S(2)}, u32[]{:S(2)}) collective-permute-start(f32[4,16,256]{2,1,0:T(8,128)S(1)} %add.100), channel_id=1, source_target_pairs={{0,4},{1,5},{2,6},{3,7},{4,0},{5,1},{6,2},{7,3},{8,12},{9,13},{10,... | collective-permute-start | bytes 196616 | tf_op jit(solution)/shard_map/ppermute | solution.py:460
  87.2 3.7 %collective-permute-start.14 = (f32[4,16,256]{2,1,0:T(8,128)S(1)}, f32[4,16,256]{2,1,0:T(8,128)S(1)}, u32[]{:S(2)}, u32[]{:S(2)}) collective-permute-start(f32[4,16,256]{2,1,0:T(8,128)S(1)} %add_add_fusion.5.z_mine.refs_1_), channel_id=1, source_target_pairs={{0,1},{1,0},{2,3},{3,2},{4,5},{5,4},{6,7},{7,6},{8,9},{9,8},{10,11... | collective-permute-start | bytes 196616 | tf_op jit(solution)/shard_map/ppermute | solution.py:462
  109.0 5.9 %collective-permute-start.17 = (f32[4,16,256]{2,1,0:T(8,128)S(1)}, f32[4,16,256]{2,1,0:T(8,128)S(1)}, u32[]{:S(2)}, u32[]{:S(2)}) collective-permute-start(f32[4,16,256]{2,1,0:T(8,128)S(1)} %add.104), channel_id=1, source_target_pairs={{0,6},{1,3},{2,0},{3,5},{4,2},{5,7},{6,4},{7,1},{8,14},{9,11},{10,... | collective-permute-start | bytes 196616 | tf_op jit(solution)/shard_map/ppermute | solution.py:460
  109.6 5.3 %collective-permute-start.16 = (f32[4,16,256]{2,1,0:T(8,128)S(1)}, f32[4,16,256]{2,1,0:T(8,128)S(1)}, u32[]{:S(2)}, u32[]{:S(2)}) collective-permute-start(f32[4,16,256]{2,1,0:T(8,128)S(1)} %add.104), channel_id=1, source_target_pairs={{0,4},{1,5},{2,6},{3,7},{4,0},{5,1},{6,2},{7,3},{8,12},{9,13},{10,... | collective-permute-start | bytes 196616 | tf_op jit(solution)/shard_map/ppermute | solution.py:460
  114.9 3.6 %collective-permute-start.19 = (f32[4,16,256]{2,1,0:T(8,128)S(1)}, f32[4,16,256]{2,1,0:T(8,128)S(1)}, u32[]{:S(2)}, u32[]{:S(2)}) collective-permute-start(f32[4,16,256]{2,1,0:T(8,128)S(1)} %add_add_fusion.4.z_mine.refs_1_), channel_id=1, source_target_pairs={{0,1},{1,0},{2,3},{3,2},{4,5},{5,4},{6,7},{7,6},{8,9},{9,8},{10,11... | collective-permute-start | bytes 196616 | tf_op jit(solution)/shard_map/ppermute | solution.py:462
  136.5 6.0 %collective-permute-start.22 = (f32[4,16,256]{2,1,0:T(8,128)S(1)}, f32[4,16,256]{2,1,0:T(8,128)S(1)}, u32[]{:S(2)}, u32[]{:S(2)}) collective-permute-start(f32[4,16,256]{2,1,0:T(8,128)S(1)} %add.108), channel_id=1, source_target_pairs={{0,6},{1,3},{2,0},{3,5},{4,2},{5,7},{6,4},{7,1},{8,14},{9,11},{10,... | collective-permute-start | bytes 196616 | tf_op jit(solution)/shard_map/ppermute | solution.py:460
  137.2 5.3 %collective-permute-start.21 = (f32[4,16,256]{2,1,0:T(8,128)S(1)}, f32[4,16,256]{2,1,0:T(8,128)S(1)}, u32[]{:S(2)}, u32[]{:S(2)}) collective-permute-start(f32[4,16,256]{2,1,0:T(8,128)S(1)} %add.108), channel_id=1, source_target_pairs={{0,4},{1,5},{2,6},{3,7},{4,0},{5,1},{6,2},{7,3},{8,12},{9,13},{10,... | collective-permute-start | bytes 196616 | tf_op jit(solution)/shard_map/ppermute | solution.py:460
  142.5 3.5 %collective-permute-start.24 = (f32[4,16,256]{2,1,0:T(8,128)S(1)}, f32[4,16,256]{2,1,0:T(8,128)S(1)}, u32[]{:S(2)}, u32[]{:S(2)}) collective-permute-start(f32[4,16,256]{2,1,0:T(8,128)S(1)} %add_add_fusion.3.z_mine.refs_1_), channel_id=1, source_target_pairs={{0,1},{1,0},{2,3},{3,2},{4,5},{5,4},{6,7},{7,6},{8,9},{9,8},{10,11... | collective-permute-start | bytes 196616 | tf_op jit(solution)/shard_map/ppermute | solution.py:462
  164.1 6.0 %collective-permute-start.27 = (f32[4,16,256]{2,1,0:T(8,128)S(1)}, f32[4,16,256]{2,1,0:T(8,128)S(1)}, u32[]{:S(2)}, u32[]{:S(2)}) collective-permute-start(f32[4,16,256]{2,1,0:T(8,128)S(1)} %add.112), channel_id=1, source_target_pairs={{0,6},{1,3},{2,0},{3,5},{4,2},{5,7},{6,4},{7,1},{8,14},{9,11},{10,... | collective-permute-start | bytes 196616 | tf_op jit(solution)/shard_map/ppermute | solution.py:460
  164.7 5.3 %collective-permute-start.26 = (f32[4,16,256]{2,1,0:T(8,128)S(1)}, f32[4,16,256]{2,1,0:T(8,128)S(1)}, u32[]{:S(2)}, u32[]{:S(2)}) collective-permute-start(f32[4,16,256]{2,1,0:T(8,128)S(1)} %add.112), channel_id=1, source_target_pairs={{0,4},{1,5},{2,6},{3,7},{4,0},{5,1},{6,2},{7,3},{8,12},{9,13},{10,... | collective-permute-start | bytes 196616 | tf_op jit(solution)/shard_map/ppermute | solution.py:460
  170.1 3.5 %collective-permute-start.29 = (f32[4,16,256]{2,1,0:T(8,128)S(1)}, f32[4,16,256]{2,1,0:T(8,128)S(1)}, u32[]{:S(2)}, u32[]{:S(2)}) collective-permute-start(f32[4,16,256]{2,1,0:T(8,128)S(1)} %add_add_fusion.2.z_mine), channel_id=1, source_target_pairs={{0,1},{1,0},{2,3},{3,2},{4,5},{5,4},{6,7},{7,6},{8,9},{9,8},{10,11... | collective-permute-start | bytes 196616 | tf_op jit(solution)/shard_map/ppermute | solution.py:462
  191.7 6.0 %collective-permute-start.32 = (f32[4,16,256]{2,1,0:T(8,128)S(1)}, f32[4,16,256]{2,1,0:T(8,128)S(1)}, u32[]{:S(2)}, u32[]{:S(2)}) collective-permute-start(f32[4,16,256]{2,1,0:T(8,128)S(1)} %add.116), channel_id=1, source_target_pairs={{0,6},{1,3},{2,0},{3,5},{4,2},{5,7},{6,4},{7,1},{8,14},{9,11},{10,... | collective-permute-start | bytes 196616 | tf_op jit(solution)/shard_map/ppermute | solution.py:460
  192.3 5.3 %collective-permute-start.31 = (f32[4,16,256]{2,1,0:T(8,128)S(1)}, f32[4,16,256]{2,1,0:T(8,128)S(1)}, u32[]{:S(2)}, u32[]{:S(2)}) collective-permute-start(f32[4,16,256]{2,1,0:T(8,128)S(1)} %add.116), channel_id=1, source_target_pairs={{0,4},{1,5},{2,6},{3,7},{4,0},{5,1},{6,2},{7,3},{8,12},{9,13},{10,... | collective-permute-start | bytes 196616 | tf_op jit(solution)/shard_map/ppermute | solution.py:460
  197.7 3.5 %collective-permute-start.34 = (f32[4,16,256]{2,1,0:T(8,128)S(1)}, f32[4,16,256]{2,1,0:T(8,128)S(1)}, u32[]{:S(2)}, u32[]{:S(2)}) collective-permute-start(f32[4,16,256]{2,1,0:T(8,128)S(1)} %add_add_fusion.1.refs_12_.refs_0_), channel_id=1, source_target_pairs={{0,1},{1,0},{2,3},{3,2},{4,5},{5,4},{6,7},{7,6},{8,9},{9,8},{10,11... | collective-permute-start | bytes 196616 | tf_op jit(solution)/shard_map/ppermute | solution.py:462
  202.0 9.9 %all-to-all-start.7 = ((f32[16,8,128]{2,1,0:T(8,128)}), f32[16,8,128]{2,1,0:T(8,128)S(1)}, u32[]{:S(2)}, u32[]{:S(2)}) async-start(f32[16,8,128]{2,1,0:T(8,128)} %shard_map.142), calls=%async_computation.7 | async-start | bytes 131072 | tf_op jit(solution)/shard_map/all_to_all | solution.py:527
  (14 other events, 55.4 us)
